TPU v7x, 512 devices: a whole 4x8x8 slice. The times are simulated.
512 devices in a mesh: section: 8 (over z_lo, core), dp: 64 (over z_hi, y, x).
Axes of the slice: x: 4, y: 8, z: 8 (z_hi: 2, z_lo: 4; z = z_hi * 4 + z_lo), core: 2. Of those that a mesh axis runs over, the one named last changes fastest.
Arguments:
- x_in: bfloat16 [8, 8192, 5120], P('section', 'dp'), may hold values from -8 to 8
- top_grad: bfloat16 [8192, 5120], P('dp'), may hold values from -6 to 6
- norm_gain: bfloat16 [8, 5120], P('section'), may hold values from 0.25 to 1.75
- proj_in: bfloat16 [8, 5120, 384], P('section', 'dp'), may hold values from -1 to 1
- proj_out: bfloat16 [8, 128, 5120], P('section', None, 'dp'), may hold values from -0.5 to 0.5
- key_cache: bfloat16 [8, 18432, 128], P('section', 'dp'), may hold values from -6 to 6
- value_cache: bfloat16 [8, 18432, 128], P('section', 'dp'), may hold values from -6 to 6
- prefix_len: int32 [64], P('dp'), may hold values from 72 to 288, as said below
- early_out: bfloat16 [8, 2048, 128], P('section', 'dp'), may hold values from -0.59765625 to 0.59765625
- early_dy: bfloat16 [8, 2048, 5120], P('section', 'dp'), may hold values from -16 to 16
Outputs:
- grad_x: bfloat16 [8, 8192, 5120], P('section', 'dp')
- key_cache_grad: bfloat16 [8, 18432, 128], P('section', 'dp')
- value_cache_grad: bfloat16 [8, 18432, 128], P('section', 'dp')
- wo_grad: float32 [8, 128, 5120], P('section', None, 'dp')
Inputs may be any that keep to these rules, and one draw needn't show every extreme that they name: `prefix_len`: some sequence has all 288 cached positions.
All inputs are finite; a program needn't handle non-finite values.
Results may differ from a plain program's by a relative error of at most 0.02.
Values may be sent and summed in bfloat16 or wider, within the bound.
No kernel may reach another device: no remote copies, remote signals or barrier semaphores. Data moves between devices by JAX's collectives and lax.ppermute only.
A program may use at most 64 MiB of HBM per device.

v0:
```python
import jax
import jax.numpy as jnp
from jax import lax
from jax.sharding import PartitionSpec as P

eps = 1e-06


def passed_along(block, axis, distance):
    devices = range(lax.axis_size(axis))
    route = [(i - distance, i) for i in devices if i - distance in devices]
    return lax.ppermute(block, axis, route)


def body(
    x_in,
    top_grad,
    norm_gain,
    proj_in,
    proj_out,
    key_cache,
    value_cache,
    prefix_len,
    early_out,
    early_dy,
):
    layers = lax.axis_size("section")
    section_pos = lax.axis_index("section")
    top_section = layers - 1
    in_full, out_full = (
        lax.all_gather(proj_in, "dp", axis=1, tiled=True),
        lax.all_gather(proj_out, "dp", axis=2, tiled=True),
    )
    in_full = in_full[0]
    out_full = out_full[0]
    head_size = out_full.shape[0]
    x_rows = x_in[0]
    group_rows = x_rows.shape[0]
    width = x_rows.shape[1]
    cache_keys = key_cache[0]
    cache_rows = cache_keys.shape[0]
    key_count = cache_rows + group_rows
    score_scale = head_size ** (-0.5)
    gain_row = norm_gain[0].astype(jnp.float32)
    widened = x_rows.astype(jnp.float32)
    inv_rms = lax.rsqrt(jnp.mean(widened * widened, axis=1, keepdims=True) + eps)
    normed = (widened * inv_rms * gain_row).astype(jnp.bfloat16)
    projected = jnp.dot(normed, in_full, preferred_element_type=jnp.float32).astype(jnp.bfloat16)
    queries = projected[:, :head_size]
    all_keys = jnp.concatenate([cache_keys, projected[:, head_size : 2 * head_size]], axis=0)
    all_values = jnp.concatenate([value_cache[0], projected[:, 2 * head_size :]], axis=0)
    column = lax.broadcasted_iota(jnp.int32, (group_rows, key_count), 1)
    position = lax.broadcasted_iota(jnp.int32, (group_rows, key_count), 0)
    visible = jnp.where(
        column < cache_rows, column < prefix_len[0], column - cache_rows <= position
    )
    scores = (
        jnp.einsum("qh,kh->qk", queries, all_keys, preferred_element_type=jnp.float32) * score_scale
    )
    highest = jnp.max(jnp.where(visible, scores, -jnp.inf), axis=1, keepdims=True)
    weights = jnp.where(visible, jnp.exp(scores - highest), 0.0)
    prob_full = weights / jnp.sum(weights, axis=1, keepdims=True)
    prob_low = prob_full.astype(jnp.bfloat16)
    attended = jnp.dot(prob_low, all_values, preferred_element_type=jnp.float32).astype(
        jnp.bfloat16
    )
    part_count = 1
    part_rows = group_rows // part_count
    turn_count = layers + part_count - 1

    def backward(part_index, grad_in, carried):
        outgoing, grad_all, key_grad, value_grad, wo_grad = carried
        part_start = part_index * part_rows
        grad_out = jnp.einsum(
            "rd,hd->rh", grad_in, out_full, preferred_element_type=jnp.float32
        ).astype(jnp.bfloat16)
        grad_prob = jnp.einsum(
            "rh,kh->rk", grad_out, all_values, preferred_element_type=jnp.float32
        )
        row_delta = jnp.sum(prob_full * grad_prob, axis=1, keepdims=True)
        grad_score = (prob_full * (grad_prob - row_delta) * score_scale).astype(jnp.bfloat16)
        grad_query = jnp.dot(grad_score, all_keys, preferred_element_type=jnp.float32)
        key_grad = key_grad + jnp.einsum(
            "rk,rh->kh", grad_score, queries, preferred_element_type=jnp.float32
        )
        value_grad = value_grad + jnp.einsum(
            "rk,rh->kh", prob_low, grad_out, preferred_element_type=jnp.float32
        )
        own_keys = lax.dynamic_slice_in_dim(key_grad, cache_rows + part_start, part_rows, 0)
        own_values = lax.dynamic_slice_in_dim(value_grad, cache_rows + part_start, part_rows, 0)
        grad_proj = jnp.concatenate([grad_query, own_keys, own_values], axis=1).astype(jnp.bfloat16)
        grad_norm = jnp.einsum("rc,dc->rd", grad_proj, in_full, preferred_element_type=jnp.float32)
        scaled = grad_norm * gain_row
        branch = inv_rms * scaled - widened * inv_rms * inv_rms * inv_rms * jnp.mean(
            widened * scaled, axis=1, keepdims=True
        )
        grad_part = (grad_in.astype(jnp.float32) + branch).astype(jnp.bfloat16)
        grad_all = grad_part
        wo_grad = wo_grad + jnp.einsum(
            "rh,rd->hd", attended, grad_in, preferred_element_type=jnp.float32
        )
        return (grad_part, grad_all, key_grad, value_grad, wo_grad)

    def advance(turn_index, carried):
        part_index = top_section - section_pos + part_count - 1 - turn_index
        active = jnp.logical_and(part_index >= 0, part_index < part_count)
        part_index = jnp.clip(part_index, 0, part_count - 1)
        grad_in = jnp.where(section_pos == top_section, top_grad, carried[0])

        def waiting(current):
            silent = (jnp.zeros_like(current[0]),) + current[1:]
            return silent

        return lax.cond(
            active, lambda current: backward(part_index, grad_in, current), waiting, carried
        )

    carried = (
        jnp.zeros((part_rows, width), jnp.bfloat16),
        jnp.zeros_like(x_rows),
        jnp.zeros((key_count, head_size), jnp.float32),
        jnp.zeros((key_count, head_size), jnp.float32),
        jnp.zeros((head_size, width), jnp.float32),
    )

    def one_turn(turn_index, current):
        current = advance(turn_index, current)
        passed = passed_along(current[0], "section", -1)
        return (passed,) + current[1:]

    carried = lax.fori_loop(0, turn_count - 1, one_turn, carried)
    carried = advance(turn_count - 1, carried)
    wo_grad = carried[4] + jnp.einsum(
        "eh,ed->hd", early_out[0], early_dy[0], preferred_element_type=jnp.float32
    )
    wo_shard = lax.psum_scatter(wo_grad, "dp", scatter_dimension=1, tiled=True)
    key_out = carried[2][:cache_rows].astype(jnp.bfloat16)
    value_out = carried[3][:cache_rows].astype(jnp.bfloat16)
    return (carried[1][None], key_out[None], value_out[None], wo_shard[None])


def solution(mesh):
    in_specs = (
        P("section", "dp", None),
        P("dp", None),
        P("section", None),
        P("section", "dp", None),
        P("section", None, "dp"),
        P("section", "dp", None),
        P("section", "dp", None),
        P("dp"),
        P("section", "dp", None),
        P("section", "dp", None),
    )
    out_specs = (
        P("section", "dp", None),
        P("section", "dp", None),
        P("section", "dp", None),
        P("section", None, "dp"),
    )
    return jax.shard_map(body, mesh=mesh, in_specs=in_specs, out_specs=out_specs, check_vma=False)
```

profile of v0, /device:TPU:64, one launch (start us, length us, event | category | flops | bytes accessed | tf_op | source)
XLA Modules:
  0.0 977.4 jit_solution(9989542307010455076)
XLA Ops:
  8.7 1.3 mul.154
  10.7 1.7 multiply_reduce_fusion.4
  12.4 3.2 convert_bitcast_fusion
  15.6 130.7 %all-gather.3.cloned.1.call-done = bf16[1,128,5120]{1,2,0:T(8,128)(2,1)} async-done(((bf16[1,128,80]{1,2,0:T(8,128)(2,1)}), bf16[1,128,5120]{1,2,0:T(8,128)(2,1)}) %all-gather.3.cloned.1.call-update) | async-done | bytes 1310736 | tf_op jit(solution)/shard_map/all_gather | solution.py:32
  146.3 2.4 copy.17
  148.7 150.8 %all-gather.5.cloned.1.call-done = bf16[1,5120,384]{2,1,0:T(8,128)(2,1)} async-done(((bf16[1,80,384]{2,1,0:T(8,128)(2,1)}), bf16[1,5120,384]{2,1,0:T(8,128)(2,1)}) %all-gather.5.cloned.1.call-update) | async-done | bytes 3932176 | tf_op jit(solution)/shard_map/all_gather | solution.py:31
  299.5 3.1 fusion.28
  305.0 1.7 broadcast_in_dim.35
  306.9 1.2 broadcast.87.clone
  308.8 209.9 %while.23 = (s32[]{:T(128)}, bf16[128,5120]{1,0:T(8,128)(2,1)S(1)}, bf16[128,5120]{1,0:T(8,128)(2,1)}, f32[416,128]{1,0:T(8,128)S(1)}, f32[416,128]{1,0:T(8,128)...) while((s32[]{:T(128)}, bf16[128,5120]{1,0:T(8,128)(2,1)S(1)}, ...), condition=%wide.region_8.9_spmd, body=%wide.region_3.8_spmd.sunk | while | flops 903315328 | bytes 57385136 | solution.py:131
  308.8 1.3 conditional.4
  308.8 1.3 broadcast.76
  310.0 1.9 collective-permute-start
  312.0 15.4 %collective-permute-done = bf16[128,5120]{1,0:T(8,128)(2,1)S(1)} collective-permute-done((bf16[128,5120]{1,0:T(8,128)(2,1)}, bf16[128,5120]{1,0:T(8,128)(2,1)S(1)}, u32[]{:S(2)}, u32[]{:S(2)}) %collective-permute-start) | collective-permute-done | bytes 1310752 | tf_op jit(solution)/shard_map/while/body/eval_jaxpr/ppermute | solution.py:12
  327.4 1.3 conditional.4
  327.4 1.3 broadcast.76
  328.6 3.7 collective-permute-start
  332.4 15.4 %collective-permute-done = bf16[128,5120]{1,0:T(8,128)(2,1)S(1)} collective-permute-done((bf16[128,5120]{1,0:T(8,128)(2,1)}, bf16[128,5120]{1,0:T(8,128)(2,1)S(1)}, u32[]{:S(2)}, u32[]{:S(2)}) %collective-permute-start) | collective-permute-done | bytes 1310752 | tf_op jit(solution)/shard_map/while/body/eval_jaxpr/ppermute | solution.py:12
  347.8 1.3 conditional.4
  347.8 1.3 broadcast.76
  349.0 3.7 collective-permute-start
  352.8 15.4 %collective-permute-done = bf16[128,5120]{1,0:T(8,128)(2,1)S(1)} collective-permute-done((bf16[128,5120]{1,0:T(8,128)(2,1)}, bf16[128,5120]{1,0:T(8,128)(2,1)S(1)}, u32[]{:S(2)}, u32[]{:S(2)}) %collective-permute-start) | collective-permute-done | bytes 1310752 | tf_op jit(solution)/shard_map/while/body/eval_jaxpr/ppermute | solution.py:12
  368.2 1.3 conditional.4
  368.2 1.3 broadcast.76
  369.4 3.7 collective-permute-start
  373.1 15.4 %collective-permute-done = bf16[128,5120]{1,0:T(8,128)(2,1)S(1)} collective-permute-done((bf16[128,5120]{1,0:T(8,128)(2,1)}, bf16[128,5120]{1,0:T(8,128)(2,1)S(1)}, u32[]{:S(2)}, u32[]{:S(2)}) %collective-permute-start) | collective-permute-done | bytes 1310752 | tf_op jit(solution)/shard_map/while/body/eval_jaxpr/ppermute | solution.py:12
  388.6 1.3 conditional.4
  388.6 1.3 broadcast.76
  389.8 3.7 collective-permute-start
  393.5 52.5 %collective-permute-done = bf16[128,5120]{1,0:T(8,128)(2,1)S(1)} collective-permute-done((bf16[128,5120]{1,0:T(8,128)(2,1)}, bf16[128,5120]{1,0:T(8,128)(2,1)S(1)}, u32[]{:S(2)}, u32[]{:S(2)}) %collective-permute-start) | collective-permute-done | bytes 1310752 | tf_op jit(solution)/shard_map/while/body/eval_jaxpr/ppermute | solution.py:12
  446.1 18.1 %conditional.4 = (bf16[128,5120]{1,0:T(8,128)(2,1)}, bf16[128,5120]{1,0:T(8,128)(2,1)}, f32[416,128]{1,0:T(8,128)S(1)}, f32[416,128]{1,0:T(8,128)}, f32[128,5120]{0,1:T(8,128)}) conditional(s32[]{:T(128)} %convert_element_type.112, (bf16[128,5120]{1,0:T(8,128)(2,1)}, f32[416,128]{1,0:T(8,128)S(1)}, f32[416,128]{1,0:T(8,128)}, ...), branch_computations={%region_4.4_spmd, %region_5.7_spmd} | conditional | flops 903315328 | bytes 52141804 | solution.py:114
  446.2 1.2 copy-done.3
  448.4 1.9 fusion.1
  450.2 0.8 dynamic-slice_convert_fusion
  451.3 4.5 multiply_reduce_fusion
  455.9 2.0 add_convert_fusion
  457.8 2.5 copy.29
  460.3 3.8 fusion
  464.1 1.9 collective-permute-start
  466.0 15.4 %collective-permute-done = bf16[128,5120]{1,0:T(8,128)(2,1)S(1)} collective-permute-done((bf16[128,5120]{1,0:T(8,128)(2,1)}, bf16[128,5120]{1,0:T(8,128)(2,1)S(1)}, u32[]{:S(2)}, u32[]{:S(2)}) %collective-permute-start) | collective-permute-done | bytes 1310752 | tf_op jit(solution)/shard_map/while/body/eval_jaxpr/ppermute | solution.py:12
  481.5 1.3 conditional.4
  481.5 1.3 broadcast.76
  482.7 20.5 %collective-permute-start = (bf16[128,5120]{1,0:T(8,128)(2,1)}, bf16[128,5120]{1,0:T(8,128)(2,1)S(1)}, u32[]{:S(2)}, u32[]{:S(2)}) collective-permute-start(bf16[128,5120]{1,0:T(8,128)(2,1)} %get-tuple-element.899), channel_id=1, source_target_pairs={{64,0},{128,64},{192,128},{256,192},{320,256},{384,320},{448,384},... | collective-permute-start | bytes 3932168 | tf_op jit(solution)/shard_map/while/body/eval_jaxpr/ppermute | solution.py:12
  503.2 15.4 %collective-permute-done = bf16[128,5120]{1,0:T(8,128)(2,1)S(1)} collective-permute-done((bf16[128,5120]{1,0:T(8,128)(2,1)}, bf16[128,5120]{1,0:T(8,128)(2,1)S(1)}, u32[]{:S(2)}, u32[]{:S(2)}) %collective-permute-start) | collective-permute-done | bytes 1310752 | tf_op jit(solution)/shard_map/while/body/eval_jaxpr/ppermute | solution.py:12
  518.6 1.6 conditional.2
  518.6 1.6 fusion.8
  520.2 3.9 convolution_add_fusion.2
  524.1 446.7 %reduce-scatter.2.cloned.1.call-done = f32[128,80]{0,1:T(8,128)} async-done(((f32[128,5120]{0,1:T(8,128)}), f32[128,80]{0,1:T(8,128)}) %reduce-scatter.2.cloned.1.call-update) | async-done | bytes 40976 | tf_op jit(solution)/shard_map/reduce_scatter | solution.py:136
  (43 shorter events, 6.1 us)
Async XLA Ops:
  7.2 513.1 %copy-start = (bf16[1,32,5120]{2,1,0:T(8,128)(2,1)S(1)}, bf16[1,32,5120]{2,1,0:T(8,128)(2,1)}, u32[]{:S(2)}) copy-start(bf16[1,32,5120]{2,1,0:T(8,128)(2,1)} %param.25) | copy-start | bytes 983044
  7.2 139.1 %all-gather.3.cloned.1.call-start = ((), (), s32[]{:S(2)}) async-start(), calls=%async_computation.1 | async-start | bytes 1331200 | tf_op jit(solution)/shard_map/all_gather | solution.py:32
  7.9 291.6 %all-gather.5.cloned.1.call-start = ((), (), s32[]{:S(2)}) async-start(), calls=%async_computation.2 | async-start | bytes 3993600 | tf_op jit(solution)/shard_map/all_gather | solution.py:31
  8.7 962.2 %reduce-scatter.2.cloned.1.call-start = ((), (), s32[]{:S(2)}) async-start(), calls=%async_computation.3 | async-start | bytes 2662400 | tf_op jit(solution)/shard_map/reduce_scatter | solution.py:136
  12.4 287.1 %copy-start.7 = (bf16[1,128,5120]{2,1,0:T(8,128)(2,1)S(1)}, bf16[1,128,5120]{2,1,0:T(8,128)(2,1)}, u32[]{:S(2)}) copy-start(bf16[1,128,5120]{2,1,0:T(8,128)(2,1)} %param.16) | copy-start | bytes 3932164
  299.5 3.1 copy-start.13
  299.5 4.7 copy-start.12
  303.4 3.5 copy-start.10
  310.0 17.3 %collective-permute-start = (bf16[128,5120]{1,0:T(8,128)(2,1)}, bf16[128,5120]{1,0:T(8,128)(2,1)S(1)}, u32[]{:S(2)}, u32[]{:S(2)}) collective-permute-start(bf16[128,5120]{1,0:T(8,128)(2,1)} %get-tuple-element.899), channel_id=1, source_target_pairs={{64,0},{128,64},{192,128},{256,192},{320,256},{384,320},{448,384},... | collective-permute-start | bytes 3932168 | tf_op jit(solution)/shard_map/while/body/eval_jaxpr/ppermute | solution.py:12
  328.6 19.1 %collective-permute-start = (bf16[128,5120]{1,0:T(8,128)(2,1)}, bf16[128,5120]{1,0:T(8,128)(2,1)S(1)}, u32[]{:S(2)}, u32[]{:S(2)}) collective-permute-start(bf16[128,5120]{1,0:T(8,128)(2,1)} %get-tuple-element.899), channel_id=1, source_target_pairs={{64,0},{128,64},{192,128},{256,192},{320,256},{384,320},{448,384},... | collective-permute-start | bytes 3932168 | tf_op jit(solution)/shard_map/while/body/eval_jaxpr/ppermute | solution.py:12
  349.0 19.1 %collective-permute-start = (bf16[128,5120]{1,0:T(8,128)(2,1)}, bf16[128,5120]{1,0:T(8,128)(2,1)S(1)}, u32[]{:S(2)}, u32[]{:S(2)}) collective-permute-start(bf16[128,5120]{1,0:T(8,128)(2,1)} %get-tuple-element.899), channel_id=1, source_target_pairs={{64,0},{128,64},{192,128},{256,192},{320,256},{384,320},{448,384},... | collective-permute-start | bytes 3932168 | tf_op jit(solution)/shard_map/while/body/eval_jaxpr/ppermute | solution.py:12
  369.4 19.1 %collective-permute-start = (bf16[128,5120]{1,0:T(8,128)(2,1)}, bf16[128,5120]{1,0:T(8,128)(2,1)S(1)}, u32[]{:S(2)}, u32[]{:S(2)}) collective-permute-start(bf16[128,5120]{1,0:T(8,128)(2,1)} %get-tuple-element.899), channel_id=1, source_target_pairs={{64,0},{128,64},{192,128},{256,192},{320,256},{384,320},{448,384},... | collective-permute-start | bytes 3932168 | tf_op jit(solution)/shard_map/while/body/eval_jaxpr/ppermute | solution.py:12
  389.8 56.2 %collective-permute-start = (bf16[128,5120]{1,0:T(8,128)(2,1)}, bf16[128,5120]{1,0:T(8,128)(2,1)S(1)}, u32[]{:S(2)}, u32[]{:S(2)}) collective-permute-start(bf16[128,5120]{1,0:T(8,128)(2,1)} %get-tuple-element.899), channel_id=1, source_target_pairs={{64,0},{128,64},{192,128},{256,192},{320,256},{384,320},{448,384},... | collective-permute-start | bytes 3932168 | tf_op jit(solution)/shard_map/while/body/eval_jaxpr/ppermute | solution.py:12
  446.1 1.3 copy-start.3
  446.2 2.2 copy-start.9
  446.2 4.9 copy-start.8
  451.3 4.5 copy-start.1
  464.1 17.3 %collective-permute-start = (bf16[128,5120]{1,0:T(8,128)(2,1)}, bf16[128,5120]{1,0:T(8,128)(2,1)S(1)}, u32[]{:S(2)}, u32[]{:S(2)}) collective-permute-start(bf16[128,5120]{1,0:T(8,128)(2,1)} %get-tuple-element.899), channel_id=1, source_target_pairs={{64,0},{128,64},{192,128},{256,192},{320,256},{384,320},{448,384},... | collective-permute-start | bytes 3932168 | tf_op jit(solution)/shard_map/while/body/eval_jaxpr/ppermute | solution.py:12
  482.7 35.9 %collective-permute-start = (bf16[128,5120]{1,0:T(8,128)(2,1)}, bf16[128,5120]{1,0:T(8,128)(2,1)S(1)}, u32[]{:S(2)}, u32[]{:S(2)}) collective-permute-start(bf16[128,5120]{1,0:T(8,128)(2,1)} %get-tuple-element.899), channel_id=1, source_target_pairs={{64,0},{128,64},{192,128},{256,192},{320,256},{384,320},{448,384},... | collective-permute-start | bytes 3932168 | tf_op jit(solution)/shard_map/while/body/eval_jaxpr/ppermute | solution.py:12
Sparse Core Ops, SparseCore 0:
  12.5 133.7 all-gather.2
  150.8 148.6 all-gather.4
  524.3 446.5 reduce-scatter.1
where the time goes:
time: 978 us; the launch traced here: 977 us
  waiting for transfers between devices  875 us (89%)
  starting transfers between devices  39.2 us (4%)
  local copies, waits for them, and re-layouts  20.6 us (2%)
  matrix products  18.8 us (2%)
  between operations  14.5 us (1%)
    reduce_scatter x1, waiting for transfers between devices, body(): wo_shard = lax.psum_scatter(wo_grad, 'dp', scatter_dimension=1, tiled=True)  447 us
    all_gather x1, waiting for transfers between devices, body(): lax.all_gather(proj_in, 'dp', axis=1, tiled=True)  151 us
    ppermute x7, waiting for transfers between devices, passed_along(): return lax.ppermute(block, axis, route)  145 us
    all_gather x1, waiting for transfers between devices, body(): lax.all_gather(proj_out, 'dp', axis=2, tiled=True)  131 us
    ppermute x7, starting transfers between devices, passed_along(): return lax.ppermute(block, axis, route)  39.1 us
  transfers between devices with their start and end apart: 10, of which 10 were waited for; matrix products, arithmetic and copies ran while one was open for 1% of the time, Pallas kernels for 0%

commit v1 on v0

v1 whole, which is shorter than its diff:
```python
import functools

import jax
import jax.numpy as jnp
from jax import lax
from jax.experimental import pallas as pl
from jax.experimental.pallas import tpu as pltpu
from jax.sharding import Mesh
from jax.sharding import PartitionSpec as P

eps = 1e-06
bf16 = jnp.bfloat16
f32 = jnp.float32
PARTS = 4
SECTION = ("zl", "core")
PLANE = ("y", "x")
DP = ("zh", "y", "x")
VMEM = pl.BlockSpec(memory_space=pltpu.VMEM)
ANY = pl.BlockSpec(memory_space=pl.ANY)
SMEM = pl.BlockSpec(memory_space=pltpu.SMEM)


def dot(a, b, ca=1, cb=0):
    return lax.dot_general(a, b, (((ca,), (cb,)), ((), ())), preferred_element_type=f32)


def chunk_of(width):
    return 640 if width % 640 == 0 else width


def forward_kernel(len_ref, normed, wg, kc, vc, q_ref, kn_ref, vn_ref, pc_ref, pn_ref, proj_ref, att_ref):
    half = wg.shape[0]
    hd = kc.shape[1]
    rows = normed.shape[0]
    step = chunk_of(half)
    acc = jnp.zeros((rows, 3 * hd), f32)
    for h in range(2):
        for c in range(0, half, step):
            acc = acc + dot(
                normed[:, h * half + c : h * half + c + step],
                wg[c : c + step, h * 4 * hd : h * 4 * hd + 3 * hd],
            )
    proj_ref[...] = acc
    low = acc.astype(bf16)
    q = low[:, :hd]
    kn = low[:, hd : 2 * hd]
    vn = low[:, 2 * hd :]
    q_ref[...] = q
    kn_ref[...] = kn
    vn_ref[...] = vn
    scale = hd ** (-0.5)
    sc = dot(q, kc[...], 1, 1) * scale
    sn = dot(q, kn, 1, 1) * scale
    see_c = lax.broadcasted_iota(jnp.int32, sc.shape, 1) < len_ref[0]
    see_n = lax.broadcasted_iota(jnp.int32, sn.shape, 1) <= lax.broadcasted_iota(jnp.int32, sn.shape, 0)
    sc = jnp.where(see_c, sc, -jnp.inf)
    sn = jnp.where(see_n, sn, -jnp.inf)
    top = jnp.maximum(jnp.max(sc, axis=1, keepdims=True), jnp.max(sn, axis=1, keepdims=True))
    wc = jnp.where(see_c, jnp.exp(sc - top), 0.0)
    wn = jnp.where(see_n, jnp.exp(sn - top), 0.0)
    total = jnp.sum(wc, axis=1, keepdims=True) + jnp.sum(wn, axis=1, keepdims=True)
    pc = wc / total
    pn = wn / total
    pc_ref[...] = pc
    pn_ref[...] = pn
    att_ref[...] = (dot(pc.astype(bf16), vc[...]) + dot(pn.astype(bf16), vn)).astype(bf16)


def stage_kernel(
    flags, recv, top, wg, x, gain, inv, q, kc, kn, vc, vn, pc, pn, proj, gkn_in, gvn_in, gsc_in, go_in,
    send, gkn, gvn, gsc, go_all, gin, wo_buf, wi_buf, x_buf, gin_sem, wo_sem, wi_sem, x_sem,
):
    rows = send.shape[0]
    hd = q.shape[1]
    half = wg.shape[0]
    step = chunk_of(half)
    scale = hd ** (-0.5)
    active = flags[0] == 1
    r0 = pl.multiple_of(flags[1] * rows, rows)
    is_top = flags[2] == 1
    mine = pl.ds(r0, rows)
    pieces = [(h, c) for h in range(2) for c in range(0, half, step)]
    take_top = pltpu.make_async_copy(top.at[mine, :], gin, gin_sem)
    take_recv = pltpu.make_async_copy(recv, gin, gin_sem)
    take_x = pltpu.make_async_copy(x.at[mine, :], x_buf, x_sem)
    take_wo = []
    take_wi = []
    for n, (h, c) in enumerate(pieces):
        take_wo.append(
            pltpu.make_async_copy(
                wg.at[pl.ds(c, step), pl.ds(h * 4 * hd + 3 * hd, hd)],
                wo_buf.at[pl.ds(n * step, step), :],
                wo_sem.at[n],
            )
        )
        take_wi.append(
            pltpu.make_async_copy(
                wg.at[pl.ds(c, step), pl.ds(h * 4 * hd, 3 * hd)],
                wi_buf.at[pl.ds(n * step, step), :],
                wi_sem.at[n],
            )
        )

    @pl.when(jnp.logical_and(active, is_top))
    def _():
        take_top.start()

    @pl.when(jnp.logical_and(active, jnp.logical_not(is_top)))
    def _():
        take_recv.start()

    @pl.when(active)
    def _():
        for copy in take_wo:
            copy.start()
        for copy in take_wi:
            copy.start()
        take_x.start()

    gkn[...] = gkn_in[...]
    gvn[...] = gvn_in[...]
    gsc[...] = gsc_in[...]
    go_all[...] = go_in[...]

    @pl.when(active)
    def _():
        take_recv.wait()
        acc = jnp.zeros((rows, hd), f32)
        for n in range(len(pieces)):
            take_wo[n].wait()
            acc = acc + dot(gin[:, n * step : (n + 1) * step], wo_buf[n * step : (n + 1) * step, :])
        go = acc.astype(bf16)
        go_all[mine, :] = go
        prob_c = pc[mine, :]
        prob_n = pn[mine, :]
        gp_c = dot(go, vc[...], 1, 1)
        gp_n = dot(go, vn[...], 1, 1)
        delta = jnp.sum(prob_c * gp_c, axis=1, keepdims=True) + jnp.sum(prob_n * gp_n, axis=1, keepdims=True)
        gs_c = (prob_c * (gp_c - delta) * scale).astype(bf16)
        gs_n = (prob_n * (gp_n - delta) * scale).astype(bf16)
        gsc[mine, :] = gs_c
        gq = dot(gs_c, kc[...]) + dot(gs_n, kn[...])
        gkn[...] += dot(gs_n, q[mine, :], 0, 0)
        gvn[...] += dot(prob_n.astype(bf16), go, 0, 0)
        gproj = jnp.concatenate([gq, gkn[mine, :], gvn[mine, :]], axis=1).astype(bf16)
        r = inv[mine, :]
        coef = r * r * jnp.sum(gproj.astype(f32) * proj[mine, :], axis=1, keepdims=True) * (1.0 / (2 * half))
        take_x.wait()
        for n in range(len(pieces)):
            cols = slice(n * step, (n + 1) * step)
            take_wi[n].wait()
            gn = dot(gproj, wi_buf[cols, :], 1, 1)
            out = gin[:, cols].astype(f32) + r * (gn * gain[:, cols]) - x_buf[:, cols].astype(f32) * coef
            send[:, cols] = out.astype(bf16)


def turn_kernel(gin, out):
    tokens, width = gin.shape
    planes = out.shape[0]
    shard = out.shape[1] // 2
    flipped = jnp.transpose(gin[...].astype(f32)).astype(bf16)
    for h in range(2):
        for p in range(planes):
            base = (h * planes + p) * shard
            out[p, h * shard : (h + 1) * shard, :] = flipped[base : base + shard, :]


def contract_kernel(got, att, early, out):
    planes, wide, tokens = got.shape
    acc = early[...]
    for p in range(0, planes, 2):
        lhs = jnp.concatenate([got[p], got[p + 1]], axis=1)
        rhs = jnp.concatenate([att[p, :tokens, :], att[p + 1, :tokens, :]], axis=0)
        acc = acc + dot(lhs, rhs)
    out[...] = acc


def body(x_in, top_grad, norm_gain, proj_in, proj_out, key_cache, value_cache, prefix_len, early_out, early_dy):
    sections = lax.axis_size(SECTION)
    section = lax.axis_index(SECTION)
    zh = lax.axis_index("zh")
    planes = lax.axis_size(PLANE)
    x = x_in[0]
    tokens, width = x.shape
    kc = key_cache[0]
    vc = value_cache[0]
    crow, hd = kc.shape
    shard = width // (2 * planes)
    erows = early_dy.shape[1]
    swap = [(0, 1), (1, 0)]

    with jax.named_scope("weights"):
        own = jnp.concatenate([proj_in[0], jnp.transpose(proj_out[0])], axis=1)
        other = lax.ppermute(own, "zh", swap)
        pair = jnp.where(
            zh == 0, jnp.concatenate([own, other], axis=1), jnp.concatenate([other, own], axis=1)
        )
        wg = lax.all_gather(pair, PLANE, axis=0, tiled=True)

    with jax.named_scope("early"):
        packed = early_dy[0].reshape(erows, 2, planes, 2, shard // 2)
        packed = packed.transpose(2, 4, 1, 3, 0).reshape(planes, shard // 2, 4 * erows)
        early_got = lax.all_to_all(packed, PLANE, 0, 0, tiled=True)

    with jax.named_scope("norm"):
        wide = x.astype(f32)
        gain = norm_gain.astype(f32)
        inv = lax.rsqrt(jnp.mean(wide * wide, axis=1, keepdims=True) + eps)
        normed = (wide * inv * gain).astype(bf16)

    shape = jax.ShapeDtypeStruct
    q, kn, vn, pc, pn, proj, att = pl.pallas_call(
        forward_kernel,
        name="forward",
        in_specs=[SMEM, VMEM, VMEM, VMEM, VMEM],
        out_specs=[VMEM] * 7,
        out_shape=[
            shape((tokens, hd), bf16),
            shape((tokens, hd), bf16),
            shape((tokens, hd), bf16),
            shape((tokens, crow), f32),
            shape((tokens, tokens), f32),
            shape((tokens, 3 * hd), f32),
            shape((tokens, hd), bf16),
        ],
        compiler_params=pltpu.CompilerParams(vmem_limit_bytes=24 << 20),
    )(prefix_len, normed, wg, kc, vc)

    with jax.named_scope("attended"):
        att_all = lax.all_gather(jnp.concatenate([att, early_out[0]], axis=0)[None], PLANE, axis=0, tiled=True)

    rows = tokens // PARTS
    copies = width // chunk_of(width // 2)
    stage = pl.pallas_call(
        stage_kernel,
        name="stage",
        in_specs=[SMEM] + [ANY] * 4 + [VMEM] * 14,
        out_specs=[VMEM] * 5,
        out_shape=[
            shape((rows, width), bf16),
            shape((tokens, hd), f32),
            shape((tokens, hd), f32),
            shape((tokens, crow), bf16),
            shape((tokens, hd), bf16),
        ],
        scratch_shapes=[
            pltpu.VMEM((rows, width), bf16),
            pltpu.VMEM((width, hd), bf16),
            pltpu.VMEM((width, 3 * hd), bf16),
            pltpu.VMEM((rows, width), bf16),
            pltpu.SemaphoreType.DMA,
            pltpu.SemaphoreType.DMA((copies,)),
            pltpu.SemaphoreType.DMA((copies,)),
            pltpu.SemaphoreType.DMA,
        ],
        input_output_aliases={15: 1, 16: 2, 17: 3, 18: 4},
        compiler_params=pltpu.CompilerParams(vmem_limit_bytes=24 << 20),
    )
    is_top = section == sections - 1

    def place(t):
        part = sections - 1 - section + PARTS - 1 - t
        active = jnp.logical_and(part >= 0, part < PARTS)
        return jnp.clip(part, 0, PARTS - 1), active

    def keep(whole, piece, t, also):
        part, active = place(t)
        at = part * rows
        old = lax.dynamic_slice_in_dim(whole, at, rows, 0)
        return lax.dynamic_update_slice_in_dim(
            whole, jnp.where(jnp.logical_and(active, also), piece, old), at, 0
        )

    def compute(t, recv, state):
        part, active = place(t)
        flags = jnp.stack([active.astype(jnp.int32), part, is_top.astype(jnp.int32)])
        return stage(flags, recv, top_grad, wg, x, gain, inv, q, kc, kn, vc, vn, pc, pn, proj, *state)

    def one_turn(t, carried):
        recv, gin_all, gx_all, state = carried
        send, *state = compute(t, recv, state)
        passed = lax.ppermute(send, SECTION, [(i, i - 1) for i in range(1, sections)])
        gin_all = keep(gin_all, recv, t, jnp.logical_not(is_top))
        gx_all = keep(gx_all, send, t, True)
        return passed, gin_all, gx_all, tuple(state)

    carried = (
        jnp.zeros((rows, width), bf16),
        jnp.where(is_top, top_grad, jnp.zeros_like(top_grad)),
        jnp.zeros((tokens, width), bf16),
        (
            jnp.zeros((tokens, hd), f32),
            jnp.zeros((tokens, hd), f32),
            jnp.zeros((tokens, crow), bf16),
            jnp.zeros((tokens, hd), bf16),
        ),
    )
    turns = sections + PARTS - 1
    recv, gin_all, gx_all, state = lax.fori_loop(0, turns - 1, one_turn, carried)
    gin_all = keep(gin_all, recv, turns - 1, jnp.logical_not(is_top))
    with jax.named_scope("owners"):
        turned = pl.pallas_call(
            turn_kernel,
            name="turn",
            in_specs=[VMEM],
            out_specs=VMEM,
            out_shape=shape((planes, 2 * shard, tokens), bf16),
            compiler_params=pltpu.CompilerParams(vmem_limit_bytes=24 << 20),
        )(gin_all)
        got = lax.all_to_all(turned, PLANE, 0, 0, tiled=True)
    send, gkn, gvn, gsc, go_all = compute(turns - 1, recv, state)
    gx_all = keep(gx_all, send, turns - 1, True)
    with jax.named_scope("cache"):
        key_out = dot(gsc, q, 0, 0).astype(bf16)
        value_out = dot(pc.astype(bf16), go_all, 0, 0).astype(bf16)
    with jax.named_scope("early_sum"):
        early_rows = early_got.reshape(planes, shard // 2, 4, erows)
        early = jnp.einsum("prqt,pth->qrh", early_rows, att_all[:, tokens:, :], preferred_element_type=f32)
        early = early.reshape(2 * shard, hd)
    with jax.named_scope("sum"):
        whole = pl.pallas_call(
            contract_kernel,
            name="contract",
            in_specs=[VMEM] * 3,
            out_specs=VMEM,
            out_shape=shape((2 * shard, hd), f32),
            compiler_params=pltpu.CompilerParams(vmem_limit_bytes=24 << 20),
        )(got, att_all, early)
        first, second = whole[:shard], whole[shard:]
        away = lax.ppermute(jnp.where(zh == 0, second, first), "zh", swap)
        wo = jnp.transpose(jnp.where(zh == 0, first, second) + away)
    return gx_all[None], key_out[None], value_out[None], wo[None]


def solution(mesh):
    ny, nx = (8, 4) if mesh.shape["dp"] == 64 else (2, mesh.shape["dp"] // 4)
    fine = Mesh(mesh.devices.reshape(mesh.shape["section"] // 2, 2, 2, ny, nx), ("zl", "core", "zh", "y", "x"))
    in_specs = (
        P(SECTION, DP, None),
        P(DP, None),
        P(SECTION, None),
        P(SECTION, DP, None),
        P(SECTION, None, DP),
        P(SECTION, DP, None),
        P(SECTION, DP, None),
        P(DP),
        P(SECTION, DP, None),
        P(SECTION, DP, None),
    )
    out_specs = (
        P(SECTION, DP, None),
        P(SECTION, DP, None),
        P(SECTION, DP, None),
        P(SECTION, None, DP),
    )
    return jax.shard_map(body, mesh=fine, in_specs=in_specs, out_specs=out_specs, check_vma=False)
```

time: 978 us -> 312 us (0.32)
  the two profiles are of different devices: /device:TPU:64 before, /device:TPU:1 now
where the time goes in v1:
time: 312 us; the launch traced here: 311 us
  waiting for transfers between devices  152 us (49%)
  starting transfers between devices  55.6 us (18%)
  Pallas kernels  37.7 us (12%)
  other arithmetic  30.8 us (10%)
  local copies, waits for them, and re-layouts  15.7 us (5%)
  between operations  15.1 us (5%)
  matrix products  3.66 us (1%)
    all_gather x1, waiting for transfers between devices, body(): wg = lax.all_gather(pair, PLANE, axis=0, tiled=True)  70.3 us
    ppermute x10, waiting for transfers between devices, one_turn(): lax.ppermute(send, SECTION, [(i, i - 1) for i in range(1, sections)])  58.5 us
    pallas_call x11, Pallas kernels, compute(): stage(flags, recv, top_grad, wg, x, gain, inv, q, kc, kn, vc, vn, pc, pn,...  29.9 us
    dynamic_update_slice x12, other arithmetic, keep(): lax.dynamic_update_slice_in_dim(whole, jnp.where(jnp.logical_and(active,...  24.3 us
    ppermute x10, starting transfers between devices, one_turn(): lax.ppermute(send, SECTION, [(i, i - 1) for i in range(1, sections)])  22.9 us
    all_to_all x1, waiting for transfers between devices, body(): got = lax.all_to_all(turned, PLANE, 0, 0, tiled=True)  18.5 us
    ppermute x1, starting transfers between devices, body(): other = lax.ppermute(own, 'zh', swap)  11.5 us
    all_to_all x1, starting transfers between devices, body(): early_got = lax.all_to_all(packed, PLANE, 0, 0, tiled=True)  10.1 us
  transfers between devices with their start and end apart: 16, of which 14 were waited for; matrix products, arithmetic and copies ran while one was open for 15% of the time, Pallas kernels for 12%

profile of v1, /device:TPU:1, one launch (start us, length us, event | category | flops | bytes accessed | tf_op | source)
XLA Modules:
  0.0 310.8 jit_solution(15217176132361637455)
XLA Ops:
  8.1 11.5 %collective-permute-start.1 = (bf16[80,512]{1,0:T(8,128)(2,1)S(1)}, bf16[80,512]{1,0:T(8,128)(2,1)S(1)}, u32[]{:S(2)}, u32[]{:S(2)}) collective-permute-start(bf16[80,512]{1,0:T(8,128)(2,1)S(1)} %pad_maximum_fusion), channel_id=1, source_target_pairs={{0,32},{32,0},{1,33},{33,1},{2,34},{34,2},{3,35},{35,3},{4,36},{36... | collective-permute-start | bytes 245768 | tf_op jit(solution)/shard_map/weights/ppermute | solution.py:194
  23.1 2.9 squeeze.27
  26.0 3.4 %copy.26 = bf16[32,2,32,2,40]{0,3,1,4,2:T(2,128)(2,1)S(1)} copy(bf16[32,2,32,2,40]{4,3,2,1,0:T(2,128)(2,1)S(1)} %squeeze.27) | data formatting | bytes 655360 | tf_op jit(solution)/shard_map/early/reshape;early/squeeze | solution.py:201
  30.8 10.1 %all-to-all-start.1 = ((bf16[32,40,128]{2,1,0:T(8,128)(2,1)}), bf16[32,40,128]{2,1,0:T(8,128)(2,1)}, u32[]{:S(2)}, u32[]{:S(2)}) async-start(bf16[32,40,128]{2,1,0:T(8,128)(2,1)} %reshape.40), calls=%async_computation.1 | async-start | bytes 655360 | tf_op jit(solution)/shard_map/early/all_to_all | solution.py:203
  44.4 70.3 %all-gather.4.cloned.1.call-done.wg = bf16[2560,1024]{1,0:T(8,128)(2,1)} async-done(((bf16[80,1024]{1,0:T(8,128)(2,1)}), bf16[2560,1024]{1,0:T(8,128)(2,1)}) %all-gather.4.cloned.1.call-update) | async-done | bytes 5242896 | tf_op jit(solution)/shard_map/weights/all_gather | solution.py:198
  114.8 4.5 %forward.1 = (bf16[128,128]{1,0:T(8,128)(2,1)}, bf16[128,128]{1,0:T(8,128)(2,1)}, bf16[128,128]{1,0:T(8,128)(2,1)}, f32[128,288]{1,0:T(8,128)S(1)}, f32[128,128]...) custom-call(s32[1]{0:T(128)S(6)} %copy.67.len_ref, bf16[128,5120]{1,0:T(8,128)(2,1)S(1)} %fusion.2.normed, ...), custom_call_target="tpu_custom_call" | custom-call | tf_op jit(solution)/shard_map/forward/pallas_call | solution.py:212
  121.3 132.8 %while.27 = (s32[]{:T(128)}, bf16[32,5120]{1,0:T(8,128)(2,1)S(1)}, bf16[128,5120]{1,0:T(8,128)(2,1)}, bf16[128,5120]{1,0:T(8,128)(2,1)}, f32[128,128]{1,0:T(8,12...) while((s32[]{:T(128)}, bf16[32,5120]{1,0:T(8,128)(2,1)S(1)}, ...), condition=%wide.region_2.3_spmd, body=%wide.region_1.2_spmd.sunk | while | flops 327701 | bytes 3932607 | solution.py:299
  122.2 5.6 %collective-permute-start = (bf16[32,5120]{1,0:T(8,128)(2,1)S(1)}, bf16[32,5120]{1,0:T(8,128)(2,1)S(1)}, u32[]{:S(2)}, u32[]{:S(2)}) collective-permute-start(bf16[32,5120]{1,0:T(8,128)(2,1)S(1)} %get-tuple-element.784), channel_id=1, source_target_pairs={{64,0},{128,64},{192,128},{256,192},{320,256},{384,320},{448,384},... | collective-permute-start | bytes 983048 | tf_op jit(solution)/shard_map/while/body/eval_jaxpr/ppermute | solution.py:282
  127.8 2.1 select_dynamic-update-slice_fusion.4
  129.9 3.9 %collective-permute-done = bf16[32,5120]{1,0:T(8,128)(2,1)S(1)} collective-permute-done((bf16[32,5120]{1,0:T(8,128)(2,1)S(1)}, bf16[32,5120]{1,0:T(8,128)(2,1)S(1)}, u32[]{:S(2)}, u32[]{:S(2)}) %collective-permute-start) | collective-permute-done | bytes 327712 | tf_op jit(solution)/shard_map/while/body/eval_jaxpr/ppermute | solution.py:282
  134.7 1.9 collective-permute-start
  136.6 2.1 select_dynamic-update-slice_fusion.4
  138.7 4.4 %collective-permute-done = bf16[32,5120]{1,0:T(8,128)(2,1)S(1)} collective-permute-done((bf16[32,5120]{1,0:T(8,128)(2,1)S(1)}, bf16[32,5120]{1,0:T(8,128)(2,1)S(1)}, u32[]{:S(2)}, u32[]{:S(2)}) %collective-permute-start) | collective-permute-done | bytes 327712 | tf_op jit(solution)/shard_map/while/body/eval_jaxpr/ppermute | solution.py:282
  144.0 1.9 collective-permute-start
  145.9 2.1 select_dynamic-update-slice_fusion.4
  148.0 4.4 %collective-permute-done = bf16[32,5120]{1,0:T(8,128)(2,1)S(1)} collective-permute-done((bf16[32,5120]{1,0:T(8,128)(2,1)S(1)}, bf16[32,5120]{1,0:T(8,128)(2,1)S(1)}, u32[]{:S(2)}, u32[]{:S(2)}) %collective-permute-start) | collective-permute-done | bytes 327712 | tf_op jit(solution)/shard_map/while/body/eval_jaxpr/ppermute | solution.py:282
  153.3 1.9 collective-permute-start
  155.2 2.1 select_dynamic-update-slice_fusion.4
  157.3 4.8 %collective-permute-done = bf16[32,5120]{1,0:T(8,128)(2,1)S(1)} collective-permute-done((bf16[32,5120]{1,0:T(8,128)(2,1)S(1)}, bf16[32,5120]{1,0:T(8,128)(2,1)S(1)}, u32[]{:S(2)}, u32[]{:S(2)}) %collective-permute-start) | collective-permute-done | bytes 327712 | tf_op jit(solution)/shard_map/while/body/eval_jaxpr/ppermute | solution.py:282
  163.0 1.9 collective-permute-start
  164.9 2.1 select_dynamic-update-slice_fusion.4
  167.0 4.4 %collective-permute-done = bf16[32,5120]{1,0:T(8,128)(2,1)S(1)} collective-permute-done((bf16[32,5120]{1,0:T(8,128)(2,1)S(1)}, bf16[32,5120]{1,0:T(8,128)(2,1)S(1)}, u32[]{:S(2)}, u32[]{:S(2)}) %collective-permute-start) | collective-permute-done | bytes 327712 | tf_op jit(solution)/shard_map/while/body/eval_jaxpr/ppermute | solution.py:282
  172.3 1.9 collective-permute-start
  174.2 2.1 select_dynamic-update-slice_fusion.4
  176.3 18.7 %collective-permute-done = bf16[32,5120]{1,0:T(8,128)(2,1)S(1)} collective-permute-done((bf16[32,5120]{1,0:T(8,128)(2,1)S(1)}, bf16[32,5120]{1,0:T(8,128)(2,1)S(1)}, u32[]{:S(2)}, u32[]{:S(2)}) %collective-permute-start) | collective-permute-done | bytes 327712 | tf_op jit(solution)/shard_map/while/body/eval_jaxpr/ppermute | solution.py:282
  195.1 6.1 %stage.9 = (bf16[32,5120]{1,0:T(8,128)(2,1)S(1)}, f32[128,128]{1,0:T(8,128)S(1)}, f32[128,128]{1,0:T(8,128)S(1)}, bf16[128,288]{1,0:T(8,128)(2,1)S(1)}, bf16[128,128]{1,0:T(8,128)(2,1)S(1)}) custom-call(s32[3]{0:T(128)S(1)} %pad_add_fusion.3.flags, ...), custom_call_target="tpu_custom_call", output_to_operand_aliasing={{1}: (15, {}), {2}: (16, {}), {3}: (17, {}), {4}: (18, {})} | custom-call | tf_op jit(solution)/shard_map/while/body/eval_jaxpr/stage/pallas_call | solution.py:277
  201.3 1.9 collective-permute-start
  203.2 2.1 select_dynamic-update-slice_fusion.4
  205.3 4.7 %collective-permute-done = bf16[32,5120]{1,0:T(8,128)(2,1)S(1)} collective-permute-done((bf16[32,5120]{1,0:T(8,128)(2,1)S(1)}, bf16[32,5120]{1,0:T(8,128)(2,1)S(1)}, u32[]{:S(2)}, u32[]{:S(2)}) %collective-permute-start) | collective-permute-done | bytes 327712 | tf_op jit(solution)/shard_map/while/body/eval_jaxpr/ppermute | solution.py:282
  210.1 6.1 %stage.9 = (bf16[32,5120]{1,0:T(8,128)(2,1)S(1)}, f32[128,128]{1,0:T(8,128)S(1)}, f32[128,128]{1,0:T(8,128)S(1)}, bf16[128,288]{1,0:T(8,128)(2,1)S(1)}, bf16[128,128]{1,0:T(8,128)(2,1)S(1)}) custom-call(s32[3]{0:T(128)S(1)} %pad_add_fusion.3.flags, ...), custom_call_target="tpu_custom_call", output_to_operand_aliasing={{1}: (15, {}), {2}: (16, {}), {3}: (17, {}), {4}: (18, {})} | custom-call | tf_op jit(solution)/shard_map/while/body/eval_jaxpr/stage/pallas_call | solution.py:277
  216.2 1.9 collective-permute-start
  218.2 2.1 select_dynamic-update-slice_fusion.4
  220.3 4.4 %collective-permute-done = bf16[32,5120]{1,0:T(8,128)(2,1)S(1)} collective-permute-done((bf16[32,5120]{1,0:T(8,128)(2,1)S(1)}, bf16[32,5120]{1,0:T(8,128)(2,1)S(1)}, u32[]{:S(2)}, u32[]{:S(2)}) %collective-permute-start) | collective-permute-done | bytes 327712 | tf_op jit(solution)/shard_map/while/body/eval_jaxpr/ppermute | solution.py:282
  224.8 6.1 %stage.9 = (bf16[32,5120]{1,0:T(8,128)(2,1)S(1)}, f32[128,128]{1,0:T(8,128)S(1)}, f32[128,128]{1,0:T(8,128)S(1)}, bf16[128,288]{1,0:T(8,128)(2,1)S(1)}, bf16[128,128]{1,0:T(8,128)(2,1)S(1)}) custom-call(s32[3]{0:T(128)S(1)} %pad_add_fusion.3.flags, ...), custom_call_target="tpu_custom_call", output_to_operand_aliasing={{1}: (15, {}), {2}: (16, {}), {3}: (17, {}), {4}: (18, {})} | custom-call | tf_op jit(solution)/shard_map/while/body/eval_jaxpr/stage/pallas_call | solution.py:277
  230.9 1.9 collective-permute-start
  232.8 2.1 select_dynamic-update-slice_fusion.4
  234.9 4.5 %collective-permute-done = bf16[32,5120]{1,0:T(8,128)(2,1)S(1)} collective-permute-done((bf16[32,5120]{1,0:T(8,128)(2,1)S(1)}, bf16[32,5120]{1,0:T(8,128)(2,1)S(1)}, u32[]{:S(2)}, u32[]{:S(2)}) %collective-permute-start) | collective-permute-done | bytes 327712 | tf_op jit(solution)/shard_map/while/body/eval_jaxpr/ppermute | solution.py:282
  239.5 6.1 %stage.9 = (bf16[32,5120]{1,0:T(8,128)(2,1)S(1)}, f32[128,128]{1,0:T(8,128)S(1)}, f32[128,128]{1,0:T(8,128)S(1)}, bf16[128,288]{1,0:T(8,128)(2,1)S(1)}, bf16[128,128]{1,0:T(8,128)(2,1)S(1)}) custom-call(s32[3]{0:T(128)S(1)} %pad_add_fusion.3.flags, ...), custom_call_target="tpu_custom_call", output_to_operand_aliasing={{1}: (15, {}), {2}: (16, {}), {3}: (17, {}), {4}: (18, {})} | custom-call | tf_op jit(solution)/shard_map/while/body/eval_jaxpr/stage/pallas_call | solution.py:277
  247.6 2.1 select_dynamic-update-slice_fusion.4
  249.7 4.4 %collective-permute-done = bf16[32,5120]{1,0:T(8,128)(2,1)S(1)} collective-permute-done((bf16[32,5120]{1,0:T(8,128)(2,1)S(1)}, bf16[32,5120]{1,0:T(8,128)(2,1)S(1)}, u32[]{:S(2)}, u32[]{:S(2)}) %collective-permute-start) | collective-permute-done | bytes 327712 | tf_op jit(solution)/shard_map/while/body/eval_jaxpr/ppermute | solution.py:282
  256.0 2.8 turn.1
  258.8 5.6 %all-to-all-start = ((bf16[32,160,128]{2,1,0:T(8,128)(2,1)}), bf16[32,160,128]{2,1,0:T(8,128)(2,1)S(1)}, u32[]{:S(2)}, u32[]{:S(2)}) async-start(bf16[32,160,128]{2,1,0:T(8,128)(2,1)} %turn.1), calls=%async_computation | async-start | bytes 2621440 | tf_op jit(solution)/shard_map/owners/all_to_all | solution.py:310
  264.5 3.0 reshape.41
  267.6 2.6 copy.65
  273.6 2.0 fusion.3
  275.6 18.5 %all-to-all-done.got = bf16[32,160,128]{2,1,0:T(8,128)(2,1)S(1)} async-done(((bf16[32,160,128]{2,1,0:T(8,128)(2,1)}), bf16[32,160,128]{2,1,0:T(8,128)(2,1)S(1)}, u32[]{:S(2)}, u32[]{:S(2)}) %all-to-all-start) | async-done | bytes 1310752 | tf_op jit(solution)/shard_map/owners/all_to_all | solution.py:310
  294.6 5.4 %collective-permute-start.2 = (f32[80,128]{1,0:T(8,128)S(1)}, f32[80,128]{1,0:T(8,128)S(1)}, u32[]{:S(2)}, u32[]{:S(2)}) collective-permute-start(f32[80,128]{1,0:T(8,128)S(1)} %slice_select_fusion), channel_id=1, source_target_pairs={{0,32},{32,0},{1,33},{33,1},{2,34},{34,2},{3,35},{35,3},{4,36},{36... | collective-permute-start | bytes 122888 | tf_op jit(solution)/shard_map/sum/ppermute | solution.py:330
  300.9 2.4 collective-permute-done.2
  (115 shorter events, 25.2 us)
Async XLA Ops:
  7.2 107.6 %all-gather.4.cloned.1.call-start = ((), (), s32[]{:S(2)}) async-start(), calls=%async_computation.2 | async-start | bytes 5406720 | tf_op jit(solution)/shard_map/weights/all_gather | solution.py:198
  8.1 13.4 %collective-permute-start.1 = (bf16[80,512]{1,0:T(8,128)(2,1)S(1)}, bf16[80,512]{1,0:T(8,128)(2,1)S(1)}, u32[]{:S(2)}, u32[]{:S(2)}) collective-permute-start(bf16[80,512]{1,0:T(8,128)(2,1)S(1)} %pad_maximum_fusion), channel_id=1, source_target_pairs={{0,32},{32,0},{1,33},{33,1},{2,34},{34,2},{3,35},{35,3},{4,36},{36... | collective-permute-start | bytes 245768 | tf_op jit(solution)/shard_map/weights/ppermute | solution.py:194
  29.4 11.6 %copy-start.26 = (bf16[1,5120]{1,0:T(2,128)(2,1)S(1)}, bf16[1,5120]{1,0:T(2,128)(2,1)}, u32[]{:S(2)}) copy-start(bf16[1,5120]{1,0:T(2,128)(2,1)} %param.14) | copy-start | bytes 30724
  29.5 11.7 %copy-start.1 = (bf16[1,128,5120]{2,1,0:T(8,128)(2,1)S(1)}, bf16[1,128,5120]{2,1,0:T(8,128)(2,1)}, u32[]{:S(2)}) copy-start(bf16[1,128,5120]{2,1,0:T(8,128)(2,1)} %param.12) | copy-start | bytes 3932164
  30.8 12.0 %copy-start.2 = (bf16[128,5120]{1,0:T(8,128)(2,1)S(1)}, bf16[128,5120]{1,0:T(8,128)(2,1)}, u32[]{:S(2)}) copy-start(bf16[128,5120]{1,0:T(8,128)(2,1)} %top.1) | copy-start | bytes 3932164
  30.8 227.9 %all-to-all-start.1 = ((bf16[32,40,128]{2,1,0:T(8,128)(2,1)}), bf16[32,40,128]{2,1,0:T(8,128)(2,1)}, u32[]{:S(2)}, u32[]{:S(2)}) async-start(bf16[32,40,128]{2,1,0:T(8,128)(2,1)} %reshape.40), calls=%async_computation.1 | async-start | bytes 655360 | tf_op jit(solution)/shard_map/early/all_to_all | solution.py:203
  41.0 232.6 %all-gather.6.cloned.1.call-start = ((), (), s32[]{:S(2)}) async-start(), calls=%async_computation.3 | async-start | bytes 1351680 | tf_op jit(solution)/shard_map/attended/all_gather | solution.py:230
  41.1 2.9 copy-start.19
  44.0 70.7 %copy-start.4 = (bf16[1,288,128]{2,1,0:T(8,128)(2,1)S(1)}, bf16[1,288,128]{2,1,0:T(8,128)(2,1)}, u32[]{:S(2)}) copy-start(bf16[1,288,128]{2,1,0:T(8,128)(2,1)} %param.17) | copy-start | bytes 221188
  44.0 70.7 %copy-start.5 = (bf16[1,288,128]{2,1,0:T(8,128)(2,1)S(1)}, bf16[1,288,128]{2,1,0:T(8,128)(2,1)}, u32[]{:S(2)}) copy-start(bf16[1,288,128]{2,1,0:T(8,128)(2,1)} %param.18) | copy-start | bytes 221188
  114.8 4.6 %copy-start.27 = (bf16[1,32,128]{2,1,0:T(8,128)(2,1)S(1)}, bf16[1,32,128]{2,1,0:T(8,128)(2,1)}, u32[]{:S(2)}) copy-start(bf16[1,32,128]{2,1,0:T(8,128)(2,1)} %param.20) | copy-start | bytes 24580
  119.3 2.0 copy-start.6
  119.3 2.0 copy-start.8
  119.3 2.0 copy-start.14
  119.3 2.0 copy-start.16
  119.3 2.0 copy-start.20
  119.3 2.0 copy-start.22
  119.3 2.0 copy-start.24
  122.2 11.6 %collective-permute-start = (bf16[32,5120]{1,0:T(8,128)(2,1)S(1)}, bf16[32,5120]{1,0:T(8,128)(2,1)S(1)}, u32[]{:S(2)}, u32[]{:S(2)}) collective-permute-start(bf16[32,5120]{1,0:T(8,128)(2,1)S(1)} %get-tuple-element.784), channel_id=1, source_target_pairs={{64,0},{128,64},{192,128},{256,192},{320,256},{384,320},{448,384},... | collective-permute-start | bytes 983048 | tf_op jit(solution)/shard_map/while/body/eval_jaxpr/ppermute | solution.py:282
  134.7 8.4 %collective-permute-start = (bf16[32,5120]{1,0:T(8,128)(2,1)S(1)}, bf16[32,5120]{1,0:T(8,128)(2,1)S(1)}, u32[]{:S(2)}, u32[]{:S(2)}) collective-permute-start(bf16[32,5120]{1,0:T(8,128)(2,1)S(1)} %get-tuple-element.784), channel_id=1, source_target_pairs={{64,0},{128,64},{192,128},{256,192},{320,256},{384,320},{448,384},... | collective-permute-start | bytes 983048 | tf_op jit(solution)/shard_map/while/body/eval_jaxpr/ppermute | solution.py:282
  144.0 8.4 %collective-permute-start = (bf16[32,5120]{1,0:T(8,128)(2,1)S(1)}, bf16[32,5120]{1,0:T(8,128)(2,1)S(1)}, u32[]{:S(2)}, u32[]{:S(2)}) collective-permute-start(bf16[32,5120]{1,0:T(8,128)(2,1)S(1)} %get-tuple-element.784), channel_id=1, source_target_pairs={{64,0},{128,64},{192,128},{256,192},{320,256},{384,320},{448,384},... | collective-permute-start | bytes 983048 | tf_op jit(solution)/shard_map/while/body/eval_jaxpr/ppermute | solution.py:282
  153.3 8.8 %collective-permute-start = (bf16[32,5120]{1,0:T(8,128)(2,1)S(1)}, bf16[32,5120]{1,0:T(8,128)(2,1)S(1)}, u32[]{:S(2)}, u32[]{:S(2)}) collective-permute-start(bf16[32,5120]{1,0:T(8,128)(2,1)S(1)} %get-tuple-element.784), channel_id=1, source_target_pairs={{64,0},{128,64},{192,128},{256,192},{320,256},{384,320},{448,384},... | collective-permute-start | bytes 983048 | tf_op jit(solution)/shard_map/while/body/eval_jaxpr/ppermute | solution.py:282
  163.0 8.4 %collective-permute-start = (bf16[32,5120]{1,0:T(8,128)(2,1)S(1)}, bf16[32,5120]{1,0:T(8,128)(2,1)S(1)}, u32[]{:S(2)}, u32[]{:S(2)}) collective-permute-start(bf16[32,5120]{1,0:T(8,128)(2,1)S(1)} %get-tuple-element.784), channel_id=1, source_target_pairs={{64,0},{128,64},{192,128},{256,192},{320,256},{384,320},{448,384},... | collective-permute-start | bytes 983048 | tf_op jit(solution)/shard_map/while/body/eval_jaxpr/ppermute | solution.py:282
  172.3 22.7 %collective-permute-start = (bf16[32,5120]{1,0:T(8,128)(2,1)S(1)}, bf16[32,5120]{1,0:T(8,128)(2,1)S(1)}, u32[]{:S(2)}, u32[]{:S(2)}) collective-permute-start(bf16[32,5120]{1,0:T(8,128)(2,1)S(1)} %get-tuple-element.784), channel_id=1, source_target_pairs={{64,0},{128,64},{192,128},{256,192},{320,256},{384,320},{448,384},... | collective-permute-start | bytes 983048 | tf_op jit(solution)/shard_map/while/body/eval_jaxpr/ppermute | solution.py:282
  201.3 8.7 %collective-permute-start = (bf16[32,5120]{1,0:T(8,128)(2,1)S(1)}, bf16[32,5120]{1,0:T(8,128)(2,1)S(1)}, u32[]{:S(2)}, u32[]{:S(2)}) collective-permute-start(bf16[32,5120]{1,0:T(8,128)(2,1)S(1)} %get-tuple-element.784), channel_id=1, source_target_pairs={{64,0},{128,64},{192,128},{256,192},{320,256},{384,320},{448,384},... | collective-permute-start | bytes 983048 | tf_op jit(solution)/shard_map/while/body/eval_jaxpr/ppermute | solution.py:282
  216.2 8.4 %collective-permute-start = (bf16[32,5120]{1,0:T(8,128)(2,1)S(1)}, bf16[32,5120]{1,0:T(8,128)(2,1)S(1)}, u32[]{:S(2)}, u32[]{:S(2)}) collective-permute-start(bf16[32,5120]{1,0:T(8,128)(2,1)S(1)} %get-tuple-element.784), channel_id=1, source_target_pairs={{64,0},{128,64},{192,128},{256,192},{320,256},{384,320},{448,384},... | collective-permute-start | bytes 983048 | tf_op jit(solution)/shard_map/while/body/eval_jaxpr/ppermute | solution.py:282
  230.9 8.5 %collective-permute-start = (bf16[32,5120]{1,0:T(8,128)(2,1)S(1)}, bf16[32,5120]{1,0:T(8,128)(2,1)S(1)}, u32[]{:S(2)}, u32[]{:S(2)}) collective-permute-start(bf16[32,5120]{1,0:T(8,128)(2,1)S(1)} %get-tuple-element.784), channel_id=1, source_target_pairs={{64,0},{128,64},{192,128},{256,192},{320,256},{384,320},{448,384},... | collective-permute-start | bytes 983048 | tf_op jit(solution)/shard_map/while/body/eval_jaxpr/ppermute | solution.py:282
  245.7 8.4 %collective-permute-start = (bf16[32,5120]{1,0:T(8,128)(2,1)S(1)}, bf16[32,5120]{1,0:T(8,128)(2,1)S(1)}, u32[]{:S(2)}, u32[]{:S(2)}) collective-permute-start(bf16[32,5120]{1,0:T(8,128)(2,1)S(1)} %get-tuple-element.784), channel_id=1, source_target_pairs={{64,0},{128,64},{192,128},{256,192},{320,256},{384,320},{448,384},... | collective-permute-start | bytes 983048 | tf_op jit(solution)/shard_map/while/body/eval_jaxpr/ppermute | solution.py:282
  254.1 4.7 %copy-start.10 = (f32[128,128]{1,0:T(8,128)}, f32[128,128]{1,0:T(8,128)S(1)}, u32[]{:S(2)}) copy-start(f32[128,128]{1,0:T(8,128)S(1)} %get-tuple-element.523.gkn_in) | copy-start | bytes 196612
  254.1 4.7 %copy-start.12 = (f32[128,128]{1,0:T(8,128)}, f32[128,128]{1,0:T(8,128)S(1)}, u32[]{:S(2)}) copy-start(f32[128,128]{1,0:T(8,128)S(1)} %get-tuple-element.524.gvn_in) | copy-start | bytes 196612
  258.8 35.3 %all-to-all-start = ((bf16[32,160,128]{2,1,0:T(8,128)(2,1)}), bf16[32,160,128]{2,1,0:T(8,128)(2,1)S(1)}, u32[]{:S(2)}, u32[]{:S(2)}) async-start(bf16[32,160,128]{2,1,0:T(8,128)(2,1)} %turn.1), calls=%async_computation | async-start | bytes 2621440 | tf_op jit(solution)/shard_map/owners/all_to_all | solution.py:310
  267.5 2.6 copy-start.3
  267.5 2.6 copy-start.7
  267.5 2.6 copy-start.9
  267.5 2.6 copy-start.11
  267.5 2.7 copy-start.13
  267.5 2.7 copy-start.15
  267.6 2.6 copy-start.17
  267.6 2.6 copy-start.21
  267.6 2.6 copy-start.23
  267.6 2.6 copy-start.25
  273.6 20.5 %copy-start = (bf16[5120,128]{1,0:T(8,128)(2,1)S(1)}, bf16[5120,128]{1,0:T(8,128)(2,1)}, u32[]{:S(2)}) copy-start(bf16[5120,128]{1,0:T(8,128)(2,1)} %all-gather.6.cloned.1.call-done) | copy-start | bytes 3932164
  294.1 6.0 %copy-start.18 = (bf16[128,128]{1,0:T(8,128)(2,1)S(1)}, bf16[128,128]{1,0:T(8,128)(2,1)}, u32[]{:S(2)}) copy-start(bf16[128,128]{1,0:T(8,128)(2,1)} %get-tuple-element.806.q) | copy-start | bytes 98308
  294.6 8.7 %collective-permute-start.2 = (f32[80,128]{1,0:T(8,128)S(1)}, f32[80,128]{1,0:T(8,128)S(1)}, u32[]{:S(2)}, u32[]{:S(2)}) collective-permute-start(f32[80,128]{1,0:T(8,128)S(1)} %slice_select_fusion), channel_id=1, source_target_pairs={{0,32},{32,0},{1,33},{33,1},{2,34},{34,2},{3,35},{35,3},{4,36},{36... | collective-permute-start | bytes 122888 | tf_op jit(solution)/shard_map/sum/ppermute | solution.py:330
Sparse Core Ops, SparseCore 0:
  23.2 91.5 all-gather.3
  120.1 77.6 all-gather.5

commit v2 on v1

v2 whole, which is shorter than its diff:
```python
import functools

import jax
import jax.numpy as jnp
from jax import lax
from jax.experimental import pallas as pl
from jax.experimental.pallas import tpu as pltpu
from jax.sharding import Mesh
from jax.sharding import PartitionSpec as P


eps = 1e-06
bf16 = jnp.bfloat16
f32 = jnp.float32
PARTS = 4
SECTION = ("zl", "core")
PLANE = ("y", "x")
DP = ("zh", "y", "x")
VMEM = pl.BlockSpec(memory_space=pltpu.VMEM)
ANY = pl.BlockSpec(memory_space=pl.ANY)
SMEM = pl.BlockSpec(memory_space=pltpu.SMEM)


def dot(a, b, ca=1, cb=0):
    return lax.dot_general(a, b, (((ca,), (cb,)), ((), ())), preferred_element_type=f32)


def near(a):
    return pltpu.with_memory_space_constraint(a, pltpu.VMEM)


def chunk_of(width):
    return 640 if width % 640 == 0 else width


def forward_kernel(
    len_ref, normed, wa, wb, kc, vc, eo, w, q_ref, kn_ref, vn_ref, pc_ref, pn_ref, proj_ref, att_ref, sem_a, sem_b,
):
    hd = kc.shape[1]
    rows = normed.shape[0]
    nx, ny, shard, _ = wb.shape
    half = nx * ny * shard
    step = chunk_of(half)
    take_a = [
        pltpu.make_async_copy(
            wa.at[p // nx, lax.rem(len_ref[1] - p % nx + nx, nx)], w.at[pl.ds(p * shard, shard), :], sem_a.at[p]
        )
        for p in range(nx * ny)
    ]
    take_b = [
        pltpu.make_async_copy(wb.at[p % nx, p // nx], w.at[pl.ds(half + p * shard, shard), :], sem_b.at[p])
        for p in range(nx * ny)
    ]
    for copy in take_a + take_b:
        copy.start()
    acc = jnp.zeros((rows, 3 * hd), f32)
    for h in range(2):
        for c in range(0, half, step):
            for p in range(c // shard, (c + step) // shard):
                (take_a, take_b)[h][p].wait()
            at = h * half + c
            acc = acc + dot(normed[:, at : at + step], w[at : at + step, : 3 * hd])
    proj_ref[...] = acc
    low = acc.astype(bf16)
    q = low[:, :hd]
    kn = low[:, hd : 2 * hd]
    vn = low[:, 2 * hd :]
    q_ref[...] = q
    kn_ref[...] = kn
    vn_ref[...] = vn
    scale = hd ** (-0.5)
    sc = dot(q, kc[...], 1, 1) * scale
    sn = dot(q, kn, 1, 1) * scale
    see_c = lax.broadcasted_iota(jnp.int32, sc.shape, 1) < len_ref[0]
    see_n = lax.broadcasted_iota(jnp.int32, sn.shape, 1) <= lax.broadcasted_iota(jnp.int32, sn.shape, 0)
    sc = jnp.where(see_c, sc, -jnp.inf)
    sn = jnp.where(see_n, sn, -jnp.inf)
    top = jnp.maximum(jnp.max(sc, axis=1, keepdims=True), jnp.max(sn, axis=1, keepdims=True))
    wc = jnp.where(see_c, jnp.exp(sc - top), 0.0)
    wn = jnp.where(see_n, jnp.exp(sn - top), 0.0)
    total = jnp.sum(wc, axis=1, keepdims=True) + jnp.sum(wn, axis=1, keepdims=True)
    pc = wc / total
    pn = wn / total
    pc_ref[...] = pc
    pn_ref[...] = pn
    att_ref[:rows, :] = (dot(pc.astype(bf16), vc[...]) + dot(pn.astype(bf16), vn)).astype(bf16)
    att_ref[rows:, :] = eo[...]


def stage_kernel(
    flags, recv, top, w, x, gain, inv, q, kc, kn, vc, vn, pc, pn, proj, gkn_in, gvn_in, gsc_in, go_in,
    send, gkn, gvn, gsc, go_all, gin,
):
    rows = send.shape[0]
    hd = q.shape[1]
    width = w.shape[0]
    step = chunk_of(width // 2)
    scale = hd ** (-0.5)
    active = flags[0] == 1
    r0 = pl.multiple_of(flags[1] * rows, rows)
    is_top = flags[2] == 1
    mine = pl.ds(r0, rows)
    pieces = [slice(c, c + step) for c in range(0, width, step)]

    gkn[...] = gkn_in[...]
    gvn[...] = gvn_in[...]
    gsc[...] = gsc_in[...]
    go_all[...] = go_in[...]

    @pl.when(jnp.logical_and(active, is_top))
    def _():
        gin[...] = top[mine, :]

    @pl.when(jnp.logical_and(active, jnp.logical_not(is_top)))
    def _():
        gin[...] = recv[...]

    @pl.when(active)
    def _():
        acc = jnp.zeros((rows, hd), f32)
        for cols in pieces:
            acc = acc + dot(gin[:, cols], w[cols, 3 * hd :])
        go = acc.astype(bf16)
        go_all[mine, :] = go
        prob_c = pc[mine, :]
        prob_n = pn[mine, :]
        gp_c = dot(go, vc[...], 1, 1)
        gp_n = dot(go, vn[...], 1, 1)
        delta = jnp.sum(prob_c * gp_c, axis=1, keepdims=True) + jnp.sum(prob_n * gp_n, axis=1, keepdims=True)
        gs_c = (prob_c * (gp_c - delta) * scale).astype(bf16)
        gs_n = (prob_n * (gp_n - delta) * scale).astype(bf16)
        gsc[mine, :] = gs_c
        gq = dot(gs_c, kc[...]) + dot(gs_n, kn[...])
        gkn[...] += dot(gs_n, q[mine, :], 0, 0)
        gvn[...] += dot(prob_n.astype(bf16), go, 0, 0)
        gproj = jnp.concatenate([gq, gkn[mine, :], gvn[mine, :]], axis=1).astype(bf16)
        r = inv[mine, :]
        coef = r * r * jnp.sum(gproj.astype(f32) * proj[mine, :], axis=1, keepdims=True) * (1.0 / width)

        @pl.loop(0, width // step)
        def _(n):
            cols = pl.ds(pl.multiple_of(n * step, step), step)
            gn = dot(gproj, w[cols, : 3 * hd], 1, 1)
            out = gin[:, cols].astype(f32) + r * (gn * gain[:, cols]) - x[mine, cols].astype(f32) * coef
            send[:, cols] = out.astype(bf16)


def flip(block, out):
    planes, shard, _ = out.shape
    half = planes * shard
    pair = jnp.concatenate([block[:, :half], block[:, half:]], axis=0)
    turned = jnp.transpose(pair.astype(f32)).astype(bf16)
    for p in range(planes):
        out[p] = turned[p * shard : (p + 1) * shard, :]


def turn_early_half(gin, out):
    tokens = gin.shape[0]
    flip(gin[tokens // 2 :, :], out)


def turn_late_half(flag, gin, recv, out):
    tokens = gin.shape[0]
    rows = recv.shape[0]
    first = jnp.where(flag[0] == 1, recv[...], gin[:rows, :])
    flip(jnp.concatenate([first, gin[rows : tokens // 2, :]], axis=0), out)


def contract_kernel(start, got, att, sofar, out):
    planes, _, tokens = got.shape
    tokens = tokens // 2
    hd = att.shape[2]
    acc = sofar[...]
    none = jnp.zeros((tokens, hd), bf16)
    for p in range(0, planes, 2):
        lhs = jnp.concatenate([got[p], got[p + 1]], axis=1)
        rhs = []
        for b in (p, p + 1):
            a = att[b, start : start + tokens, :]
            rhs += [jnp.concatenate([a, none], axis=1), jnp.concatenate([none, a], axis=1)]
        acc = acc + dot(lhs, jnp.concatenate(rhs, axis=0))
    out[...] = acc


def body(x_in, top_grad, norm_gain, proj_in, proj_out, key_cache, value_cache, prefix_len, early_out, early_dy):
    sections = lax.axis_size(SECTION)
    section = lax.axis_index(SECTION)
    zh = lax.axis_index("zh")
    planes = lax.axis_size(PLANE)
    x = x_in[0]
    tokens, width = x.shape
    kc = key_cache[0]
    vc = value_cache[0]
    crow, hd = kc.shape
    shard = width // (2 * planes)
    erows = early_dy.shape[1]
    swap = [(0, 1), (1, 0)]

    own = jnp.concatenate([proj_in[0], jnp.transpose(proj_out[0])], axis=1)
    other = lax.ppermute(own, "zh", swap)
    lower = jnp.where(zh == 0, own, other)
    upper = jnp.where(zh == 0, other, own)
    nx = lax.axis_size("x")
    ny = lax.axis_size("y")
    along_y = lax.all_to_all(jnp.broadcast_to(upper[None], (ny, *upper.shape)), "y", 0, 0, tiled=True)
    turns_x = [lower] + [lax.ppermute(lower, "x", [(i, (i + d) % nx) for i in range(nx)]) for d in range(1, nx)]
    wa = lax.all_gather(jnp.stack(turns_x)[None], "y", axis=0, tiled=True)
    wb = lax.all_to_all(jnp.broadcast_to(along_y[None], (nx, *along_y.shape)), "x", 0, 0, tiled=True)

    wide = x.astype(f32)
    gain = norm_gain.astype(f32)
    inv = lax.rsqrt(jnp.mean(wide * wide, axis=1, keepdims=True) + eps)
    normed = (wide * inv * gain).astype(bf16)

    packed = early_dy[0].reshape(erows, 2, planes, 2, shard // 2)
    packed = packed.transpose(2, 4, 1, 3, 0).reshape(planes, shard // 2, 4 * erows)

    shape = jax.ShapeDtypeStruct
    room = pltpu.CompilerParams(vmem_limit_bytes=24 << 20)
    w, q, kn, vn, pc, pn, proj, att = pl.pallas_call(
        forward_kernel,
        name="forward",
        in_specs=[SMEM, VMEM, ANY, ANY, VMEM, VMEM, VMEM],
        out_specs=[VMEM] * 8,
        out_shape=[
            shape((width, 4 * hd), bf16),
            shape((tokens, hd), bf16),
            shape((tokens, hd), bf16),
            shape((tokens, hd), bf16),
            shape((tokens, crow), f32),
            shape((tokens, tokens), f32),
            shape((tokens, 3 * hd), f32),
            shape((tokens + erows, hd), bf16),
        ],
        scratch_shapes=[
            pltpu.SemaphoreType.DMA((planes,)),
            pltpu.SemaphoreType.DMA((planes,)),
        ],
        compiler_params=room,
    )(jnp.stack([prefix_len[0], lax.axis_index("x")]), normed, wa, wb, kc, vc, early_out[0])
    w = near(w)

    att_all = lax.all_gather(att[None], PLANE, axis=0, tiled=True)

    rows = tokens // PARTS
    stage = pl.pallas_call(
        stage_kernel,
        name="stage",
        in_specs=[SMEM] + [VMEM] * 18,
        out_specs=[VMEM] * 5,
        out_shape=[
            shape((rows, width), bf16),
            shape((tokens, hd), f32),
            shape((tokens, hd), f32),
            shape((tokens, crow), bf16),
            shape((tokens, hd), bf16),
        ],
        scratch_shapes=[pltpu.VMEM((rows, width), bf16)],
        input_output_aliases={15: 1, 16: 2, 17: 3, 18: 4},
        compiler_params=room,
    )
    is_top = section == sections - 1

    def place(t):
        part = sections - 1 - section + PARTS - 1 - t
        active = jnp.logical_and(part >= 0, part < PARTS)
        return jnp.clip(part, 0, PARTS - 1), active

    def keep(whole, piece, t, also):
        part, active = place(t)
        at = part * rows
        old = lax.dynamic_slice_in_dim(whole, at, rows, 0)
        return lax.dynamic_update_slice_in_dim(
            whole, jnp.where(jnp.logical_and(active, also), piece, old), at, 0
        )

    def compute(t, recv, state):
        part, active = place(t)
        flags = jnp.stack([active.astype(jnp.int32), part, is_top.astype(jnp.int32)])
        return stage(flags, recv, top_grad, w, x, gain, inv, q, kc, kn, vc, vn, pc, pn, proj, *state)

    packed, _ = lax.optimization_barrier((packed, att))
    early_got = lax.all_to_all(packed, PLANE, 0, 0, tiled=True)

    recv = jnp.zeros((rows, width), bf16)
    gin_all = jnp.where(is_top, top_grad, jnp.zeros_like(top_grad))
    gx_all = jnp.zeros((tokens, width), bf16)
    state = (
        jnp.zeros((tokens, hd), f32),
        jnp.zeros((tokens, hd), f32),
        jnp.zeros((tokens, crow), bf16),
        jnp.zeros((tokens, hd), bf16),
    )
    turns = sections + PARTS - 1
    block = shape((planes, shard, tokens), bf16)
    down = [(i, i - 1) for i in range(1, sections)]

    halfway = sections + PARTS // 2 - 2
    for t in range(turns):
        if t == turns - 1:
            flag = (section == 0).astype(jnp.int32)[None]
            late = pl.pallas_call(
                turn_late_half,
                name="turn_late",
                in_specs=[SMEM, VMEM, VMEM],
                out_specs=VMEM,
                out_shape=block,
                compiler_params=room,
            )(flag, gin_all, recv)
            recv, late, got_soon = lax.optimization_barrier((recv, late, got_soon))
            got_late = lax.all_to_all(late, PLANE, 0, 0, tiled=True)
        elif t > 0:
            gin_all = keep(gin_all, recv, t, jnp.logical_not(is_top))
        send, *state = compute(t, recv, state)
        gx_all = keep(gx_all, send, t, True)
        if t == halfway:
            gin_now, _, early_got = lax.optimization_barrier((gin_all, send, early_got))
            soon = pl.pallas_call(
                turn_early_half,
                name="turn_soon",
                in_specs=[VMEM],
                out_specs=VMEM,
                out_shape=block,
                compiler_params=room,
            )(gin_now)
            got_soon = lax.all_to_all(soon, PLANE, 0, 0, tiled=True)
        if t < turns - 1:
            recv = lax.ppermute(send, SECTION, down)
    _, _, gsc, go_all = state
    key_out = dot(gsc, q, 0, 0).astype(bf16)
    value_out = dot(pc.astype(bf16), go_all, 0, 0).astype(bf16)
    early_got, _ = lax.optimization_barrier((early_got, send))
    early_rows = early_got.reshape(planes, shard // 2, 4, erows)
    early = jnp.einsum("prqt,pth->qrh", early_rows, att_all[:, tokens:, :], preferred_element_type=f32)
    early = early.reshape(2, shard, hd)
    early = jnp.concatenate([early[0], early[1]], axis=1)

    def contract(start, got, sofar):
        return pl.pallas_call(
            functools.partial(contract_kernel, start),
            name="contract",
            in_specs=[VMEM] * 3,
            out_specs=VMEM,
            out_shape=shape((shard, 2 * hd), f32),
            compiler_params=room,
        )(got, att_all, sofar)

    whole = contract(tokens // 2, got_soon, early)
    whole = contract(0, got_late, whole)
    first, second = whole[:, :hd], whole[:, hd:]
    away = lax.ppermute(jnp.where(zh == 0, second, first), "zh", swap)
    wo = jnp.transpose(jnp.where(zh == 0, first, second) + away)
    return gx_all[None], key_out[None], value_out[None], wo[None]


def solution(mesh):
    ny, nx = (8, 4) if mesh.shape["dp"] == 64 else (2, mesh.shape["dp"] // 4)
    fine = Mesh(mesh.devices.reshape(mesh.shape["section"] // 2, 2, 2, ny, nx), ("zl", "core", "zh", "y", "x"))
    in_specs = (
        P(SECTION, DP, None),
        P(DP, None),
        P(SECTION, None),
        P(SECTION, DP, None),
        P(SECTION, None, DP),
        P(SECTION, DP, None),
        P(SECTION, DP, None),
        P(DP),
        P(SECTION, DP, None),
        P(SECTION, DP, None),
    )
    out_specs = (
        P(SECTION, DP, None),
        P(SECTION, DP, None),
        P(SECTION, DP, None),
        P(SECTION, None, DP),
    )
    return jax.shard_map(body, mesh=fine, in_specs=in_specs, out_specs=out_specs, check_vma=False)
```

time: 312 us -> 308 us (0.987)
  waiting for transfers between devices: 152 us -> 101 us
  starting transfers between devices: 55.6 us -> 90.9 us
  local copies, waits for them, and re-layouts: 15.7 us -> 42.3 us
  other arithmetic: 30.8 us -> 19.7 us
  Pallas kernels: 37.7 us -> 32.9 us
    all_gather x2, waiting for transfers between devices: 70.3 us -> 0.02 us  [the longest x1 0.02 us: body(): att_all = lax.all_gather(att[None], PLANE, axis=0, tiled=True)]
    unnamed x57 -> x113, local copies, waits for them, and re-layouts: 2.68 us -> 26.1 us
    all_to_all x1 -> x4, starting transfers between devices: 5.61 us -> 28.5 us  [the longest x1 9.3 us: body(): got_late = lax.all_to_all(late, PLANE, 0, 0, tiled=True)]
    all_to_all x1 -> x4, waiting for transfers between devices: 18.5 us -> 39.3 us  [the longest x1 22 us: body(): lax.all_to_all(jnp.broadcast_to(along_y[None], (nx, *along_y.shape)), 'x'...]
    dynamic_update_slice x12 -> x19, other arithmetic: 24.3 us -> 6.73 us  [keep(): lax.dynamic_update_slice_in_dim(whole, jnp.where(jnp.logical_and(active,...]
    ppermute x10 -> x13, starting transfers between devices: 22.9 us -> 38.4 us  [the longest x10 27.6 us: body(): recv = lax.ppermute(send, SECTION, down)]
    another operation x3 -> x6, local copies, waits for them, and re-layouts: 1.2 us -> 8.57 us  [the longest x2 8.41 us: body(): packed = early_dy[0].reshape(erows, 2, planes, 2, shard // 2)]
    squeeze x2 -> x0, local copies, waits for them, and re-layouts: 6.34 us -> none  [body(): packed = early_dy[0].reshape(erows, 2, planes, 2, shard // 2)]
  transfers between devices with their start and end apart: 16 -> 22, of which waited for: 14 -> 15; matrix products, arithmetic and copies ran while one was open for 15% -> 12% of each run, Pallas kernels for 12% -> 8%
where the time goes in v2:
time: 308 us; the launch traced here: 305 us
  waiting for transfers between devices  101 us (33%)
  starting transfers between devices  90.9 us (30%)
  local copies, waits for them, and re-layouts  42.3 us (14%)
  Pallas kernels  32.9 us (11%)
  other arithmetic  19.7 us (6%)
  between operations  15.4 us (5%)
  matrix products  3.11 us (1%)
    ppermute x10, waiting for transfers between devices, body(): recv = lax.ppermute(send, SECTION, down)  55.7 us
    ppermute x10, starting transfers between devices, body(): recv = lax.ppermute(send, SECTION, down)  27.6 us
    unnamed x113, local copies, waits for them, and re-layouts  26.1 us
    pallas_call x11, Pallas kernels, compute(): stage(flags, recv, top_grad, w, x, gain, inv, q, kc, kn, vc, vn, pc, pn,...  22.3 us
    all_to_all x1, waiting for transfers between devices, body(): lax.all_to_all(jnp.broadcast_to(along_y[None], (nx, *along_y.shape)), 'x'...  22 us
    all_to_all x1, waiting for transfers between devices, body(): got_late = lax.all_to_all(late, PLANE, 0, 0, tiled=True)  15.3 us
    ppermute x1, starting transfers between devices, body(): other = lax.ppermute(own, 'zh', swap)  11.5 us
    ppermute x3, starting transfers between devices, body(): lax.ppermute(lower, 'x', [(i, (i + d) % nx) for i in range(nx)])  10.8 us
  transfers between devices with their start and end apart: 22, of which 15 were waited for; matrix products, arithmetic and copies ran while one was open for 12% of the time, Pallas kernels for 8%

profile of v2, /device:TPU:1, one launch (start us, length us, event | category | flops | bytes accessed | tf_op | source)
XLA Modules:
  0.0 305.3 jit_solution(9946505483539995356)
XLA Ops:
  8.2 11.5 %collective-permute-start = (bf16[80,512]{1,0:T(8,128)(2,1)S(1)}, bf16[80,512]{1,0:T(8,128)(2,1)S(1)}, u32[]{:S(2)}, u32[]{:S(2)}) collective-permute-start(bf16[80,512]{1,0:T(8,128)(2,1)S(1)} %pad_maximum_fusion.1), channel_id=1, source_target_pairs={{0,32},{32,0},{1,33},{33,1},{2,34},{34,2},{3,35},{35,3},{4,36},{36... | collective-permute-start | bytes 245768 | tf_op jit(solution)/shard_map/ppermute | solution.py:200
  19.6 1.9 collective-permute-done
  22.4 3.3 %collective-permute-start.1 = (bf16[80,512]{1,0:T(8,128)(2,1)S(1)}, bf16[80,512]{1,0:T(8,128)(2,1)S(1)}, u32[]{:S(2)}, u32[]{:S(2)}) collective-permute-start(bf16[80,512]{1,0:T(8,128)(2,1)S(1)} %get-tuple-element.141), channel_id=1, source_target_pairs={{0,1},{1,2},{2,3},{3,0},{4,5},{5,6},{6,7},{7,4},{8,9},{9,10},{10,1... | collective-permute-start | bytes 245768 | tf_op jit(solution)/shard_map/ppermute | solution.py:206
  25.8 4.4 %collective-permute-start.2 = (bf16[80,512]{1,0:T(8,128)(2,1)S(1)}, bf16[80,512]{1,0:T(8,128)(2,1)S(1)}, u32[]{:S(2)}, u32[]{:S(2)}) collective-permute-start(bf16[80,512]{1,0:T(8,128)(2,1)S(1)} %get-tuple-element.141), channel_id=1, source_target_pairs={{0,2},{1,3},{2,0},{3,1},{4,6},{5,7},{6,4},{7,5},{8,10},{9,11},{10,... | collective-permute-start | bytes 245768 | tf_op jit(solution)/shard_map/ppermute | solution.py:206
  30.1 3.1 %collective-permute-start.3 = (bf16[80,512]{1,0:T(8,128)(2,1)S(1)}, bf16[80,512]{1,0:T(8,128)(2,1)S(1)}, u32[]{:S(2)}, u32[]{:S(2)}) collective-permute-start(bf16[80,512]{1,0:T(8,128)(2,1)S(1)} %get-tuple-element.141), channel_id=1, source_target_pairs={{0,3},{1,0},{2,1},{3,2},{4,7},{5,4},{6,5},{7,6},{8,11},{9,8},{10,9... | collective-permute-start | bytes 245768 | tf_op jit(solution)/shard_map/ppermute | solution.py:206
  33.2 2.7 collective-permute-done.3
  38.8 6.8 %all-to-all-start = ((bf16[8,80,512]{2,1,0:T(8,128)(2,1)}), bf16[8,80,512]{2,1,0:T(8,128)(2,1)}, u32[]{:S(2)}, u32[]{:S(2)}) async-start(bf16[8,80,512]{2,1,0:T(8,128)(2,1)} %broadcast_in_dim.45), calls=%async_computation | async-start | bytes 1310720 | tf_op jit(solution)/shard_map/all_to_all | solution.py:205
  46.3 2.9 reshape_squeeze.3
  49.2 5.6 %copy.106 = bf16[32,2,32,2,40]{0,3,1,4,2:T(2,128)(2,1)S(1)} copy(bf16[32,2,32,2,40]{4,3,2,1,0:T(2,128)(2,1)} %reshape_squeeze.3) | data formatting | bytes 655360 | tf_op jit(solution)/shard_map/reshape;squeeze | solution.py:215
  62.2 2.0 all-to-all-done
  64.2 2.9 broadcast_in_dim.46
  67.1 4.7 %all-to-all-start.1 = ((bf16[4,8,80,512]{3,2,1,0:T(8,128)(2,1)}), bf16[4,8,80,512]{3,2,1,0:T(8,128)(2,1)}, u32[]{:S(2)}, u32[]{:S(2)}) async-start(bf16[4,8,80,512]{3,2,1,0:T(8,128)(2,1)} %broadcast_in_dim.46), calls=%async_computation.1 | async-start | bytes 5242880 | tf_op jit(solution)/shard_map/all_to_all | solution.py:208
  74.5 22.0 %all-to-all-done.1.wb = bf16[4,8,80,512]{3,2,1,0:T(8,128)(2,1)} async-done(((bf16[4,8,80,512]{3,2,1,0:T(8,128)(2,1)}), bf16[4,8,80,512]{3,2,1,0:T(8,128)(2,1)}, u32[]{:S(2)}, u32[]{:S(2)}) %all-to-all-start.1) | async-done | bytes 2621472 | tf_op jit(solution)/shard_map/all_to_all | solution.py:208
  99.6 7.1 %forward.1 = (bf16[5120,512]{1,0:T(8,128)(2,1)S(1)}, bf16[128,128]{1,0:T(8,128)(2,1)S(1)}, bf16[128,128]{1,0:T(8,128)(2,1)S(1)}, bf16[128,128]{1,0:T(8,128)(2,1)...) custom-call(s32[2]{0:T(128)S(1)} %pad_add_fusion.len_ref, ...), custom_call_target="tpu_custom_call" | custom-call | tf_op jit(solution)/shard_map/forward/pallas_call | solution.py:220
  107.5 1.9 stage.11
  109.9 10.2 %collective-permute-start.4 = (bf16[32,5120]{1,0:T(8,128)(2,1)}, bf16[32,5120]{1,0:T(8,128)(2,1)}, u32[]{:S(2)}, u32[]{:S(2)}) collective-permute-start(bf16[32,5120]{1,0:T(8,128)(2,1)} %get-tuple-element.79), channel_id=1, source_target_pairs={{64,0},{128,64},{192,128},{256,192},{320,256},{384,320},{448,384},... | collective-permute-start | bytes 983048 | tf_op jit(solution)/shard_map/ppermute | solution.py:328
  120.1 5.8 %all-to-all-start.2 = ((bf16[32,40,128]{2,1,0:T(8,128)(2,1)}), bf16[32,40,128]{2,1,0:T(8,128)(2,1)}, u32[]{:S(2)}, u32[]{:S(2)}) async-start(bf16[32,40,128]{2,1,0:T(8,128)(2,1)} %reshape.44), calls=%async_computation.2 | async-start | bytes 655360 | tf_op jit(solution)/shard_map/all_to_all | solution.py:283
  126.7 2.5 copy-done.1
  130.3 1.9 collective-permute-start.5
  132.5 6.6 %collective-permute-done.5.recv = bf16[32,5120]{1,0:T(8,128)(2,1)S(1)} collective-permute-done((bf16[32,5120]{1,0:T(8,128)(2,1)S(1)}, bf16[32,5120]{1,0:T(8,128)(2,1)S(1)}, u32[]{:S(2)}, u32[]{:S(2)}) %collective-permute-start.5) | collective-permute-done | bytes 327712 | tf_op jit(solution)/shard_map/ppermute | solution.py:328
  139.7 1.9 collective-permute-start.6
  141.9 6.6 %collective-permute-done.6.recv = bf16[32,5120]{1,0:T(8,128)(2,1)S(1)} collective-permute-done((bf16[32,5120]{1,0:T(8,128)(2,1)S(1)}, bf16[32,5120]{1,0:T(8,128)(2,1)S(1)}, u32[]{:S(2)}, u32[]{:S(2)}) %collective-permute-start.6) | collective-permute-done | bytes 327712 | tf_op jit(solution)/shard_map/ppermute | solution.py:328
  149.1 1.9 collective-permute-start.7
  151.2 6.7 %collective-permute-done.7.recv = bf16[32,5120]{1,0:T(8,128)(2,1)S(1)} collective-permute-done((bf16[32,5120]{1,0:T(8,128)(2,1)S(1)}, bf16[32,5120]{1,0:T(8,128)(2,1)S(1)}, u32[]{:S(2)}, u32[]{:S(2)}) %collective-permute-start.7) | collective-permute-done | bytes 327712 | tf_op jit(solution)/shard_map/ppermute | solution.py:328
  158.5 2.1 collective-permute-start.8
  160.8 6.1 %collective-permute-done.8.recv = bf16[32,5120]{1,0:T(8,128)(2,1)S(1)} collective-permute-done((bf16[32,5120]{1,0:T(8,128)(2,1)S(1)}, bf16[32,5120]{1,0:T(8,128)(2,1)S(1)}, u32[]{:S(2)}, u32[]{:S(2)}) %collective-permute-start.8) | collective-permute-done | bytes 327712 | tf_op jit(solution)/shard_map/ppermute | solution.py:328
  167.5 1.9 collective-permute-start.9
  169.6 12.8 %collective-permute-done.9.recv = bf16[32,5120]{1,0:T(8,128)(2,1)S(1)} collective-permute-done((bf16[32,5120]{1,0:T(8,128)(2,1)S(1)}, bf16[32,5120]{1,0:T(8,128)(2,1)S(1)}, u32[]{:S(2)}, u32[]{:S(2)}) %collective-permute-start.9) | collective-permute-done | bytes 327712 | tf_op jit(solution)/shard_map/ppermute | solution.py:328
  182.4 3.8 %stage.17 = (bf16[32,5120]{1,0:T(8,128)(2,1)S(1)}, f32[128,128]{1,0:T(8,128)S(1)}, f32[128,128]{1,0:T(8,128)S(1)}, bf16[128,288]{1,0:T(8,128)(2,1)S(1)}, bf16[128,128]{1,0:T(8,128)(2,1)S(1)}) custom-call(s32[3]{0:T(128)S(1)} %copy-done.45, ...), custom_call_target="tpu_custom_call", output_to_operand_aliasing={{1}: (15, {}), {2}: (16, {}), {3}: (17, {}), {4}: (18, {})} | custom-call | tf_op jit(solution)/shard_map/stage/pallas_call | solution.py:280
  186.2 1.9 collective-permute-start.10
  188.3 6.7 %collective-permute-done.10.recv = bf16[32,5120]{1,0:T(8,128)(2,1)S(1)} collective-permute-done((bf16[32,5120]{1,0:T(8,128)(2,1)S(1)}, bf16[32,5120]{1,0:T(8,128)(2,1)S(1)}, u32[]{:S(2)}, u32[]{:S(2)}) %collective-permute-start.10) | collective-permute-done | bytes 327712 | tf_op jit(solution)/shard_map/ppermute | solution.py:328
  195.0 3.7 %stage.18 = (bf16[32,5120]{1,0:T(8,128)(2,1)S(1)}, f32[128,128]{1,0:T(8,128)S(1)}, f32[128,128]{1,0:T(8,128)S(1)}, bf16[128,288]{1,0:T(8,128)(2,1)S(1)}, bf16[128,128]{1,0:T(8,128)(2,1)S(1)}) custom-call(s32[3]{0:T(128)S(1)} %copy-done.44, ...), custom_call_target="tpu_custom_call", output_to_operand_aliasing={{1}: (15, {}), {2}: (16, {}), {3}: (17, {}), {4}: (18, {})} | custom-call | tf_op jit(solution)/shard_map/stage/pallas_call | solution.py:280
  198.7 1.9 collective-permute-start.11
  200.9 6.2 %collective-permute-done.11.recv = bf16[32,5120]{1,0:T(8,128)(2,1)S(1)} collective-permute-done((bf16[32,5120]{1,0:T(8,128)(2,1)S(1)}, bf16[32,5120]{1,0:T(8,128)(2,1)S(1)}, u32[]{:S(2)}, u32[]{:S(2)}) %collective-permute-start.11) | collective-permute-done | bytes 327712 | tf_op jit(solution)/shard_map/ppermute | solution.py:328
  207.1 4.5 %stage.19 = (bf16[32,5120]{1,0:T(8,128)(2,1)}, f32[128,128]{1,0:T(8,128)S(1)}, f32[128,128]{1,0:T(8,128)S(1)}, bf16[128,288]{1,0:T(8,128)(2,1)S(1)}, bf16[128,128]{1,0:T(8,128)(2,1)S(1)}) custom-call(s32[3]{0:T(128)S(1)} %copy-done.43, ...), custom_call_target="tpu_custom_call", output_to_operand_aliasing={{1}: (15, {}), {2}: (16, {}), {3}: (17, {}), {4}: (18, {})} | custom-call | tf_op jit(solution)/shard_map/stage/pallas_call | solution.py:280
  211.6 1.9 collective-permute-start.12
  217.2 7.7 %all-to-all-start.3 = ((bf16[32,80,128]{2,1,0:T(8,128)(2,1)}), bf16[32,80,128]{2,1,0:T(8,128)(2,1)}, u32[]{:S(2)}, u32[]{:S(2)}) async-start(bf16[32,80,128]{2,1,0:T(8,128)(2,1)} %copy-done.33), calls=%async_computation.3 | async-start | bytes 1310720 | tf_op jit(solution)/shard_map/all_to_all | solution.py:326
  225.0 1.9 select_dynamic-update-slice_fusion.10
  226.9 2.5 copy-done.2
  233.0 4.3 %stage.20 = (bf16[32,5120]{1,0:T(8,128)(2,1)S(1)}, f32[128,128]{1,0:T(8,128)S(1)}, f32[128,128]{1,0:T(8,128)S(1)}, bf16[128,288]{1,0:T(8,128)(2,1)S(1)}, bf16[128,128]{1,0:T(8,128)(2,1)S(1)}) custom-call(s32[3]{0:T(128)S(1)} %copy-done.41, ...), custom_call_target="tpu_custom_call", output_to_operand_aliasing={{1}: (15, {}), {2}: (16, {}), {3}: (17, {}), {4}: (18, {})} | custom-call | tf_op jit(solution)/shard_map/stage/pallas_call | solution.py:280
  237.3 1.9 collective-permute-start.13
  241.8 3.9 %collective-permute-done.13.recv = bf16[32,5120]{1,0:T(8,128)(2,1)S(1)} collective-permute-done((bf16[32,5120]{1,0:T(8,128)(2,1)S(1)}, bf16[32,5120]{1,0:T(8,128)(2,1)S(1)}, u32[]{:S(2)}, u32[]{:S(2)}) %collective-permute-start.13) | collective-permute-done | bytes 327712 | tf_op jit(solution)/shard_map/ppermute | solution.py:328
  247.6 2.5 copy-done.3
  256.0 2.3 reshape.45
  259.7 9.3 %all-to-all-start.4 = ((bf16[32,80,128]{2,1,0:T(8,128)(2,1)}), bf16[32,80,128]{2,1,0:T(8,128)(2,1)S(1)}, u32[]{:S(2)}, u32[]{:S(2)}) async-start(bf16[32,80,128]{2,1,0:T(8,128)(2,1)} %turn_late.1), calls=%async_computation.4 | async-start | bytes 1310720 | tf_op jit(solution)/shard_map/all_to_all | solution.py:311
  271.5 1.8 bitcast_dynamic-update-slice_fusion
  273.3 15.3 %all-to-all-done.4.got = bf16[32,80,128]{2,1,0:T(8,128)(2,1)S(1)} async-done(((bf16[32,80,128]{2,1,0:T(8,128)(2,1)}), bf16[32,80,128]{2,1,0:T(8,128)(2,1)S(1)}, u32[]{:S(2)}, u32[]{:S(2)}) %all-to-all-start.4) | async-done | bytes 655392 | tf_op jit(solution)/shard_map/all_to_all | solution.py:311
  289.1 6.7 %collective-permute-start.14 = (f32[80,128]{1,0:T(8,128)S(1)}, f32[80,128]{1,0:T(8,128)S(1)}, u32[]{:S(2)}, u32[]{:S(2)}) collective-permute-start(f32[80,128]{1,0:T(8,128)S(1)} %slice_select_fusion), channel_id=1, source_target_pairs={{0,32},{32,0},{1,33},{33,1},{2,34},{34,2},{3,35},{35,3},{4,36},{36... | collective-permute-start | bytes 122888 | tf_op jit(solution)/shard_map/ppermute | solution.py:351
  (186 shorter events, 49.6 us)
Async XLA Ops:
  7.2 30.3 %copy-start.4 = (bf16[1,128,5120]{2,1,0:T(8,128)(2,1)S(1)}, bf16[1,128,5120]{2,1,0:T(8,128)(2,1)}, u32[]{:S(2)}) copy-start(bf16[1,128,5120]{2,1,0:T(8,128)(2,1)} %param.10) | copy-start | bytes 3932164
  7.2 89.3 %all-gather.5.cloned.1.call-start = ((), (), s32[]{:S(2)}) async-start(), calls=%async_computation.5 | async-start | bytes 2949120 | tf_op jit(solution)/shard_map/all_gather | solution.py:207
  8.2 13.4 %collective-permute-start = (bf16[80,512]{1,0:T(8,128)(2,1)S(1)}, bf16[80,512]{1,0:T(8,128)(2,1)S(1)}, u32[]{:S(2)}, u32[]{:S(2)}) collective-permute-start(bf16[80,512]{1,0:T(8,128)(2,1)S(1)} %pad_maximum_fusion.1), channel_id=1, source_target_pairs={{0,32},{32,0},{1,33},{33,1},{2,34},{34,2},{3,35},{35,3},{4,36},{36... | collective-permute-start | bytes 245768 | tf_op jit(solution)/shard_map/ppermute | solution.py:200
  22.4 10.8 %collective-permute-start.1 = (bf16[80,512]{1,0:T(8,128)(2,1)S(1)}, bf16[80,512]{1,0:T(8,128)(2,1)S(1)}, u32[]{:S(2)}, u32[]{:S(2)}) collective-permute-start(bf16[80,512]{1,0:T(8,128)(2,1)S(1)} %get-tuple-element.141), channel_id=1, source_target_pairs={{0,1},{1,2},{2,3},{3,0},{4,5},{5,6},{6,7},{7,4},{8,9},{9,10},{10,1... | collective-permute-start | bytes 245768 | tf_op jit(solution)/shard_map/ppermute | solution.py:206
  25.8 7.4 %collective-permute-start.2 = (bf16[80,512]{1,0:T(8,128)(2,1)S(1)}, bf16[80,512]{1,0:T(8,128)(2,1)S(1)}, u32[]{:S(2)}, u32[]{:S(2)}) collective-permute-start(bf16[80,512]{1,0:T(8,128)(2,1)S(1)} %get-tuple-element.141), channel_id=1, source_target_pairs={{0,2},{1,3},{2,0},{3,1},{4,6},{5,7},{6,4},{7,5},{8,10},{9,11},{10,... | collective-permute-start | bytes 245768 | tf_op jit(solution)/shard_map/ppermute | solution.py:206
  30.1 5.8 %collective-permute-start.3 = (bf16[80,512]{1,0:T(8,128)(2,1)S(1)}, bf16[80,512]{1,0:T(8,128)(2,1)S(1)}, u32[]{:S(2)}, u32[]{:S(2)}) collective-permute-start(bf16[80,512]{1,0:T(8,128)(2,1)S(1)} %get-tuple-element.141), channel_id=1, source_target_pairs={{0,3},{1,0},{2,1},{3,2},{4,7},{5,4},{6,5},{7,6},{8,11},{9,8},{10,9... | collective-permute-start | bytes 245768 | tf_op jit(solution)/shard_map/ppermute | solution.py:206
  37.8 8.3 %copy-start.55 = (bf16[1,5120]{1,0:T(2,128)(2,1)S(1)}, bf16[1,5120]{1,0:T(2,128)(2,1)}, u32[]{:S(2)}) copy-start(bf16[1,5120]{1,0:T(2,128)(2,1)} %param.12) | copy-start | bytes 30724
  37.8 8.5 %copy-start.54 = (bf16[1,32,5120]{2,1,0:T(8,128)(2,1)S(1)}, bf16[1,32,5120]{2,1,0:T(8,128)(2,1)}, u32[]{:S(2)}) copy-start(bf16[1,32,5120]{2,1,0:T(8,128)(2,1)} %param.19) | copy-start | bytes 983044
  38.8 25.4 %all-to-all-start = ((bf16[8,80,512]{2,1,0:T(8,128)(2,1)}), bf16[8,80,512]{2,1,0:T(8,128)(2,1)}, u32[]{:S(2)}, u32[]{:S(2)}) async-start(bf16[8,80,512]{2,1,0:T(8,128)(2,1)} %broadcast_in_dim.45), calls=%async_computation | async-start | bytes 1310720 | tf_op jit(solution)/shard_map/all_to_all | solution.py:205
  46.2 26.8 %copy-start.27 = (f32[1,5120]{1,0:T(1,128)}, f32[1,5120]{1,0:T(1,128)S(1)}, u32[]{:S(2)}) copy-start(f32[1,5120]{1,0:T(1,128)S(1)} %convert_element_type.13.gain) | copy-start | bytes 61444
  67.1 4.7 %copy-start.5 = (bf16[128,5120]{1,0:T(8,128)(2,1)S(1)}, bf16[128,5120]{1,0:T(8,128)(2,1)}, u32[]{:S(2)}) copy-start(bf16[128,5120]{1,0:T(8,128)(2,1)} %top.21) | copy-start | bytes 3932164
  67.1 29.4 %all-to-all-start.1 = ((bf16[4,8,80,512]{3,2,1,0:T(8,128)(2,1)}), bf16[4,8,80,512]{3,2,1,0:T(8,128)(2,1)}, u32[]{:S(2)}, u32[]{:S(2)}) async-start(bf16[4,8,80,512]{3,2,1,0:T(8,128)(2,1)} %broadcast_in_dim.46), calls=%async_computation.1 | async-start | bytes 5242880 | tf_op jit(solution)/shard_map/all_to_all | solution.py:208
  71.8 186.5 %all-gather.7.cloned.1.call-start = ((), (), s32[]{:S(2)}) async-start(), calls=%async_computation.6 | async-start | bytes 1351680 | tf_op jit(solution)/shard_map/all_gather | solution.py:243
  73.0 23.5 %copy-start.10 = (bf16[1,288,128]{2,1,0:T(8,128)(2,1)S(1)}, bf16[1,288,128]{2,1,0:T(8,128)(2,1)}, u32[]{:S(2)}) copy-start(bf16[1,288,128]{2,1,0:T(8,128)(2,1)} %param.15) | copy-start | bytes 221188
  73.0 23.5 %copy-start.11 = (bf16[1,288,128]{2,1,0:T(8,128)(2,1)S(1)}, bf16[1,288,128]{2,1,0:T(8,128)(2,1)}, u32[]{:S(2)}) copy-start(bf16[1,288,128]{2,1,0:T(8,128)(2,1)} %param.16) | copy-start | bytes 221188
  73.0 23.5 %copy-start.39 = (bf16[1,32,128]{2,1,0:T(8,128)(2,1)S(1)}, bf16[1,32,128]{2,1,0:T(8,128)(2,1)}, u32[]{:S(2)}) copy-start(bf16[1,32,128]{2,1,0:T(8,128)(2,1)} %param.18) | copy-start | bytes 24580
  99.6 7.9 %copy-start.28 = (f32[1,5120]{1,0:T(1,128)S(1)}, f32[1,5120]{1,0:T(1,128)}, u32[]{:S(2)}) copy-start(f32[1,5120]{1,0:T(1,128)} %copy-done.27) | copy-start | bytes 61444
  99.6 7.9 %copy-start.42 = (s32[3]{0:T(128)S(1)}, s32[3]{0:T(128)}, u32[]{:S(2)}) copy-start(s32[3]{0:T(128)} %add_add_fusion.flags) | copy-start | bytes 40
  107.3 2.5 copy-start.19
  107.3 2.5 copy-start.23
  109.9 16.5 %collective-permute-start.4 = (bf16[32,5120]{1,0:T(8,128)(2,1)}, bf16[32,5120]{1,0:T(8,128)(2,1)}, u32[]{:S(2)}, u32[]{:S(2)}) collective-permute-start(bf16[32,5120]{1,0:T(8,128)(2,1)} %get-tuple-element.79), channel_id=1, source_target_pairs={{64,0},{128,64},{192,128},{256,192},{320,256},{384,320},{448,384},... | collective-permute-start | bytes 983048 | tf_op jit(solution)/shard_map/ppermute | solution.py:328
  120.1 94.8 %all-to-all-start.2 = ((bf16[32,40,128]{2,1,0:T(8,128)(2,1)}), bf16[32,40,128]{2,1,0:T(8,128)(2,1)}, u32[]{:S(2)}, u32[]{:S(2)}) async-start(bf16[32,40,128]{2,1,0:T(8,128)(2,1)} %reshape.44), calls=%async_computation.2 | async-start | bytes 655360 | tf_op jit(solution)/shard_map/all_to_all | solution.py:283
  129.1 3.2 %copy-start.6 = (bf16[128,5120]{1,0:T(8,128)(2,1)S(1)}, bf16[128,5120]{1,0:T(8,128)(2,1)}, u32[]{:S(2)}) copy-start(bf16[128,5120]{1,0:T(8,128)(2,1)} %broadcast_select_fusion) | copy-start | bytes 3932164
  130.3 8.8 %copy-start.49 = (s32[3]{0:T(128)S(1)}, s32[3]{0:T(128)}, u32[]{:S(2)}) copy-start(s32[3]{0:T(128)} %add_add_fusion.2.flags) | copy-start | bytes 40
  130.3 8.8 %collective-permute-start.5 = (bf16[32,5120]{1,0:T(8,128)(2,1)S(1)}, bf16[32,5120]{1,0:T(8,128)(2,1)S(1)}, u32[]{:S(2)}, u32[]{:S(2)}) collective-permute-start(bf16[32,5120]{1,0:T(8,128)(2,1)S(1)} %get-tuple-element.84), channel_id=1, source_target_pairs={{64,0},{128,64},{192,128},{256,192},{320,256},{384,320},{448,384},... | collective-permute-start | bytes 983048 | tf_op jit(solution)/shard_map/ppermute | solution.py:328
  139.7 8.7 %copy-start.48 = (s32[3]{0:T(128)S(1)}, s32[3]{0:T(128)}, u32[]{:S(2)}) copy-start(s32[3]{0:T(128)} %add_add_fusion.3.flags) | copy-start | bytes 40
  139.7 8.7 %collective-permute-start.6 = (bf16[32,5120]{1,0:T(8,128)(2,1)S(1)}, bf16[32,5120]{1,0:T(8,128)(2,1)S(1)}, u32[]{:S(2)}, u32[]{:S(2)}) collective-permute-start(bf16[32,5120]{1,0:T(8,128)(2,1)S(1)} %get-tuple-element.89), channel_id=1, source_target_pairs={{64,0},{128,64},{192,128},{256,192},{320,256},{384,320},{448,384},... | collective-permute-start | bytes 983048 | tf_op jit(solution)/shard_map/ppermute | solution.py:328
  149.1 8.8 %copy-start.47 = (s32[3]{0:T(128)S(1)}, s32[3]{0:T(128)}, u32[]{:S(2)}) copy-start(s32[3]{0:T(128)} %add_add_fusion.4.flags) | copy-start | bytes 40
  149.1 8.8 %collective-permute-start.7 = (bf16[32,5120]{1,0:T(8,128)(2,1)S(1)}, bf16[32,5120]{1,0:T(8,128)(2,1)S(1)}, u32[]{:S(2)}, u32[]{:S(2)}) collective-permute-start(bf16[32,5120]{1,0:T(8,128)(2,1)S(1)} %get-tuple-element.94), channel_id=1, source_target_pairs={{64,0},{128,64},{192,128},{256,192},{320,256},{384,320},{448,384},... | collective-permute-start | bytes 983048 | tf_op jit(solution)/shard_map/ppermute | solution.py:328
  158.5 8.4 %copy-start.46 = (s32[3]{0:T(128)S(1)}, s32[3]{0:T(128)}, u32[]{:S(2)}) copy-start(s32[3]{0:T(128)} %add_add_fusion.5.flags) | copy-start | bytes 40
  158.5 8.4 %collective-permute-start.8 = (bf16[32,5120]{1,0:T(8,128)(2,1)S(1)}, bf16[32,5120]{1,0:T(8,128)(2,1)S(1)}, u32[]{:S(2)}, u32[]{:S(2)}) collective-permute-start(bf16[32,5120]{1,0:T(8,128)(2,1)S(1)} %get-tuple-element.99), channel_id=1, source_target_pairs={{64,0},{128,64},{192,128},{256,192},{320,256},{384,320},{448,384},... | collective-permute-start | bytes 983048 | tf_op jit(solution)/shard_map/ppermute | solution.py:328
  167.5 14.9 %copy-start.45 = (s32[3]{0:T(128)S(1)}, s32[3]{0:T(128)}, u32[]{:S(2)}) copy-start(s32[3]{0:T(128)} %add_add_fusion.6.flags) | copy-start | bytes 40
  167.5 14.9 %collective-permute-start.9 = (bf16[32,5120]{1,0:T(8,128)(2,1)S(1)}, bf16[32,5120]{1,0:T(8,128)(2,1)S(1)}, u32[]{:S(2)}, u32[]{:S(2)}) collective-permute-start(bf16[32,5120]{1,0:T(8,128)(2,1)S(1)} %get-tuple-element.104), channel_id=1, source_target_pairs={{64,0},{128,64},{192,128},{256,192},{320,256},{384,320},{448,384},... | collective-permute-start | bytes 983048 | tf_op jit(solution)/shard_map/ppermute | solution.py:328
  186.2 8.8 %copy-start.44 = (s32[3]{0:T(128)S(1)}, s32[3]{0:T(128)}, u32[]{:S(2)}) copy-start(s32[3]{0:T(128)} %add_add_fusion.7.flags) | copy-start | bytes 40
  186.2 8.8 %collective-permute-start.10 = (bf16[32,5120]{1,0:T(8,128)(2,1)S(1)}, bf16[32,5120]{1,0:T(8,128)(2,1)S(1)}, u32[]{:S(2)}, u32[]{:S(2)}) collective-permute-start(bf16[32,5120]{1,0:T(8,128)(2,1)S(1)} %get-tuple-element.109), channel_id=1, source_target_pairs={{64,0},{128,64},{192,128},{256,192},{320,256},{384,320},{448,384},... | collective-permute-start | bytes 983048 | tf_op jit(solution)/shard_map/ppermute | solution.py:328
  198.7 8.4 %copy-start.43 = (s32[3]{0:T(128)S(1)}, s32[3]{0:T(128)}, u32[]{:S(2)}) copy-start(s32[3]{0:T(128)} %add_add_fusion.8.flags) | copy-start | bytes 40
  198.7 8.4 %collective-permute-start.11 = (bf16[32,5120]{1,0:T(8,128)(2,1)S(1)}, bf16[32,5120]{1,0:T(8,128)(2,1)S(1)}, u32[]{:S(2)}, u32[]{:S(2)}) collective-permute-start(bf16[32,5120]{1,0:T(8,128)(2,1)S(1)} %get-tuple-element.114), channel_id=1, source_target_pairs={{64,0},{128,64},{192,128},{256,192},{320,256},{384,320},{448,384},... | collective-permute-start | bytes 983048 | tf_op jit(solution)/shard_map/ppermute | solution.py:328
  200.8 10.9 %copy-start.51 = (bf16[128,5120]{1,0:T(8,128)(2,1)}, bf16[128,5120]{1,0:T(8,128)(2,1)S(1)}, u32[]{:S(2)}) copy-start(bf16[128,5120]{1,0:T(8,128)(2,1)S(1)} %select_dynamic-update-slice_fusion.11) | copy-start | bytes 3932164
  211.6 15.2 %collective-permute-start.12 = (bf16[32,5120]{1,0:T(8,128)(2,1)}, bf16[32,5120]{1,0:T(8,128)(2,1)}, u32[]{:S(2)}, u32[]{:S(2)}) collective-permute-start(bf16[32,5120]{1,0:T(8,128)(2,1)} %get-tuple-element.119), channel_id=1, source_target_pairs={{64,0},{128,64},{192,128},{256,192},{320,256},{384,320},{448,384},... | collective-permute-start | bytes 983048 | tf_op jit(solution)/shard_map/ppermute | solution.py:328
  217.2 30.3 %all-to-all-start.3 = ((bf16[32,80,128]{2,1,0:T(8,128)(2,1)}), bf16[32,80,128]{2,1,0:T(8,128)(2,1)}, u32[]{:S(2)}, u32[]{:S(2)}) async-start(bf16[32,80,128]{2,1,0:T(8,128)(2,1)} %copy-done.33), calls=%async_computation.3 | async-start | bytes 1310720 | tf_op jit(solution)/shard_map/all_to_all | solution.py:326
  233.0 6.3 %copy-start.52 = (bf16[128,5120]{1,0:T(8,128)(2,1)S(1)}, bf16[128,5120]{1,0:T(8,128)(2,1)}, u32[]{:S(2)}) copy-start(bf16[128,5120]{1,0:T(8,128)(2,1)} %select_dynamic-update-slice_fusion.10) | copy-start | bytes 3932164
  233.0 6.4 %copy-start.9 = (bf16[128,5120]{1,0:T(8,128)(2,1)S(1)}, bf16[128,5120]{1,0:T(8,128)(2,1)}, u32[]{:S(2)}) copy-start(bf16[128,5120]{1,0:T(8,128)(2,1)} %copy-done.7) | copy-start | bytes 3932164
  237.3 8.4 %collective-permute-start.13 = (bf16[32,5120]{1,0:T(8,128)(2,1)S(1)}, bf16[32,5120]{1,0:T(8,128)(2,1)S(1)}, u32[]{:S(2)}, u32[]{:S(2)}) collective-permute-start(bf16[32,5120]{1,0:T(8,128)(2,1)S(1)} %get-tuple-element.124), channel_id=1, source_target_pairs={{64,0},{128,64},{192,128},{256,192},{320,256},{384,320},{448,384},... | collective-permute-start | bytes 983048 | tf_op jit(solution)/shard_map/ppermute | solution.py:328
  239.4 6.3 %copy-start.53 = (bf16[128,5120]{1,0:T(8,128)(2,1)}, bf16[128,5120]{1,0:T(8,128)(2,1)S(1)}, u32[]{:S(2)}) copy-start(bf16[128,5120]{1,0:T(8,128)(2,1)S(1)} %select_dynamic-update-slice_fusion.9) | copy-start | bytes 3932164
  259.7 9.3 %copy-start.12 = (bf16[5120,128]{1,0:T(8,128)(2,1)S(1)}, bf16[5120,128]{1,0:T(8,128)(2,1)}, u32[]{:S(2)}) copy-start(bf16[5120,128]{1,0:T(8,128)(2,1)} %all-gather.7.cloned.1.call-done) | copy-start | bytes 3932164
  259.7 28.9 %all-to-all-start.4 = ((bf16[32,80,128]{2,1,0:T(8,128)(2,1)}), bf16[32,80,128]{2,1,0:T(8,128)(2,1)S(1)}, u32[]{:S(2)}, u32[]{:S(2)}) async-start(bf16[32,80,128]{2,1,0:T(8,128)(2,1)} %turn_late.1), calls=%async_computation.4 | async-start | bytes 1310720 | tf_op jit(solution)/shard_map/all_to_all | solution.py:311
  273.3 22.6 %copy-start.18 = (bf16[128,128]{1,0:T(8,128)(2,1)S(1)}, bf16[128,128]{1,0:T(8,128)(2,1)}, u32[]{:S(2)}) copy-start(bf16[128,128]{1,0:T(8,128)(2,1)} %copy-done.14) | copy-start | bytes 98308
  289.1 8.7 %collective-permute-start.14 = (f32[80,128]{1,0:T(8,128)S(1)}, f32[80,128]{1,0:T(8,128)S(1)}, u32[]{:S(2)}, u32[]{:S(2)}) collective-permute-start(f32[80,128]{1,0:T(8,128)S(1)} %slice_select_fusion), channel_id=1, source_target_pairs={{0,32},{32,0},{1,33},{33,1},{2,34},{34,2},{3,35},{35,3},{4,36},{36... | collective-permute-start | bytes 122888 | tf_op jit(solution)/shard_map/ppermute | solution.py:351
  (30 other events, 35.5 us)
Sparse Core Ops, SparseCore 0:
  36.9 51.1 all-gather.4
  120.2 77.2 all-gather.6

commit v3 on v2

--- a/solution.py
+++ b/solution.py
@@ -1,5 +1,3 @@
-import functools
-
 import jax
 import jax.numpy as jnp
 from jax import lax
@@ -17,7 +15,7 @@
 PLANE = ("y", "x")
 DP = ("zh", "y", "x")
 VMEM = pl.BlockSpec(memory_space=pltpu.VMEM)
-ANY = pl.BlockSpec(memory_space=pl.ANY)
+HBM = pl.BlockSpec(memory_space=pltpu.HBM)
 SMEM = pl.BlockSpec(memory_space=pltpu.SMEM)
 
 
@@ -34,32 +32,33 @@
 
 
 def forward_kernel(
-    len_ref, normed, wa, wb, kc, vc, eo, w, q_ref, kn_ref, vn_ref, pc_ref, pn_ref, proj_ref, att_ref, sem_a, sem_b,
+    place, normed_hbm, wa, wb, kc, vc, eo, w, q_ref, kn_ref, vn_ref, pc_ref, pn_ref, proj_ref, att_ref,
+    normed, sem_a, sem_b, sem_n,
 ):
+    len_ref = place
     hd = kc.shape[1]
-    rows = normed.shape[0]
+    rows, width = normed.shape
     nx, ny, shard, _ = wb.shape
-    half = nx * ny * shard
-    step = chunk_of(half)
+    half = width // 2
+    zh = place[2]
     take_a = [
-        pltpu.make_async_copy(
-            wa.at[p // nx, lax.rem(len_ref[1] - p % nx + nx, nx)], w.at[pl.ds(p * shard, shard), :], sem_a.at[p]
-        )
-        for p in range(nx * ny)
+        pltpu.make_async_copy(wa.at[:, lax.rem(place[1] - j + nx, nx)], w.at[zh, :, j], sem_a.at[j]) for j in range(nx)
     ]
-    take_b = [
-        pltpu.make_async_copy(wb.at[p % nx, p // nx], w.at[pl.ds(half + p * shard, shard), :], sem_b.at[p])
-        for p in range(nx * ny)
-    ]
+    take_b = [pltpu.make_async_copy(wb.at[j], w.at[1 - zh, :, j], sem_b.at[j]) for j in range(nx)]
+    take_n = pltpu.make_async_copy(normed_hbm, normed, sem_n)
+    take_n.start()
     for copy in take_a + take_b:
         copy.start()
+    take_n.wait()
     acc = jnp.zeros((rows, 3 * hd), f32)
-    for h in range(2):
-        for c in range(0, half, step):
-            for p in range(c // shard, (c + step) // shard):
-                (take_a, take_b)[h][p].wait()
-            at = h * half + c
-            acc = acc + dot(normed[:, at : at + step], w[at : at + step, : 3 * hd])
+    deep = max(1, ny // 4)
+    step = deep * nx * shard
+    for h, copies in ((zh, take_a), (1 - zh, take_b)):
+        for copy in copies:
+            copy.wait()
+        for c in range(0, ny, deep):
+            cols = pl.ds(pl.multiple_of(h * half + c * nx * shard, 128), step)
+            acc = acc + dot(normed[:, cols], w[h, c : c + deep, :, :, : 3 * hd].reshape(step, 3 * hd))
     proj_ref[...] = acc
     low = acc.astype(bf16)
     q = low[:, :hd]
@@ -146,16 +145,18 @@
 
 
 def flip(block, out):
-    planes, shard, _ = out.shape
-    half = planes * shard
+    planes = out.shape[0]
+    half = block.shape[1] // 2
+    shard = half // planes
     pair = jnp.concatenate([block[:, :half], block[:, half:]], axis=0)
     turned = jnp.transpose(pair.astype(f32)).astype(bf16)
     for p in range(planes):
-        out[p] = turned[p * shard : (p + 1) * shard, :]
-
-
-def turn_early_half(gin, out):
+        out[p, :shard, :] = turned[p * shard : (p + 1) * shard, :]
+
+
+def turn_early_half(gin, packed, out):
     tokens = gin.shape[0]
+    out[:, out.shape[1] - packed.shape[1] :, :] = packed[...]
     flip(gin[tokens // 2 :, :], out)
 
 
@@ -166,19 +167,39 @@
     flip(jnp.concatenate([first, gin[rows : tokens // 2, :]], axis=0), out)
 
 
-def contract_kernel(start, got, att, sofar, out):
-    planes, _, tokens = got.shape
-    tokens = tokens // 2
-    hd = att.shape[2]
+def spread(a, times):
+    none = jnp.zeros_like(a)
+    return [jnp.concatenate([none] * i + [a] + [none] * (times - 1 - i), axis=1) for i in range(times)]
+
+
+def contract_early_half(got, att, out):
+    planes, _, lanes = got.shape
+    shard, two = out.shape
+    hd = two // 2
+    acc = jnp.zeros((shard, two), f32)
+    old = jnp.zeros((shard // 2, 2 * two), f32)
+    for p in range(0, planes, 2):
+        pair = jnp.concatenate([got[p], got[p + 1]], axis=1)
+        rhs = []
+        far = []
+        for b in (p, p + 1):
+            rhs += spread(att[b, lanes // 2 : lanes, :], 2)
+            far += spread(att[b, lanes:, :], 4)
+        acc = acc + dot(pair[:shard], jnp.concatenate(rhs, axis=0))
+        old = old + dot(pair[shard:], jnp.concatenate(far, axis=0))
+    quarters = [old[:, i * hd : (i + 1) * hd] for i in range(4)]
+    out[:, :hd] = acc[:, :hd] + jnp.concatenate(quarters[:2], axis=0)
+    out[:, hd:] = acc[:, hd:] + jnp.concatenate(quarters[2:], axis=0)
+
+
+def contract_late_half(got, att, sofar, out):
+    planes, _, lanes = got.shape
     acc = sofar[...]
-    none = jnp.zeros((tokens, hd), bf16)
     for p in range(0, planes, 2):
-        lhs = jnp.concatenate([got[p], got[p + 1]], axis=1)
         rhs = []
         for b in (p, p + 1):
-            a = att[b, start : start + tokens, :]
-            rhs += [jnp.concatenate([a, none], axis=1), jnp.concatenate([none, a], axis=1)]
-        acc = acc + dot(lhs, jnp.concatenate(rhs, axis=0))
+            rhs += spread(att[b, : lanes // 2, :], 2)
+        acc = acc + dot(jnp.concatenate([got[p], got[p + 1]], axis=1), jnp.concatenate(rhs, axis=0))
     out[...] = acc
 
 
@@ -196,15 +217,15 @@
     erows = early_dy.shape[1]
     swap = [(0, 1), (1, 0)]
 
+    nx = lax.axis_size("x")
+    ny = lax.axis_size("y")
     own = jnp.concatenate([proj_in[0], jnp.transpose(proj_out[0])], axis=1)
     other = lax.ppermute(own, "zh", swap)
-    lower = jnp.where(zh == 0, own, other)
-    upper = jnp.where(zh == 0, other, own)
-    nx = lax.axis_size("x")
-    ny = lax.axis_size("y")
-    along_y = lax.all_to_all(jnp.broadcast_to(upper[None], (ny, *upper.shape)), "y", 0, 0, tiled=True)
-    turns_x = [lower] + [lax.ppermute(lower, "x", [(i, (i + d) % nx) for i in range(nx)]) for d in range(1, nx)]
+    turns_x = [own]
+    for d in range(1, nx):
+        turns_x.append(lax.ppermute(own, "x", [(i, (i + d) % nx) for i in range(nx)]))
     wa = lax.all_gather(jnp.stack(turns_x)[None], "y", axis=0, tiled=True)
+    along_y = lax.all_to_all(jnp.broadcast_to(other[None], (ny, *other.shape)), "y", 0, 0, tiled=True)
     wb = lax.all_to_all(jnp.broadcast_to(along_y[None], (nx, *along_y.shape)), "x", 0, 0, tiled=True)
 
     wide = x.astype(f32)
@@ -220,10 +241,10 @@
     w, q, kn, vn, pc, pn, proj, att = pl.pallas_call(
         forward_kernel,
         name="forward",
-        in_specs=[SMEM, VMEM, ANY, ANY, VMEM, VMEM, VMEM],
+        in_specs=[SMEM, HBM, HBM, HBM, VMEM, VMEM, VMEM],
         out_specs=[VMEM] * 8,
         out_shape=[
-            shape((width, 4 * hd), bf16),
+            shape((2, ny, nx, shard, 4 * hd), bf16),
             shape((tokens, hd), bf16),
             shape((tokens, hd), bf16),
             shape((tokens, hd), bf16),
@@ -233,12 +254,14 @@
             shape((tokens + erows, hd), bf16),
         ],
         scratch_shapes=[
-            pltpu.SemaphoreType.DMA((planes,)),
-            pltpu.SemaphoreType.DMA((planes,)),
+            pltpu.VMEM((tokens, width), bf16),
+            pltpu.SemaphoreType.DMA((nx,)),
+            pltpu.SemaphoreType.DMA((nx,)),
+            pltpu.SemaphoreType.DMA,
         ],
         compiler_params=room,
-    )(jnp.stack([prefix_len[0], lax.axis_index("x")]), normed, wa, wb, kc, vc, early_out[0])
-    w = near(w)
+    )(jnp.stack([prefix_len[0], lax.axis_index("x"), zh]), normed, wa, wb, kc, vc, early_out[0])
+    w = near(w.reshape(width, 4 * hd))
 
     att_all = lax.all_gather(att[None], PLANE, axis=0, tiled=True)
 
@@ -278,9 +301,6 @@
         part, active = place(t)
         flags = jnp.stack([active.astype(jnp.int32), part, is_top.astype(jnp.int32)])
         return stage(flags, recv, top_grad, w, x, gain, inv, q, kc, kn, vc, vn, pc, pn, proj, *state)
-
-    packed, _ = lax.optimization_barrier((packed, att))
-    early_got = lax.all_to_all(packed, PLANE, 0, 0, tiled=True)
 
     recv = jnp.zeros((rows, width), bf16)
     gin_all = jnp.where(is_top, top_grad, jnp.zeros_like(top_grad))
@@ -314,39 +334,32 @@
         send, *state = compute(t, recv, state)
         gx_all = keep(gx_all, send, t, True)
         if t == halfway:
-            gin_now, _, early_got = lax.optimization_barrier((gin_all, send, early_got))
+            gin_now, _ = lax.optimization_barrier((gin_all, send))
             soon = pl.pallas_call(
                 turn_early_half,
                 name="turn_soon",
-                in_specs=[VMEM],
+                in_specs=[VMEM, VMEM],
                 out_specs=VMEM,
-                out_shape=block,
+                out_shape=shape((planes, shard + shard // 2, tokens), bf16),
                 compiler_params=room,
-            )(gin_now)
+            )(gin_now, packed)
             got_soon = lax.all_to_all(soon, PLANE, 0, 0, tiled=True)
         if t < turns - 1:
             recv = lax.ppermute(send, SECTION, down)
     _, _, gsc, go_all = state
     key_out = dot(gsc, q, 0, 0).astype(bf16)
     value_out = dot(pc.astype(bf16), go_all, 0, 0).astype(bf16)
-    early_got, _ = lax.optimization_barrier((early_got, send))
-    early_rows = early_got.reshape(planes, shard // 2, 4, erows)
-    early = jnp.einsum("prqt,pth->qrh", early_rows, att_all[:, tokens:, :], preferred_element_type=f32)
-    early = early.reshape(2, shard, hd)
-    early = jnp.concatenate([early[0], early[1]], axis=1)
-
-    def contract(start, got, sofar):
+
+    def contract(kernel, *operands):
         return pl.pallas_call(
-            functools.partial(contract_kernel, start),
-            name="contract",
-            in_specs=[VMEM] * 3,
+            kernel,
+            in_specs=[VMEM] * len(operands),
             out_specs=VMEM,
             out_shape=shape((shard, 2 * hd), f32),
             compiler_params=room,
-        )(got, att_all, sofar)
-
-    whole = contract(tokens // 2, got_soon, early)
-    whole = contract(0, got_late, whole)
+        )(*operands)
+
+    whole = contract(contract_late_half, got_late, att_all, contract(contract_early_half, got_soon, att_all))
     first, second = whole[:, :hd], whole[:, hd:]
     away = lax.ppermute(jnp.where(zh == 0, second, first), "zh", swap)
     wo = jnp.transpose(jnp.where(zh == 0, first, second) + away)

time: 308 us -> 292 us (0.948)
  the two profiles are of different devices: /device:TPU:1 before, /device:TPU:66 now
where the time goes in v3:
time: 292 us; the launch traced here: 290 us
  waiting for transfers between devices  102 us (35%)
  starting transfers between devices  84.3 us (29%)
  local copies, waits for them, and re-layouts  35.5 us (12%)
  Pallas kernels  30.4 us (10%)
  other arithmetic  20.8 us (7%)
  between operations  15.5 us (5%)
    ppermute x10, waiting for transfers between devices, body(): recv = lax.ppermute(send, SECTION, down)  46.5 us
    ppermute x10, starting transfers between devices, body(): recv = lax.ppermute(send, SECTION, down)  30.3 us
    all_to_all x1, waiting for transfers between devices, body(): lax.all_to_all(jnp.broadcast_to(along_y[None], (nx, *along_y.shape)), 'x'...  24.8 us
    unnamed x115, local copies, waits for them, and re-layouts  24.6 us
    pallas_call x11, Pallas kernels, compute(): stage(flags, recv, top_grad, w, x, gain, inv, q, kc, kn, vc, vn, pc, pn,...  22.3 us
    all_to_all x1, waiting for transfers between devices, body(): lax.all_to_all(jnp.broadcast_to(other[None], (ny, *other.shape)), 'y', 0,...  12.9 us
    ppermute x3, starting transfers between devices, body(): lax.ppermute(own, 'x', [(i, (i + d) % nx) for i in range(nx)])  10.5 us
    ppermute x1, starting transfers between devices, body(): other = lax.ppermute(own, 'zh', swap)  10 us
  transfers between devices with their start and end apart: 21, of which 17 were waited for; matrix products, arithmetic and copies ran while one was open for 12% of the time, Pallas kernels for 8%

profile of v3, /device:TPU:66, one launch (start us, length us, event | category | flops | bytes accessed | tf_op | source)
XLA Modules:
  0.0 289.9 jit_solution(5035639335127580020)
XLA Ops:
  8.1 3.4 %collective-permute-start = (bf16[80,512]{1,0:T(8,128)(2,1)S(1)}, bf16[80,512]{1,0:T(8,128)(2,1)S(1)}, u32[]{:S(2)}, u32[]{:S(2)}) collective-permute-start(bf16[80,512]{1,0:T(8,128)(2,1)S(1)} %get-tuple-element.135), channel_id=1, source_target_pairs={{0,1},{1,2},{2,3},{3,0},{4,5},{5,6},{6,7},{7,4},{8,9},{9,10},{10,1... | collective-permute-start | bytes 245768 | tf_op jit(solution)/shard_map/ppermute | solution.py:226
  11.5 3.0 %collective-permute-start.1 = (bf16[80,512]{1,0:T(8,128)(2,1)S(1)}, bf16[80,512]{1,0:T(8,128)(2,1)S(1)}, u32[]{:S(2)}, u32[]{:S(2)}) collective-permute-start(bf16[80,512]{1,0:T(8,128)(2,1)S(1)} %get-tuple-element.135), channel_id=1, source_target_pairs={{0,2},{1,3},{2,0},{3,1},{4,6},{5,7},{6,4},{7,5},{8,10},{9,11},{10,... | collective-permute-start | bytes 245768 | tf_op jit(solution)/shard_map/ppermute | solution.py:226
  14.5 4.1 %collective-permute-start.2 = (bf16[80,512]{1,0:T(8,128)(2,1)S(1)}, bf16[80,512]{1,0:T(8,128)(2,1)S(1)}, u32[]{:S(2)}, u32[]{:S(2)}) collective-permute-start(bf16[80,512]{1,0:T(8,128)(2,1)S(1)} %get-tuple-element.135), channel_id=1, source_target_pairs={{0,3},{1,0},{2,1},{3,2},{4,7},{5,4},{6,5},{7,6},{8,11},{9,8},{10,9... | collective-permute-start | bytes 245768 | tf_op jit(solution)/shard_map/ppermute | solution.py:226
  21.7 10.0 %collective-permute-start.3 = (bf16[80,512]{1,0:T(8,128)(2,1)S(1)}, bf16[80,512]{1,0:T(8,128)(2,1)S(1)}, u32[]{:S(2)}, u32[]{:S(2)}) collective-permute-start(bf16[80,512]{1,0:T(8,128)(2,1)S(1)} %get-tuple-element.135), channel_id=1, source_target_pairs={{0,32},{32,0},{1,33},{33,1},{2,34},{34,2},{3,35},{35,3},{4,36},{36... | collective-permute-start | bytes 245768 | tf_op jit(solution)/shard_map/ppermute | solution.py:223
  36.0 7.1 %all-to-all-start = ((bf16[8,80,512]{2,1,0:T(8,128)(2,1)}), bf16[8,80,512]{2,1,0:T(8,128)(2,1)}, u32[]{:S(2)}, u32[]{:S(2)}) async-start(bf16[8,80,512]{2,1,0:T(8,128)(2,1)} %broadcast_in_dim.45), calls=%async_computation | async-start | bytes 1310720 | tf_op jit(solution)/shard_map/all_to_all | solution.py:228
  44.5 1.9 reshape_squeeze.3
  46.4 3.4 %copy.105 = bf16[32,2,32,2,40]{0,3,1,4,2:T(2,128)(2,1)S(1)} copy(bf16[32,2,32,2,40]{4,3,2,1,0:T(2,128)(2,1)S(1)} %reshape_squeeze.3) | data formatting | bytes 655360 | tf_op jit(solution)/shard_map/reshape;squeeze | solution.py:236
  57.0 12.9 %all-to-all-done = bf16[8,80,512]{2,1,0:T(8,128)(2,1)} async-done(((bf16[8,80,512]{2,1,0:T(8,128)(2,1)}), bf16[8,80,512]{2,1,0:T(8,128)(2,1)}, u32[]{:S(2)}, u32[]{:S(2)}) %all-to-all-start) | async-done | bytes 655392 | tf_op jit(solution)/shard_map/all_to_all | solution.py:228
  69.9 2.9 %broadcast_in_dim.46 = bf16[4,8,80,512]{3,2,1,0:T(8,128)(2,1)} broadcast(bf16[8,80,512]{2,1,0:T(8,128)(2,1)} %all-to-all-done), dimensions={1,2,3} | broadcast | bytes 3276800 | tf_op jit(solution)/shard_map/broadcast_in_dim | solution.py:229
  72.8 5.8 %all-to-all-start.1 = ((bf16[4,8,80,512]{3,2,1,0:T(8,128)(2,1)}), bf16[4,8,80,512]{3,2,1,0:T(8,128)(2,1)}, u32[]{:S(2)}, u32[]{:S(2)}) async-start(bf16[4,8,80,512]{3,2,1,0:T(8,128)(2,1)} %broadcast_in_dim.46), calls=%async_computation.1 | async-start | bytes 5242880 | tf_op jit(solution)/shard_map/all_to_all | solution.py:229
  81.9 24.8 %all-to-all-done.1.wb = bf16[4,8,80,512]{3,2,1,0:T(8,128)(2,1)} async-done(((bf16[4,8,80,512]{3,2,1,0:T(8,128)(2,1)}), bf16[4,8,80,512]{3,2,1,0:T(8,128)(2,1)}, u32[]{:S(2)}, u32[]{:S(2)}) %all-to-all-start.1) | async-done | bytes 2621472 | tf_op jit(solution)/shard_map/all_to_all | solution.py:229
  109.8 3.8 %forward.1 = (bf16[2,8,4,80,512]{4,3,2,1,0:T(8,128)(2,1)S(1)}, bf16[128,128]{1,0:T(8,128)(2,1)S(1)}, bf16[128,128]{1,0:T(8,128)(2,1)S(1)}, bf16[128,128]{1,0:T(8...) custom-call(s32[3]{0:T(128)S(1)} %pad_add_fusion.place, ...), custom_call_target="tpu_custom_call" | custom-call | tf_op jit(solution)/shard_map/forward/pallas_call | solution.py:241
  113.7 1.9 stage.11
  116.0 1.9 collective-permute-start.4
  118.3 4.6 %collective-permute-done.4.recv = bf16[32,5120]{1,0:T(8,128)(2,1)} collective-permute-done((bf16[32,5120]{1,0:T(8,128)(2,1)}, bf16[32,5120]{1,0:T(8,128)(2,1)}, u32[]{:S(2)}, u32[]{:S(2)}) %collective-permute-start.4) | collective-permute-done | bytes 327712 | tf_op jit(solution)/shard_map/ppermute | solution.py:348
  122.9 2.5 copy-done.1
  126.5 3.8 %collective-permute-start.5 = (bf16[32,5120]{1,0:T(8,128)(2,1)S(1)}, bf16[32,5120]{1,0:T(8,128)(2,1)S(1)}, u32[]{:S(2)}, u32[]{:S(2)}) collective-permute-start(bf16[32,5120]{1,0:T(8,128)(2,1)S(1)} %get-tuple-element.81), channel_id=1, source_target_pairs={{64,0},{128,64},{192,128},{256,192},{320,256},{384,320},{448,384},... | collective-permute-start | bytes 983048 | tf_op jit(solution)/shard_map/ppermute | solution.py:348
  130.6 4.3 %collective-permute-done.5.recv = bf16[32,5120]{1,0:T(8,128)(2,1)S(1)} collective-permute-done((bf16[32,5120]{1,0:T(8,128)(2,1)S(1)}, bf16[32,5120]{1,0:T(8,128)(2,1)S(1)}, u32[]{:S(2)}, u32[]{:S(2)}) %collective-permute-start.5) | collective-permute-done | bytes 327712 | tf_op jit(solution)/shard_map/ppermute | solution.py:348
  135.6 4.2 %collective-permute-start.6 = (bf16[32,5120]{1,0:T(8,128)(2,1)S(1)}, bf16[32,5120]{1,0:T(8,128)(2,1)S(1)}, u32[]{:S(2)}, u32[]{:S(2)}) collective-permute-start(bf16[32,5120]{1,0:T(8,128)(2,1)S(1)} %get-tuple-element.86), channel_id=1, source_target_pairs={{64,0},{128,64},{192,128},{256,192},{320,256},{384,320},{448,384},... | collective-permute-start | bytes 983048 | tf_op jit(solution)/shard_map/ppermute | solution.py:348
  140.0 4.3 %collective-permute-done.6.recv = bf16[32,5120]{1,0:T(8,128)(2,1)S(1)} collective-permute-done((bf16[32,5120]{1,0:T(8,128)(2,1)S(1)}, bf16[32,5120]{1,0:T(8,128)(2,1)S(1)}, u32[]{:S(2)}, u32[]{:S(2)}) %collective-permute-start.6) | collective-permute-done | bytes 327712 | tf_op jit(solution)/shard_map/ppermute | solution.py:348
  145.0 3.8 %collective-permute-start.7 = (bf16[32,5120]{1,0:T(8,128)(2,1)S(1)}, bf16[32,5120]{1,0:T(8,128)(2,1)S(1)}, u32[]{:S(2)}, u32[]{:S(2)}) collective-permute-start(bf16[32,5120]{1,0:T(8,128)(2,1)S(1)} %get-tuple-element.91), channel_id=1, source_target_pairs={{64,0},{128,64},{192,128},{256,192},{320,256},{384,320},{448,384},... | collective-permute-start | bytes 983048 | tf_op jit(solution)/shard_map/ppermute | solution.py:348
  149.0 4.4 %collective-permute-done.7.recv = bf16[32,5120]{1,0:T(8,128)(2,1)S(1)} collective-permute-done((bf16[32,5120]{1,0:T(8,128)(2,1)S(1)}, bf16[32,5120]{1,0:T(8,128)(2,1)S(1)}, u32[]{:S(2)}, u32[]{:S(2)}) %collective-permute-start.7) | collective-permute-done | bytes 327712 | tf_op jit(solution)/shard_map/ppermute | solution.py:348
  154.0 4.2 %collective-permute-start.8 = (bf16[32,5120]{1,0:T(8,128)(2,1)S(1)}, bf16[32,5120]{1,0:T(8,128)(2,1)S(1)}, u32[]{:S(2)}, u32[]{:S(2)}) collective-permute-start(bf16[32,5120]{1,0:T(8,128)(2,1)S(1)} %get-tuple-element.96), channel_id=1, source_target_pairs={{64,0},{128,64},{192,128},{256,192},{320,256},{384,320},{448,384},... | collective-permute-start | bytes 983048 | tf_op jit(solution)/shard_map/ppermute | solution.py:348
  158.4 5.1 %collective-permute-done.8.recv = bf16[32,5120]{1,0:T(8,128)(2,1)S(1)} collective-permute-done((bf16[32,5120]{1,0:T(8,128)(2,1)S(1)}, bf16[32,5120]{1,0:T(8,128)(2,1)S(1)}, u32[]{:S(2)}, u32[]{:S(2)}) %collective-permute-start.8) | collective-permute-done | bytes 327712 | tf_op jit(solution)/shard_map/ppermute | solution.py:348
  163.5 3.8 %stage.16 = (bf16[32,5120]{1,0:T(8,128)(2,1)S(1)}, f32[128,128]{1,0:T(8,128)S(1)}, f32[128,128]{1,0:T(8,128)S(1)}, bf16[128,288]{1,0:T(8,128)(2,1)S(1)}, bf16[128,128]{1,0:T(8,128)(2,1)S(1)}) custom-call(s32[3]{0:T(128)S(1)} %copy-done.50, ...), custom_call_target="tpu_custom_call", output_to_operand_aliasing={{1}: (15, {}), {2}: (16, {}), {3}: (17, {}), {4}: (18, {})} | custom-call | tf_op jit(solution)/shard_map/stage/pallas_call | solution.py:303
  167.3 2.1 collective-permute-start.9
  169.6 6.1 %collective-permute-done.9.recv = bf16[32,5120]{1,0:T(8,128)(2,1)S(1)} collective-permute-done((bf16[32,5120]{1,0:T(8,128)(2,1)S(1)}, bf16[32,5120]{1,0:T(8,128)(2,1)S(1)}, u32[]{:S(2)}, u32[]{:S(2)}) %collective-permute-start.9) | collective-permute-done | bytes 327712 | tf_op jit(solution)/shard_map/ppermute | solution.py:348
  175.7 3.8 %stage.17 = (bf16[32,5120]{1,0:T(8,128)(2,1)S(1)}, f32[128,128]{1,0:T(8,128)S(1)}, f32[128,128]{1,0:T(8,128)S(1)}, bf16[128,288]{1,0:T(8,128)(2,1)S(1)}, bf16[128,128]{1,0:T(8,128)(2,1)S(1)}) custom-call(s32[3]{0:T(128)S(1)} %copy-done.49, ...), custom_call_target="tpu_custom_call", output_to_operand_aliasing={{1}: (15, {}), {2}: (16, {}), {3}: (17, {}), {4}: (18, {})} | custom-call | tf_op jit(solution)/shard_map/stage/pallas_call | solution.py:303
  179.5 1.9 collective-permute-start.10
  181.6 6.6 %collective-permute-done.10.recv = bf16[32,5120]{1,0:T(8,128)(2,1)S(1)} collective-permute-done((bf16[32,5120]{1,0:T(8,128)(2,1)S(1)}, bf16[32,5120]{1,0:T(8,128)(2,1)S(1)}, u32[]{:S(2)}, u32[]{:S(2)}) %collective-permute-start.10) | collective-permute-done | bytes 327712 | tf_op jit(solution)/shard_map/ppermute | solution.py:348
  188.3 3.8 %stage.18 = (bf16[32,5120]{1,0:T(8,128)(2,1)S(1)}, f32[128,128]{1,0:T(8,128)S(1)}, f32[128,128]{1,0:T(8,128)S(1)}, bf16[128,288]{1,0:T(8,128)(2,1)S(1)}, bf16[128,128]{1,0:T(8,128)(2,1)S(1)}) custom-call(s32[3]{0:T(128)S(1)} %copy-done.48, ...), custom_call_target="tpu_custom_call", output_to_operand_aliasing={{1}: (15, {}), {2}: (16, {}), {3}: (17, {}), {4}: (18, {})} | custom-call | tf_op jit(solution)/shard_map/stage/pallas_call | solution.py:303
  192.0 1.9 collective-permute-start.11
  194.2 6.6 %collective-permute-done.11.recv = bf16[32,5120]{1,0:T(8,128)(2,1)S(1)} collective-permute-done((bf16[32,5120]{1,0:T(8,128)(2,1)S(1)}, bf16[32,5120]{1,0:T(8,128)(2,1)S(1)}, u32[]{:S(2)}, u32[]{:S(2)}) %collective-permute-start.11) | collective-permute-done | bytes 327712 | tf_op jit(solution)/shard_map/ppermute | solution.py:348
  200.8 4.5 %stage.19 = (bf16[32,5120]{1,0:T(8,128)(2,1)}, f32[128,128]{1,0:T(8,128)S(1)}, f32[128,128]{1,0:T(8,128)S(1)}, bf16[128,288]{1,0:T(8,128)(2,1)S(1)}, bf16[128,128]{1,0:T(8,128)(2,1)S(1)}) custom-call(s32[3]{0:T(128)S(1)} %copy-done.47, ...), custom_call_target="tpu_custom_call", output_to_operand_aliasing={{1}: (15, {}), {2}: (16, {}), {3}: (17, {}), {4}: (18, {})} | custom-call | tf_op jit(solution)/shard_map/stage/pallas_call | solution.py:303
  205.3 1.9 collective-permute-start.12
  209.6 6.1 %all-to-all-start.2 = ((bf16[32,120,128]{2,1,0:T(8,128)(2,1)}), bf16[32,120,128]{2,1,0:T(8,128)(2,1)}, u32[]{:S(2)}, u32[]{:S(2)}) async-start(bf16[32,120,128]{2,1,0:T(8,128)(2,1)} %copy-done.27), calls=%async_computation.2 | async-start | bytes 1966080 | tf_op jit(solution)/shard_map/all_to_all | solution.py:346
  215.7 1.9 select_dynamic-update-slice_fusion.10
  217.7 2.5 copy-done.2
  225.0 4.5 %collective-permute-start.13 = (bf16[32,5120]{1,0:T(8,128)(2,1)S(1)}, bf16[32,5120]{1,0:T(8,128)(2,1)S(1)}, u32[]{:S(2)}, u32[]{:S(2)}) collective-permute-start(bf16[32,5120]{1,0:T(8,128)(2,1)S(1)} %get-tuple-element.121), channel_id=1, source_target_pairs={{64,0},{128,64},{192,128},{256,192},{320,256},{384,320},{448,384},... | collective-permute-start | bytes 983048 | tf_op jit(solution)/shard_map/ppermute | solution.py:348
  229.6 4.4 %collective-permute-done.13.recv = bf16[32,5120]{1,0:T(8,128)(2,1)S(1)} collective-permute-done((bf16[32,5120]{1,0:T(8,128)(2,1)S(1)}, bf16[32,5120]{1,0:T(8,128)(2,1)S(1)}, u32[]{:S(2)}, u32[]{:S(2)}) %collective-permute-start.13) | collective-permute-done | bytes 327712 | tf_op jit(solution)/shard_map/ppermute | solution.py:348
  235.9 6.6 %all-to-all-done.2.got = bf16[32,120,128]{2,1,0:T(8,128)(2,1)} async-done(((bf16[32,120,128]{2,1,0:T(8,128)(2,1)}), bf16[32,120,128]{2,1,0:T(8,128)(2,1)}, u32[]{:S(2)}, u32[]{:S(2)}) %all-to-all-start.2) | async-done | bytes 983072 | tf_op jit(solution)/shard_map/all_to_all | solution.py:346
  242.5 6.0 %all-to-all-start.3 = ((bf16[32,80,128]{2,1,0:T(8,128)(2,1)}), bf16[32,80,128]{2,1,0:T(8,128)(2,1)}, u32[]{:S(2)}, u32[]{:S(2)}) async-start(bf16[32,80,128]{2,1,0:T(8,128)(2,1)} %copy-done.33), calls=%async_computation.3 | async-start | bytes 1310720 | tf_op jit(solution)/shard_map/all_to_all | solution.py:331
  248.6 1.8 select_dynamic-update-slice_fusion.9
  250.4 2.5 copy.170
  254.2 2.2 shard_map.129.sofar
  257.1 2.5 copy-done.3
  262.8 6.3 %all-to-all-done.3.got = bf16[32,80,128]{2,1,0:T(8,128)(2,1)} async-done(((bf16[32,80,128]{2,1,0:T(8,128)(2,1)}), bf16[32,80,128]{2,1,0:T(8,128)(2,1)}, u32[]{:S(2)}, u32[]{:S(2)}) %all-to-all-start.3) | async-done | bytes 655392 | tf_op jit(solution)/shard_map/all_to_all | solution.py:331
  272.1 8.3 %collective-permute-start.14 = (f32[80,128]{1,0:T(8,128)S(1)}, f32[80,128]{1,0:T(8,128)S(1)}, u32[]{:S(2)}, u32[]{:S(2)}) collective-permute-start(f32[80,128]{1,0:T(8,128)S(1)} %slice_select_fusion), channel_id=1, source_target_pairs={{0,32},{32,0},{1,33},{33,1},{2,34},{34,2},{3,35},{35,3},{4,36},{36... | collective-permute-start | bytes 122888 | tf_op jit(solution)/shard_map/ppermute | solution.py:364
  (181 shorter events, 47.4 us)
Async XLA Ops:
  7.2 99.6 %all-gather.5.cloned.1.call-start = ((), (), s32[]{:S(2)}) async-start(), calls=%async_computation.4 | async-start | bytes 2949120 | tf_op jit(solution)/shard_map/all_gather | solution.py:227
  8.1 10.5 %collective-permute-start = (bf16[80,512]{1,0:T(8,128)(2,1)S(1)}, bf16[80,512]{1,0:T(8,128)(2,1)S(1)}, u32[]{:S(2)}, u32[]{:S(2)}) collective-permute-start(bf16[80,512]{1,0:T(8,128)(2,1)S(1)} %get-tuple-element.135), channel_id=1, source_target_pairs={{0,1},{1,2},{2,3},{3,0},{4,5},{5,6},{6,7},{7,4},{8,9},{9,10},{10,1... | collective-permute-start | bytes 245768 | tf_op jit(solution)/shard_map/ppermute | solution.py:226
  11.5 8.2 %collective-permute-start.1 = (bf16[80,512]{1,0:T(8,128)(2,1)S(1)}, bf16[80,512]{1,0:T(8,128)(2,1)S(1)}, u32[]{:S(2)}, u32[]{:S(2)}) collective-permute-start(bf16[80,512]{1,0:T(8,128)(2,1)S(1)} %get-tuple-element.135), channel_id=1, source_target_pairs={{0,2},{1,3},{2,0},{3,1},{4,6},{5,7},{6,4},{7,5},{8,10},{9,11},{10,... | collective-permute-start | bytes 245768 | tf_op jit(solution)/shard_map/ppermute | solution.py:226
  14.5 6.4 %collective-permute-start.2 = (bf16[80,512]{1,0:T(8,128)(2,1)S(1)}, bf16[80,512]{1,0:T(8,128)(2,1)S(1)}, u32[]{:S(2)}, u32[]{:S(2)}) collective-permute-start(bf16[80,512]{1,0:T(8,128)(2,1)S(1)} %get-tuple-element.135), channel_id=1, source_target_pairs={{0,3},{1,0},{2,1},{3,2},{4,7},{5,4},{6,5},{7,6},{8,11},{9,8},{10,9... | collective-permute-start | bytes 245768 | tf_op jit(solution)/shard_map/ppermute | solution.py:226
  21.7 13.4 %collective-permute-start.3 = (bf16[80,512]{1,0:T(8,128)(2,1)S(1)}, bf16[80,512]{1,0:T(8,128)(2,1)S(1)}, u32[]{:S(2)}, u32[]{:S(2)}) collective-permute-start(bf16[80,512]{1,0:T(8,128)(2,1)S(1)} %get-tuple-element.135), channel_id=1, source_target_pairs={{0,32},{32,0},{1,33},{33,1},{2,34},{34,2},{3,35},{35,3},{4,36},{36... | collective-permute-start | bytes 245768 | tf_op jit(solution)/shard_map/ppermute | solution.py:223
  33.4 10.3 %copy-start.56 = (bf16[1,5120]{1,0:T(2,128)(2,1)S(1)}, bf16[1,5120]{1,0:T(2,128)(2,1)}, u32[]{:S(2)}) copy-start(bf16[1,5120]{1,0:T(2,128)(2,1)} %param.12) | copy-start | bytes 30724
  33.4 11.1 %copy-start.55 = (bf16[1,32,5120]{2,1,0:T(8,128)(2,1)S(1)}, bf16[1,32,5120]{2,1,0:T(8,128)(2,1)}, u32[]{:S(2)}) copy-start(bf16[1,32,5120]{2,1,0:T(8,128)(2,1)} %param.19) | copy-start | bytes 983044
  36.0 33.9 %all-to-all-start = ((bf16[8,80,512]{2,1,0:T(8,128)(2,1)}), bf16[8,80,512]{2,1,0:T(8,128)(2,1)}, u32[]{:S(2)}, u32[]{:S(2)}) async-start(bf16[8,80,512]{2,1,0:T(8,128)(2,1)} %broadcast_in_dim.45), calls=%async_computation | async-start | bytes 1310720 | tf_op jit(solution)/shard_map/all_to_all | solution.py:228
  43.7 36.1 %copy-start.28 = (f32[1,5120]{1,0:T(1,128)}, f32[1,5120]{1,0:T(1,128)S(1)}, u32[]{:S(2)}) copy-start(f32[1,5120]{1,0:T(1,128)S(1)} %convert_element_type.13.gain) | copy-start | bytes 61444
  72.8 5.8 %copy-start.5 = (bf16[128,5120]{1,0:T(8,128)(2,1)S(1)}, bf16[128,5120]{1,0:T(8,128)(2,1)}, u32[]{:S(2)}) copy-start(bf16[128,5120]{1,0:T(8,128)(2,1)} %top.21) | copy-start | bytes 3932164
  72.8 33.9 %all-to-all-start.1 = ((bf16[4,8,80,512]{3,2,1,0:T(8,128)(2,1)}), bf16[4,8,80,512]{3,2,1,0:T(8,128)(2,1)}, u32[]{:S(2)}, u32[]{:S(2)}) async-start(bf16[4,8,80,512]{3,2,1,0:T(8,128)(2,1)} %broadcast_in_dim.46), calls=%async_computation.1 | async-start | bytes 5242880 | tf_op jit(solution)/shard_map/all_to_all | solution.py:229
  78.7 174.2 %all-gather.7.cloned.1.call-start = ((), (), s32[]{:S(2)}) async-start(), calls=%async_computation.5 | async-start | bytes 1351680 | tf_op jit(solution)/shard_map/all_gather | solution.py:266
  80.4 26.3 %copy-start.9 = (bf16[1,288,128]{2,1,0:T(8,128)(2,1)S(1)}, bf16[1,288,128]{2,1,0:T(8,128)(2,1)}, u32[]{:S(2)}) copy-start(bf16[1,288,128]{2,1,0:T(8,128)(2,1)} %param.15) | copy-start | bytes 221188
  80.4 26.3 %copy-start.10 = (bf16[1,288,128]{2,1,0:T(8,128)(2,1)S(1)}, bf16[1,288,128]{2,1,0:T(8,128)(2,1)}, u32[]{:S(2)}) copy-start(bf16[1,288,128]{2,1,0:T(8,128)(2,1)} %param.16) | copy-start | bytes 221188
  80.4 26.3 %copy-start.42 = (bf16[1,32,128]{2,1,0:T(8,128)(2,1)S(1)}, bf16[1,32,128]{2,1,0:T(8,128)(2,1)}, u32[]{:S(2)}) copy-start(bf16[1,32,128]{2,1,0:T(8,128)(2,1)} %param.18) | copy-start | bytes 24580
  116.0 6.8 %collective-permute-start.4 = (bf16[32,5120]{1,0:T(8,128)(2,1)}, bf16[32,5120]{1,0:T(8,128)(2,1)}, u32[]{:S(2)}, u32[]{:S(2)}) collective-permute-start(bf16[32,5120]{1,0:T(8,128)(2,1)} %get-tuple-element.76), channel_id=1, source_target_pairs={{64,0},{128,64},{192,128},{256,192},{320,256},{384,320},{448,384},... | collective-permute-start | bytes 983048 | tf_op jit(solution)/shard_map/ppermute | solution.py:348
  118.0 4.9 %copy-start.15 = (bf16[128,128]{1,0:T(8,128)(2,1)S(1)}, bf16[128,128]{1,0:T(8,128)(2,1)}, u32[]{:S(2)}) copy-start(bf16[128,128]{1,0:T(8,128)(2,1)} %copy-done.14) | copy-start | bytes 98308
  118.0 4.9 %copy-start.20 = (bf16[128,128]{1,0:T(8,128)(2,1)S(1)}, bf16[128,128]{1,0:T(8,128)(2,1)}, u32[]{:S(2)}) copy-start(bf16[128,128]{1,0:T(8,128)(2,1)} %copy-done.19) | copy-start | bytes 98308
  118.0 4.8 %copy-start.24 = (bf16[128,128]{1,0:T(8,128)(2,1)S(1)}, bf16[128,128]{1,0:T(8,128)(2,1)}, u32[]{:S(2)}) copy-start(bf16[128,128]{1,0:T(8,128)(2,1)} %copy-done.23) | copy-start | bytes 98308
  118.0 4.8 %copy-start.30 = (f32[1,5120]{1,0:T(1,128)S(1)}, f32[1,5120]{1,0:T(1,128)}, u32[]{:S(2)}) copy-start(f32[1,5120]{1,0:T(1,128)} %copy-done.28) | copy-start | bytes 61444
  118.0 4.8 %copy-start.44 = (s32[3]{0:T(128)S(1)}, s32[3]{0:T(128)}, u32[]{:S(2)}) copy-start(s32[3]{0:T(128)} %add_add_fusion.1.flags) | copy-start | bytes 40
  125.4 5.1 %copy-start.6 = (bf16[128,5120]{1,0:T(8,128)(2,1)S(1)}, bf16[128,5120]{1,0:T(8,128)(2,1)}, u32[]{:S(2)}) copy-start(bf16[128,5120]{1,0:T(8,128)(2,1)} %broadcast_select_fusion) | copy-start | bytes 3932164
  126.5 8.4 %copy-start.53 = (s32[3]{0:T(128)S(1)}, s32[3]{0:T(128)}, u32[]{:S(2)}) copy-start(s32[3]{0:T(128)} %add_add_fusion.2.flags) | copy-start | bytes 40
  126.5 8.4 %collective-permute-start.5 = (bf16[32,5120]{1,0:T(8,128)(2,1)S(1)}, bf16[32,5120]{1,0:T(8,128)(2,1)S(1)}, u32[]{:S(2)}, u32[]{:S(2)}) collective-permute-start(bf16[32,5120]{1,0:T(8,128)(2,1)S(1)} %get-tuple-element.81), channel_id=1, source_target_pairs={{64,0},{128,64},{192,128},{256,192},{320,256},{384,320},{448,384},... | collective-permute-start | bytes 983048 | tf_op jit(solution)/shard_map/ppermute | solution.py:348
  135.5 8.8 %copy-start.52 = (s32[3]{0:T(128)S(1)}, s32[3]{0:T(128)}, u32[]{:S(2)}) copy-start(s32[3]{0:T(128)} %add_add_fusion.3.flags) | copy-start | bytes 40
  135.6 8.8 %collective-permute-start.6 = (bf16[32,5120]{1,0:T(8,128)(2,1)S(1)}, bf16[32,5120]{1,0:T(8,128)(2,1)S(1)}, u32[]{:S(2)}, u32[]{:S(2)}) collective-permute-start(bf16[32,5120]{1,0:T(8,128)(2,1)S(1)} %get-tuple-element.86), channel_id=1, source_target_pairs={{64,0},{128,64},{192,128},{256,192},{320,256},{384,320},{448,384},... | collective-permute-start | bytes 983048 | tf_op jit(solution)/shard_map/ppermute | solution.py:348
  145.0 8.4 %copy-start.51 = (s32[3]{0:T(128)S(1)}, s32[3]{0:T(128)}, u32[]{:S(2)}) copy-start(s32[3]{0:T(128)} %add_add_fusion.4.flags) | copy-start | bytes 40
  145.0 8.4 %collective-permute-start.7 = (bf16[32,5120]{1,0:T(8,128)(2,1)S(1)}, bf16[32,5120]{1,0:T(8,128)(2,1)S(1)}, u32[]{:S(2)}, u32[]{:S(2)}) collective-permute-start(bf16[32,5120]{1,0:T(8,128)(2,1)S(1)} %get-tuple-element.91), channel_id=1, source_target_pairs={{64,0},{128,64},{192,128},{256,192},{320,256},{384,320},{448,384},... | collective-permute-start | bytes 983048 | tf_op jit(solution)/shard_map/ppermute | solution.py:348
  154.0 9.6 %copy-start.50 = (s32[3]{0:T(128)S(1)}, s32[3]{0:T(128)}, u32[]{:S(2)}) copy-start(s32[3]{0:T(128)} %add_add_fusion.5.flags) | copy-start | bytes 40
  154.0 9.6 %collective-permute-start.8 = (bf16[32,5120]{1,0:T(8,128)(2,1)S(1)}, bf16[32,5120]{1,0:T(8,128)(2,1)S(1)}, u32[]{:S(2)}, u32[]{:S(2)}) collective-permute-start(bf16[32,5120]{1,0:T(8,128)(2,1)S(1)} %get-tuple-element.96), channel_id=1, source_target_pairs={{64,0},{128,64},{192,128},{256,192},{320,256},{384,320},{448,384},... | collective-permute-start | bytes 983048 | tf_op jit(solution)/shard_map/ppermute | solution.py:348
  167.3 8.4 %copy-start.49 = (s32[3]{0:T(128)S(1)}, s32[3]{0:T(128)}, u32[]{:S(2)}) copy-start(s32[3]{0:T(128)} %add_add_fusion.6.flags) | copy-start | bytes 40
  167.3 8.4 %collective-permute-start.9 = (bf16[32,5120]{1,0:T(8,128)(2,1)S(1)}, bf16[32,5120]{1,0:T(8,128)(2,1)S(1)}, u32[]{:S(2)}, u32[]{:S(2)}) collective-permute-start(bf16[32,5120]{1,0:T(8,128)(2,1)S(1)} %get-tuple-element.101), channel_id=1, source_target_pairs={{64,0},{128,64},{192,128},{256,192},{320,256},{384,320},{448,384},... | collective-permute-start | bytes 983048 | tf_op jit(solution)/shard_map/ppermute | solution.py:348
  179.4 8.8 %copy-start.48 = (s32[3]{0:T(128)S(1)}, s32[3]{0:T(128)}, u32[]{:S(2)}) copy-start(s32[3]{0:T(128)} %add_add_fusion.7.flags) | copy-start | bytes 40
  179.5 8.8 %collective-permute-start.10 = (bf16[32,5120]{1,0:T(8,128)(2,1)S(1)}, bf16[32,5120]{1,0:T(8,128)(2,1)S(1)}, u32[]{:S(2)}, u32[]{:S(2)}) collective-permute-start(bf16[32,5120]{1,0:T(8,128)(2,1)S(1)} %get-tuple-element.106), channel_id=1, source_target_pairs={{64,0},{128,64},{192,128},{256,192},{320,256},{384,320},{448,384},... | collective-permute-start | bytes 983048 | tf_op jit(solution)/shard_map/ppermute | solution.py:348
  192.0 8.8 %copy-start.47 = (s32[3]{0:T(128)S(1)}, s32[3]{0:T(128)}, u32[]{:S(2)}) copy-start(s32[3]{0:T(128)} %add_add_fusion.8.flags) | copy-start | bytes 40
  192.0 8.8 %collective-permute-start.11 = (bf16[32,5120]{1,0:T(8,128)(2,1)S(1)}, bf16[32,5120]{1,0:T(8,128)(2,1)S(1)}, u32[]{:S(2)}, u32[]{:S(2)}) collective-permute-start(bf16[32,5120]{1,0:T(8,128)(2,1)S(1)} %get-tuple-element.111), channel_id=1, source_target_pairs={{64,0},{128,64},{192,128},{256,192},{320,256},{384,320},{448,384},... | collective-permute-start | bytes 983048 | tf_op jit(solution)/shard_map/ppermute | solution.py:348
  194.1 11.2 %copy-start.54 = (bf16[128,5120]{1,0:T(8,128)(2,1)}, bf16[128,5120]{1,0:T(8,128)(2,1)S(1)}, u32[]{:S(2)}) copy-start(bf16[128,5120]{1,0:T(8,128)(2,1)S(1)} %select_dynamic-update-slice_fusion.11) | copy-start | bytes 3932164
  200.8 6.5 %copy-start.37 = (bf16[32,40,128]{2,1,0:T(8,128)(2,1)S(1)}, bf16[32,40,128]{2,1,0:T(8,128)(2,1)}, u32[]{:S(2)}) copy-start(bf16[32,40,128]{2,1,0:T(8,128)(2,1)} %reshape.40.packed) | copy-start | bytes 983044
  205.3 12.4 %collective-permute-start.12 = (bf16[32,5120]{1,0:T(8,128)(2,1)}, bf16[32,5120]{1,0:T(8,128)(2,1)}, u32[]{:S(2)}, u32[]{:S(2)}) collective-permute-start(bf16[32,5120]{1,0:T(8,128)(2,1)} %get-tuple-element.116), channel_id=1, source_target_pairs={{64,0},{128,64},{192,128},{256,192},{320,256},{384,320},{448,384},... | collective-permute-start | bytes 983048 | tf_op jit(solution)/shard_map/ppermute | solution.py:348
  209.6 32.9 %all-to-all-start.2 = ((bf16[32,120,128]{2,1,0:T(8,128)(2,1)}), bf16[32,120,128]{2,1,0:T(8,128)(2,1)}, u32[]{:S(2)}, u32[]{:S(2)}) async-start(bf16[32,120,128]{2,1,0:T(8,128)(2,1)} %copy-done.27), calls=%async_computation.2 | async-start | bytes 1966080 | tf_op jit(solution)/shard_map/all_to_all | solution.py:346
  223.8 5.7 %copy-start.8 = (bf16[128,5120]{1,0:T(8,128)(2,1)S(1)}, bf16[128,5120]{1,0:T(8,128)(2,1)}, u32[]{:S(2)}) copy-start(bf16[128,5120]{1,0:T(8,128)(2,1)} %copy-done.7) | copy-start | bytes 3932164
  225.0 9.1 %copy-start.40 = (bf16[32,5120]{1,0:T(8,128)(2,1)}, bf16[32,5120]{1,0:T(8,128)(2,1)S(1)}, u32[]{:S(2)}) copy-start(bf16[32,5120]{1,0:T(8,128)(2,1)S(1)} %get-tuple-element.121) | copy-start | bytes 983044
  225.0 9.1 %collective-permute-start.13 = (bf16[32,5120]{1,0:T(8,128)(2,1)S(1)}, bf16[32,5120]{1,0:T(8,128)(2,1)S(1)}, u32[]{:S(2)}, u32[]{:S(2)}) collective-permute-start(bf16[32,5120]{1,0:T(8,128)(2,1)S(1)} %get-tuple-element.121), channel_id=1, source_target_pairs={{64,0},{128,64},{192,128},{256,192},{320,256},{384,320},{448,384},... | collective-permute-start | bytes 983048 | tf_op jit(solution)/shard_map/ppermute | solution.py:348
  242.5 26.7 %all-to-all-start.3 = ((bf16[32,80,128]{2,1,0:T(8,128)(2,1)}), bf16[32,80,128]{2,1,0:T(8,128)(2,1)}, u32[]{:S(2)}, u32[]{:S(2)}) async-start(bf16[32,80,128]{2,1,0:T(8,128)(2,1)} %copy-done.33), calls=%async_computation.3 | async-start | bytes 1310720 | tf_op jit(solution)/shard_map/all_to_all | solution.py:331
  252.8 4.2 %copy-start.43 = (s32[3]{0:T(128)S(1)}, s32[3]{0:T(128)}, u32[]{:S(2)}) copy-start(s32[3]{0:T(128)} %add_add_fusion.10.flags) | copy-start | bytes 40
  260.2 9.0 %copy-start.39 = (f32[80,256]{1,0:T(8,128)S(1)}, f32[80,256]{1,0:T(8,128)}, u32[]{:S(2)}) copy-start(f32[80,256]{1,0:T(8,128)} %copy-done.38) | copy-start | bytes 245764
  270.5 9.9 %copy-start.18 = (bf16[128,128]{1,0:T(8,128)(2,1)S(1)}, bf16[128,128]{1,0:T(8,128)(2,1)}, u32[]{:S(2)}) copy-start(bf16[128,128]{1,0:T(8,128)(2,1)} %copy-done.14) | copy-start | bytes 98308
  272.1 10.3 %collective-permute-start.14 = (f32[80,128]{1,0:T(8,128)S(1)}, f32[80,128]{1,0:T(8,128)S(1)}, u32[]{:S(2)}, u32[]{:S(2)}) collective-permute-start(f32[80,128]{1,0:T(8,128)S(1)} %slice_select_fusion), channel_id=1, source_target_pairs={{0,32},{32,0},{1,33},{33,1},{2,34},{34,2},{3,35},{35,3},{4,36},{36... | collective-permute-start | bytes 122888 | tf_op jit(solution)/shard_map/ppermute | solution.py:364
  (30 other events, 57.4 us)
Sparse Core Ops, SparseCore 0:
  21.8 62.9 all-gather.4
  118.1 78.2 all-gather.6

commit v4 on v3

--- a/solution.py
+++ b/solution.py
@@ -25,6 +25,10 @@
 
 def near(a):
     return pltpu.with_memory_space_constraint(a, pltpu.VMEM)
+
+
+def far(a):
+    return pltpu.with_memory_space_constraint(a, pltpu.HBM)
 
 
 def chunk_of(width):
@@ -224,8 +228,9 @@
     turns_x = [own]
     for d in range(1, nx):
         turns_x.append(lax.ppermute(own, "x", [(i, (i + d) % nx) for i in range(nx)]))
-    wa = lax.all_gather(jnp.stack(turns_x)[None], "y", axis=0, tiled=True)
     along_y = lax.all_to_all(jnp.broadcast_to(other[None], (ny, *other.shape)), "y", 0, 0, tiled=True)
+    mine, along_y, early_dy = lax.optimization_barrier((jnp.stack(turns_x)[None], along_y, early_dy))
+    wa = lax.all_gather(mine, "y", axis=0, tiled=True)
     wb = lax.all_to_all(jnp.broadcast_to(along_y[None], (nx, *along_y.shape)), "x", 0, 0, tiled=True)
 
     wide = x.astype(f32)
@@ -260,7 +265,7 @@
             pltpu.SemaphoreType.DMA,
         ],
         compiler_params=room,
-    )(jnp.stack([prefix_len[0], lax.axis_index("x"), zh]), normed, wa, wb, kc, vc, early_out[0])
+    )(jnp.stack([prefix_len[0], lax.axis_index("x"), zh]), far(normed), far(wa), far(wb), kc, vc, early_out[0])
     w = near(w.reshape(width, 4 * hd))
 
     att_all = lax.all_gather(att[None], PLANE, axis=0, tiled=True)

time: 292 us -> 279 us (0.955)
  waiting for transfers between devices: 102 us -> 90.1 us
    all_to_all x1, waiting for transfers between devices: 24.8 us -> 15 us  [body(): lax.all_to_all(jnp.broadcast_to(along_y[None], (nx, *along_y.shape)), 'x'...]
    all_to_all x1, waiting for transfers between devices: 12.9 us -> 6.13 us  [body(): lax.all_to_all(jnp.broadcast_to(other[None], (ny, *other.shape)), 'y', 0,...]
    ppermute x10, waiting for transfers between devices: 46.5 us -> 49.8 us  [body(): recv = lax.ppermute(send, SECTION, down)]
    unnamed x115 -> x111, local copies, waits for them, and re-layouts: 24.6 us -> 21.6 us
    another operation x2, local copies, waits for them, and re-layouts: 5.31 us -> 8.38 us  [body(): packed = early_dy[0].reshape(erows, 2, planes, 2, shard // 2)]
    dynamic_update_slice x19 -> x20, other arithmetic: 7.29 us -> 7.25 us  [keep(): lax.dynamic_update_slice_in_dim(whole, jnp.where(jnp.logical_and(active,...]
  transfers between devices with their start and end apart: 21 -> 21, of which waited for: 17 -> 17; matrix products, arithmetic and copies ran while one was open for 12% -> 13% of each run, Pallas kernels for 8% -> 8%
where the time goes in v4:
time: 279 us; the launch traced here: 277 us
  waiting for transfers between devices  90.1 us (32%)
  starting transfers between devices  82.5 us (30%)
  local copies, waits for them, and re-layouts  37 us (13%)
  Pallas kernels  31.7 us (11%)
  other arithmetic  19 us (7%)
  between operations  15.5 us (6%)
    ppermute x10, waiting for transfers between devices, body(): recv = lax.ppermute(send, SECTION, down)  49.8 us
    ppermute x10, starting transfers between devices, body(): recv = lax.ppermute(send, SECTION, down)  30.3 us
    pallas_call x11, Pallas kernels, compute(): stage(flags, recv, top_grad, w, x, gain, inv, q, kc, kn, vc, vn, pc, pn,...  22.5 us
    unnamed x111, local copies, waits for them, and re-layouts  21.6 us
    all_to_all x1, waiting for transfers between devices, body(): lax.all_to_all(jnp.broadcast_to(along_y[None], (nx, *along_y.shape)), 'x'...  15 us
    ppermute x3, starting transfers between devices, body(): lax.ppermute(own, 'x', [(i, (i + d) % nx) for i in range(nx)])  10.5 us
    ppermute x1, starting transfers between devices, body(): other = lax.ppermute(own, 'zh', swap)  10 us
    another operation x2, local copies, waits for them, and re-layouts, body(): packed = early_dy[0].reshape(erows, 2, planes, 2, shard // 2)  8.38 us
  transfers between devices with their start and end apart: 21, of which 17 were waited for; matrix products, arithmetic and copies ran while one was open for 13% of the time, Pallas kernels for 8%

profile of v4, /device:TPU:66, one launch (start us, length us, event | category | flops | bytes accessed | tf_op | source)
XLA Modules:
  0.0 277.4 jit_solution(1380384494302757361)
XLA Ops:
  8.0 10.0 %collective-permute-start.3 = (bf16[80,512]{1,0:T(8,128)(2,1)S(1)}, bf16[80,512]{1,0:T(8,128)(2,1)S(1)}, u32[]{:S(2)}, u32[]{:S(2)}) collective-permute-start(bf16[80,512]{1,0:T(8,128)(2,1)S(1)} %get-tuple-element.141), channel_id=1, source_target_pairs={{0,32},{32,0},{1,33},{33,1},{2,34},{34,2},{3,35},{35,3},{4,36},{36... | collective-permute-start | bytes 245768 | tf_op jit(solution)/shard_map/ppermute | solution.py:227
  18.1 2.4 collective-permute-done.3
  21.4 7.2 %all-to-all-start = ((bf16[8,80,512]{2,1,0:T(8,128)(2,1)}), bf16[8,80,512]{2,1,0:T(8,128)(2,1)S(1)}, u32[]{:S(2)}, u32[]{:S(2)}) async-start(bf16[8,80,512]{2,1,0:T(8,128)(2,1)} %broadcast_in_dim.45), calls=%async_computation | async-start | bytes 1310720 | tf_op jit(solution)/shard_map/all_to_all | solution.py:231
  28.7 3.4 %collective-permute-start = (bf16[80,512]{1,0:T(8,128)(2,1)S(1)}, bf16[80,512]{1,0:T(8,128)(2,1)S(1)}, u32[]{:S(2)}, u32[]{:S(2)}) collective-permute-start(bf16[80,512]{1,0:T(8,128)(2,1)S(1)} %get-tuple-element.141), channel_id=1, source_target_pairs={{0,1},{1,2},{2,3},{3,0},{4,5},{5,6},{6,7},{7,4},{8,9},{9,10},{10,1... | collective-permute-start | bytes 245768 | tf_op jit(solution)/shard_map/ppermute | solution.py:230
  32.1 3.0 %collective-permute-start.1 = (bf16[80,512]{1,0:T(8,128)(2,1)S(1)}, bf16[80,512]{1,0:T(8,128)(2,1)S(1)}, u32[]{:S(2)}, u32[]{:S(2)}) collective-permute-start(bf16[80,512]{1,0:T(8,128)(2,1)S(1)} %get-tuple-element.141), channel_id=1, source_target_pairs={{0,2},{1,3},{2,0},{3,1},{4,6},{5,7},{6,4},{7,5},{8,10},{9,11},{10,... | collective-permute-start | bytes 245768 | tf_op jit(solution)/shard_map/ppermute | solution.py:230
  35.1 4.1 %collective-permute-start.2 = (bf16[80,512]{1,0:T(8,128)(2,1)S(1)}, bf16[80,512]{1,0:T(8,128)(2,1)S(1)}, u32[]{:S(2)}, u32[]{:S(2)}) collective-permute-start(bf16[80,512]{1,0:T(8,128)(2,1)S(1)} %get-tuple-element.141), channel_id=1, source_target_pairs={{0,3},{1,0},{2,1},{3,2},{4,7},{5,4},{6,5},{7,6},{8,11},{9,8},{10,9... | collective-permute-start | bytes 245768 | tf_op jit(solution)/shard_map/ppermute | solution.py:230
  42.2 6.1 %all-to-all-done = bf16[8,80,512]{2,1,0:T(8,128)(2,1)S(1)} async-done(((bf16[8,80,512]{2,1,0:T(8,128)(2,1)}), bf16[8,80,512]{2,1,0:T(8,128)(2,1)S(1)}, u32[]{:S(2)}, u32[]{:S(2)}) %all-to-all-start) | async-done | bytes 655392 | tf_op jit(solution)/shard_map/all_to_all | solution.py:231
  58.0 5.2 %all-to-all-start.1 = ((bf16[4,8,80,512]{3,2,1,0:T(8,128)(2,1)}), bf16[4,8,80,512]{3,2,1,0:T(8,128)(2,1)}, u32[]{:S(2)}, u32[]{:S(2)}) async-start(bf16[4,8,80,512]{3,2,1,0:T(8,128)(2,1)} %broadcast_in_dim.46), calls=%async_computation.1 | async-start | bytes 5242880 | tf_op jit(solution)/shard_map/all_to_all | solution.py:234
  65.8 2.9 %reshape_squeeze.3 = bf16[32,2,32,2,40]{4,3,2,1,0:T(2,128)(2,1)} reshape(bf16[1,32,5120]{2,1,0:T(8,128)(2,1)S(1)} %copy-done.53) | data formatting | bytes 655360 | tf_op jit(solution)/shard_map/reshape;squeeze | solution.py:241
  68.7 5.5 %copy.105 = bf16[32,2,32,2,40]{0,3,1,4,2:T(2,128)(2,1)} copy(bf16[32,2,32,2,40]{4,3,2,1,0:T(2,128)(2,1)} %reshape_squeeze.3) | data formatting | bytes 655360 | tf_op jit(solution)/shard_map/reshape;squeeze | solution.py:241
  74.2 4.0 %reshape.40.packed = bf16[32,40,128]{2,1,0:T(8,128)(2,1)} reshape(bf16[32,40,2,2,32]{4,3,2,1,0:T(2,128)(2,1)} %bitcast.114) | data formatting | bytes 655360 | tf_op jit(solution)/shard_map/reshape | solution.py:242
  78.2 15.0 %all-to-all-done.1.wb = bf16[4,8,80,512]{3,2,1,0:T(8,128)(2,1)} async-done(((bf16[4,8,80,512]{3,2,1,0:T(8,128)(2,1)}), bf16[4,8,80,512]{3,2,1,0:T(8,128)(2,1)}, u32[]{:S(2)}, u32[]{:S(2)}) %all-to-all-start.1) | async-done | bytes 2621472 | tf_op jit(solution)/shard_map/all_to_all | solution.py:234
  93.2 5.0 %forward.1 = (bf16[2,8,4,80,512]{4,3,2,1,0:T(8,128)(2,1)S(1)}, bf16[128,128]{1,0:T(8,128)(2,1)S(1)}, bf16[128,128]{1,0:T(8,128)(2,1)S(1)}, bf16[128,128]{1,0:T(8...) custom-call(s32[3]{0:T(128)S(1)} %get-tuple-element.145.place, ...), custom_call_target="tpu_custom_call" | custom-call | tf_op jit(solution)/shard_map/forward/pallas_call | solution.py:246
  101.3 1.9 collective-permute-start.4
  103.5 4.6 %collective-permute-done.4.recv = bf16[32,5120]{1,0:T(8,128)(2,1)} collective-permute-done((bf16[32,5120]{1,0:T(8,128)(2,1)}, bf16[32,5120]{1,0:T(8,128)(2,1)}, u32[]{:S(2)}, u32[]{:S(2)}) %collective-permute-start.4) | collective-permute-done | bytes 327712 | tf_op jit(solution)/shard_map/ppermute | solution.py:353
  108.1 2.5 copy-done.1
  111.8 3.8 %collective-permute-start.5 = (bf16[32,5120]{1,0:T(8,128)(2,1)S(1)}, bf16[32,5120]{1,0:T(8,128)(2,1)S(1)}, u32[]{:S(2)}, u32[]{:S(2)}) collective-permute-start(bf16[32,5120]{1,0:T(8,128)(2,1)S(1)} %get-tuple-element.86), channel_id=1, source_target_pairs={{64,0},{128,64},{192,128},{256,192},{320,256},{384,320},{448,384},... | collective-permute-start | bytes 983048 | tf_op jit(solution)/shard_map/ppermute | solution.py:353
  115.8 4.3 %collective-permute-done.5.recv = bf16[32,5120]{1,0:T(8,128)(2,1)S(1)} collective-permute-done((bf16[32,5120]{1,0:T(8,128)(2,1)S(1)}, bf16[32,5120]{1,0:T(8,128)(2,1)S(1)}, u32[]{:S(2)}, u32[]{:S(2)}) %collective-permute-start.5) | collective-permute-done | bytes 327712 | tf_op jit(solution)/shard_map/ppermute | solution.py:353
  120.8 3.8 %collective-permute-start.6 = (bf16[32,5120]{1,0:T(8,128)(2,1)S(1)}, bf16[32,5120]{1,0:T(8,128)(2,1)S(1)}, u32[]{:S(2)}, u32[]{:S(2)}) collective-permute-start(bf16[32,5120]{1,0:T(8,128)(2,1)S(1)} %get-tuple-element.91), channel_id=1, source_target_pairs={{64,0},{128,64},{192,128},{256,192},{320,256},{384,320},{448,384},... | collective-permute-start | bytes 983048 | tf_op jit(solution)/shard_map/ppermute | solution.py:353
  124.8 4.4 %collective-permute-done.6.recv = bf16[32,5120]{1,0:T(8,128)(2,1)S(1)} collective-permute-done((bf16[32,5120]{1,0:T(8,128)(2,1)S(1)}, bf16[32,5120]{1,0:T(8,128)(2,1)S(1)}, u32[]{:S(2)}, u32[]{:S(2)}) %collective-permute-start.6) | collective-permute-done | bytes 327712 | tf_op jit(solution)/shard_map/ppermute | solution.py:353
  129.8 4.2 %collective-permute-start.7 = (bf16[32,5120]{1,0:T(8,128)(2,1)S(1)}, bf16[32,5120]{1,0:T(8,128)(2,1)S(1)}, u32[]{:S(2)}, u32[]{:S(2)}) collective-permute-start(bf16[32,5120]{1,0:T(8,128)(2,1)S(1)} %get-tuple-element.96), channel_id=1, source_target_pairs={{64,0},{128,64},{192,128},{256,192},{320,256},{384,320},{448,384},... | collective-permute-start | bytes 983048 | tf_op jit(solution)/shard_map/ppermute | solution.py:353
  134.2 4.4 %collective-permute-done.7.recv = bf16[32,5120]{1,0:T(8,128)(2,1)S(1)} collective-permute-done((bf16[32,5120]{1,0:T(8,128)(2,1)S(1)}, bf16[32,5120]{1,0:T(8,128)(2,1)S(1)}, u32[]{:S(2)}, u32[]{:S(2)}) %collective-permute-start.7) | collective-permute-done | bytes 327712 | tf_op jit(solution)/shard_map/ppermute | solution.py:353
  139.4 4.0 %collective-permute-start.8 = (bf16[32,5120]{1,0:T(8,128)(2,1)S(1)}, bf16[32,5120]{1,0:T(8,128)(2,1)S(1)}, u32[]{:S(2)}, u32[]{:S(2)}) collective-permute-start(bf16[32,5120]{1,0:T(8,128)(2,1)S(1)} %get-tuple-element.101), channel_id=1, source_target_pairs={{64,0},{128,64},{192,128},{256,192},{320,256},{384,320},{448,384},... | collective-permute-start | bytes 983048 | tf_op jit(solution)/shard_map/ppermute | solution.py:353
  143.7 8.1 %collective-permute-done.8.recv = bf16[32,5120]{1,0:T(8,128)(2,1)S(1)} collective-permute-done((bf16[32,5120]{1,0:T(8,128)(2,1)S(1)}, bf16[32,5120]{1,0:T(8,128)(2,1)S(1)}, u32[]{:S(2)}, u32[]{:S(2)}) %collective-permute-start.8) | collective-permute-done | bytes 327712 | tf_op jit(solution)/shard_map/ppermute | solution.py:353
  151.8 3.8 %stage.16 = (bf16[32,5120]{1,0:T(8,128)(2,1)S(1)}, f32[128,128]{1,0:T(8,128)S(1)}, f32[128,128]{1,0:T(8,128)S(1)}, bf16[128,288]{1,0:T(8,128)(2,1)S(1)}, bf16[128,128]{1,0:T(8,128)(2,1)S(1)}) custom-call(s32[3]{0:T(128)S(1)} %copy-done.46, ...), custom_call_target="tpu_custom_call", output_to_operand_aliasing={{1}: (15, {}), {2}: (16, {}), {3}: (17, {}), {4}: (18, {})} | custom-call | tf_op jit(solution)/shard_map/stage/pallas_call | solution.py:308
  155.6 1.9 collective-permute-start.9
  157.7 6.6 %collective-permute-done.9.recv = bf16[32,5120]{1,0:T(8,128)(2,1)S(1)} collective-permute-done((bf16[32,5120]{1,0:T(8,128)(2,1)S(1)}, bf16[32,5120]{1,0:T(8,128)(2,1)S(1)}, u32[]{:S(2)}, u32[]{:S(2)}) %collective-permute-start.9) | collective-permute-done | bytes 327712 | tf_op jit(solution)/shard_map/ppermute | solution.py:353
  164.3 3.8 %stage.17 = (bf16[32,5120]{1,0:T(8,128)(2,1)S(1)}, f32[128,128]{1,0:T(8,128)S(1)}, f32[128,128]{1,0:T(8,128)S(1)}, bf16[128,288]{1,0:T(8,128)(2,1)S(1)}, bf16[128,128]{1,0:T(8,128)(2,1)S(1)}) custom-call(s32[3]{0:T(128)S(1)} %copy-done.45, ...), custom_call_target="tpu_custom_call", output_to_operand_aliasing={{1}: (15, {}), {2}: (16, {}), {3}: (17, {}), {4}: (18, {})} | custom-call | tf_op jit(solution)/shard_map/stage/pallas_call | solution.py:308
  168.1 1.9 collective-permute-start.10
  170.3 6.6 %collective-permute-done.10.recv = bf16[32,5120]{1,0:T(8,128)(2,1)S(1)} collective-permute-done((bf16[32,5120]{1,0:T(8,128)(2,1)S(1)}, bf16[32,5120]{1,0:T(8,128)(2,1)S(1)}, u32[]{:S(2)}, u32[]{:S(2)}) %collective-permute-start.10) | collective-permute-done | bytes 327712 | tf_op jit(solution)/shard_map/ppermute | solution.py:353
  176.9 3.8 %stage.18 = (bf16[32,5120]{1,0:T(8,128)(2,1)S(1)}, f32[128,128]{1,0:T(8,128)S(1)}, f32[128,128]{1,0:T(8,128)S(1)}, bf16[128,288]{1,0:T(8,128)(2,1)S(1)}, bf16[128,128]{1,0:T(8,128)(2,1)S(1)}) custom-call(s32[3]{0:T(128)S(1)} %copy-done.44, ...), custom_call_target="tpu_custom_call", output_to_operand_aliasing={{1}: (15, {}), {2}: (16, {}), {3}: (17, {}), {4}: (18, {})} | custom-call | tf_op jit(solution)/shard_map/stage/pallas_call | solution.py:308
  180.7 1.9 collective-permute-start.11
  182.8 6.2 %collective-permute-done.11.recv = bf16[32,5120]{1,0:T(8,128)(2,1)S(1)} collective-permute-done((bf16[32,5120]{1,0:T(8,128)(2,1)S(1)}, bf16[32,5120]{1,0:T(8,128)(2,1)S(1)}, u32[]{:S(2)}, u32[]{:S(2)}) %collective-permute-start.11) | collective-permute-done | bytes 327712 | tf_op jit(solution)/shard_map/ppermute | solution.py:353
  189.1 4.5 %stage.19 = (bf16[32,5120]{1,0:T(8,128)(2,1)}, f32[128,128]{1,0:T(8,128)S(1)}, f32[128,128]{1,0:T(8,128)S(1)}, bf16[128,288]{1,0:T(8,128)(2,1)S(1)}, bf16[128,128]{1,0:T(8,128)(2,1)S(1)}) custom-call(s32[3]{0:T(128)S(1)} %copy-done.43, ...), custom_call_target="tpu_custom_call", output_to_operand_aliasing={{1}: (15, {}), {2}: (16, {}), {3}: (17, {}), {4}: (18, {})} | custom-call | tf_op jit(solution)/shard_map/stage/pallas_call | solution.py:308
  193.5 1.9 collective-permute-start.12
  197.8 5.9 %all-to-all-start.2 = ((bf16[32,120,128]{2,1,0:T(8,128)(2,1)}), bf16[32,120,128]{2,1,0:T(8,128)(2,1)}, u32[]{:S(2)}, u32[]{:S(2)}) async-start(bf16[32,120,128]{2,1,0:T(8,128)(2,1)} %copy-done.26), calls=%async_computation.2 | async-start | bytes 1966080 | tf_op jit(solution)/shard_map/all_to_all | solution.py:351
  203.7 1.9 select_dynamic-update-slice_fusion.10
  205.7 2.5 copy-done.2
  212.9 4.8 %collective-permute-start.13 = (bf16[32,5120]{1,0:T(8,128)(2,1)S(1)}, bf16[32,5120]{1,0:T(8,128)(2,1)S(1)}, u32[]{:S(2)}, u32[]{:S(2)}) collective-permute-start(bf16[32,5120]{1,0:T(8,128)(2,1)S(1)} %get-tuple-element.126), channel_id=1, source_target_pairs={{64,0},{128,64},{192,128},{256,192},{320,256},{384,320},{448,384},... | collective-permute-start | bytes 983048 | tf_op jit(solution)/shard_map/ppermute | solution.py:353
  217.8 4.4 %collective-permute-done.13.recv = bf16[32,5120]{1,0:T(8,128)(2,1)S(1)} collective-permute-done((bf16[32,5120]{1,0:T(8,128)(2,1)S(1)}, bf16[32,5120]{1,0:T(8,128)(2,1)S(1)}, u32[]{:S(2)}, u32[]{:S(2)}) %collective-permute-start.13) | collective-permute-done | bytes 327712 | tf_op jit(solution)/shard_map/ppermute | solution.py:353
  224.1 6.2 %all-to-all-done.2.got = bf16[32,120,128]{2,1,0:T(8,128)(2,1)} async-done(((bf16[32,120,128]{2,1,0:T(8,128)(2,1)}), bf16[32,120,128]{2,1,0:T(8,128)(2,1)}, u32[]{:S(2)}, u32[]{:S(2)}) %all-to-all-start.2) | async-done | bytes 983072 | tf_op jit(solution)/shard_map/all_to_all | solution.py:351
  230.3 6.4 %all-to-all-start.3 = ((bf16[32,80,128]{2,1,0:T(8,128)(2,1)}), bf16[32,80,128]{2,1,0:T(8,128)(2,1)}, u32[]{:S(2)}, u32[]{:S(2)}) async-start(bf16[32,80,128]{2,1,0:T(8,128)(2,1)} %copy-done.32), calls=%async_computation.3 | async-start | bytes 1310720 | tf_op jit(solution)/shard_map/all_to_all | solution.py:336
  238.5 2.5 copy.170
  242.3 2.2 shard_map.129.sofar
  245.3 2.5 copy-done.3
  251.0 6.3 %all-to-all-done.3.got = bf16[32,80,128]{2,1,0:T(8,128)(2,1)} async-done(((bf16[32,80,128]{2,1,0:T(8,128)(2,1)}), bf16[32,80,128]{2,1,0:T(8,128)(2,1)}, u32[]{:S(2)}, u32[]{:S(2)}) %all-to-all-start.3) | async-done | bytes 655392 | tf_op jit(solution)/shard_map/all_to_all | solution.py:336
  260.2 7.0 %collective-permute-start.14 = (f32[80,128]{1,0:T(8,128)S(1)}, f32[80,128]{1,0:T(8,128)S(1)}, u32[]{:S(2)}, u32[]{:S(2)}) collective-permute-start(f32[80,128]{1,0:T(8,128)S(1)} %slice_select_fusion), channel_id=1, source_target_pairs={{0,32},{32,0},{1,33},{33,1},{2,34},{34,2},{3,35},{35,3},{4,36},{36... | collective-permute-start | bytes 122888 | tf_op jit(solution)/shard_map/ppermute | solution.py:369
  268.0 1.9 collective-permute-done.14
  (177 shorter events, 44.6 us)
Async XLA Ops:
  8.0 12.5 %collective-permute-start.3 = (bf16[80,512]{1,0:T(8,128)(2,1)S(1)}, bf16[80,512]{1,0:T(8,128)(2,1)S(1)}, u32[]{:S(2)}, u32[]{:S(2)}) collective-permute-start(bf16[80,512]{1,0:T(8,128)(2,1)S(1)} %get-tuple-element.141), channel_id=1, source_target_pairs={{0,32},{32,0},{1,33},{33,1},{2,34},{34,2},{3,35},{35,3},{4,36},{36... | collective-permute-start | bytes 245768 | tf_op jit(solution)/shard_map/ppermute | solution.py:227
  21.4 27.8 %copy-start.54 = (bf16[1,5120]{1,0:T(2,128)(2,1)S(1)}, bf16[1,5120]{1,0:T(2,128)(2,1)}, u32[]{:S(2)}) copy-start(bf16[1,5120]{1,0:T(2,128)(2,1)} %param.12) | copy-start | bytes 30724
  21.4 27.8 %copy-start.4 = (bf16[1,128,5120]{2,1,0:T(8,128)(2,1)S(1)}, bf16[1,128,5120]{2,1,0:T(8,128)(2,1)}, u32[]{:S(2)}) copy-start(bf16[1,128,5120]{2,1,0:T(8,128)(2,1)} %param.10) | copy-start | bytes 3932164
  21.4 27.0 %all-to-all-start = ((bf16[8,80,512]{2,1,0:T(8,128)(2,1)}), bf16[8,80,512]{2,1,0:T(8,128)(2,1)S(1)}, u32[]{:S(2)}, u32[]{:S(2)}) async-start(bf16[8,80,512]{2,1,0:T(8,128)(2,1)} %broadcast_in_dim.45), calls=%async_computation | async-start | bytes 1310720 | tf_op jit(solution)/shard_map/all_to_all | solution.py:231
  28.6 64.6 %all-gather.4.cloned.1.call-start = ((), (), s32[]{:S(2)}) async-start(), calls=%async_computation.4 | async-start | bytes 2949120 | tf_op jit(solution)/shard_map/all_gather | solution.py:233
  28.7 10.5 %collective-permute-start = (bf16[80,512]{1,0:T(8,128)(2,1)S(1)}, bf16[80,512]{1,0:T(8,128)(2,1)S(1)}, u32[]{:S(2)}, u32[]{:S(2)}) collective-permute-start(bf16[80,512]{1,0:T(8,128)(2,1)S(1)} %get-tuple-element.141), channel_id=1, source_target_pairs={{0,1},{1,2},{2,3},{3,0},{4,5},{5,6},{6,7},{7,4},{8,9},{9,10},{10,1... | collective-permute-start | bytes 245768 | tf_op jit(solution)/shard_map/ppermute | solution.py:230
  32.1 8.4 %collective-permute-start.1 = (bf16[80,512]{1,0:T(8,128)(2,1)S(1)}, bf16[80,512]{1,0:T(8,128)(2,1)S(1)}, u32[]{:S(2)}, u32[]{:S(2)}) collective-permute-start(bf16[80,512]{1,0:T(8,128)(2,1)S(1)} %get-tuple-element.141), channel_id=1, source_target_pairs={{0,2},{1,3},{2,0},{3,1},{4,6},{5,7},{6,4},{7,5},{8,10},{9,11},{10,... | collective-permute-start | bytes 245768 | tf_op jit(solution)/shard_map/ppermute | solution.py:230
  35.1 6.3 %collective-permute-start.2 = (bf16[80,512]{1,0:T(8,128)(2,1)S(1)}, bf16[80,512]{1,0:T(8,128)(2,1)S(1)}, u32[]{:S(2)}, u32[]{:S(2)}) collective-permute-start(bf16[80,512]{1,0:T(8,128)(2,1)S(1)} %get-tuple-element.141), channel_id=1, source_target_pairs={{0,3},{1,0},{2,1},{3,2},{4,7},{5,4},{6,5},{7,6},{8,11},{9,8},{10,9... | collective-permute-start | bytes 245768 | tf_op jit(solution)/shard_map/ppermute | solution.py:230
  49.2 15.2 %copy-start.27 = (f32[1,5120]{1,0:T(1,128)}, f32[1,5120]{1,0:T(1,128)S(1)}, u32[]{:S(2)}) copy-start(f32[1,5120]{1,0:T(1,128)S(1)} %convert_element_type.13.gain) | copy-start | bytes 61444
  58.0 5.2 %copy-start.5 = (bf16[128,5120]{1,0:T(8,128)(2,1)S(1)}, bf16[128,5120]{1,0:T(8,128)(2,1)}, u32[]{:S(2)}) copy-start(bf16[128,5120]{1,0:T(8,128)(2,1)} %top.21) | copy-start | bytes 3932164
  58.0 35.2 %all-to-all-start.1 = ((bf16[4,8,80,512]{3,2,1,0:T(8,128)(2,1)}), bf16[4,8,80,512]{3,2,1,0:T(8,128)(2,1)}, u32[]{:S(2)}, u32[]{:S(2)}) async-start(bf16[4,8,80,512]{3,2,1,0:T(8,128)(2,1)} %broadcast_in_dim.46), calls=%async_computation.1 | async-start | bytes 5242880 | tf_op jit(solution)/shard_map/all_to_all | solution.py:234
  63.2 177.8 %all-gather.6.cloned.1.call-start = ((), (), s32[]{:S(2)}) async-start(), calls=%async_computation.5 | async-start | bytes 1351680 | tf_op jit(solution)/shard_map/all_gather | solution.py:271
  74.2 19.0 %copy-start.9 = (bf16[1,288,128]{2,1,0:T(8,128)(2,1)S(1)}, bf16[1,288,128]{2,1,0:T(8,128)(2,1)}, u32[]{:S(2)}) copy-start(bf16[1,288,128]{2,1,0:T(8,128)(2,1)} %param.15) | copy-start | bytes 221188
  74.2 19.0 %copy-start.10 = (bf16[1,288,128]{2,1,0:T(8,128)(2,1)S(1)}, bf16[1,288,128]{2,1,0:T(8,128)(2,1)}, u32[]{:S(2)}) copy-start(bf16[1,288,128]{2,1,0:T(8,128)(2,1)} %param.16) | copy-start | bytes 221188
  74.2 19.0 %copy-start.40 = (bf16[1,32,128]{2,1,0:T(8,128)(2,1)S(1)}, bf16[1,32,128]{2,1,0:T(8,128)(2,1)}, u32[]{:S(2)}) copy-start(bf16[1,32,128]{2,1,0:T(8,128)(2,1)} %param.18) | copy-start | bytes 24580
  93.2 5.7 %copy-start.28 = (f32[1,5120]{1,0:T(1,128)S(1)}, f32[1,5120]{1,0:T(1,128)}, u32[]{:S(2)}) copy-start(f32[1,5120]{1,0:T(1,128)} %copy-done.27) | copy-start | bytes 61444
  93.2 5.7 %copy-start.51 = (s32[3]{0:T(128)S(1)}, s32[3]{0:T(128)}, u32[]{:S(2)}) copy-start(s32[3]{0:T(128)} %get-tuple-element.144.flags) | copy-start | bytes 40
  101.3 6.8 %collective-permute-start.4 = (bf16[32,5120]{1,0:T(8,128)(2,1)}, bf16[32,5120]{1,0:T(8,128)(2,1)}, u32[]{:S(2)}, u32[]{:S(2)}) collective-permute-start(bf16[32,5120]{1,0:T(8,128)(2,1)} %get-tuple-element.81), channel_id=1, source_target_pairs={{64,0},{128,64},{192,128},{256,192},{320,256},{384,320},{448,384},... | collective-permute-start | bytes 983048 | tf_op jit(solution)/shard_map/ppermute | solution.py:353
  103.2 4.9 %copy-start.14 = (bf16[128,128]{1,0:T(8,128)(2,1)S(1)}, bf16[128,128]{1,0:T(8,128)(2,1)}, u32[]{:S(2)}) copy-start(bf16[128,128]{1,0:T(8,128)(2,1)} %copy-done.13) | copy-start | bytes 98308
  103.2 4.9 %copy-start.19 = (bf16[128,128]{1,0:T(8,128)(2,1)S(1)}, bf16[128,128]{1,0:T(8,128)(2,1)}, u32[]{:S(2)}) copy-start(bf16[128,128]{1,0:T(8,128)(2,1)} %copy-done.18) | copy-start | bytes 98308
  103.2 4.8 %copy-start.23 = (bf16[128,128]{1,0:T(8,128)(2,1)S(1)}, bf16[128,128]{1,0:T(8,128)(2,1)}, u32[]{:S(2)}) copy-start(bf16[128,128]{1,0:T(8,128)(2,1)} %copy-done.22) | copy-start | bytes 98308
  103.2 4.8 %copy-start.29 = (f32[1,5120]{1,0:T(1,128)S(1)}, f32[1,5120]{1,0:T(1,128)}, u32[]{:S(2)}) copy-start(f32[1,5120]{1,0:T(1,128)} %copy-done.27) | copy-start | bytes 61444
  110.6 5.1 %copy-start.6 = (bf16[128,5120]{1,0:T(8,128)(2,1)S(1)}, bf16[128,5120]{1,0:T(8,128)(2,1)}, u32[]{:S(2)}) copy-start(bf16[128,5120]{1,0:T(8,128)(2,1)} %broadcast_select_fusion) | copy-start | bytes 3932164
  111.7 8.4 %copy-start.49 = (s32[3]{0:T(128)S(1)}, s32[3]{0:T(128)}, u32[]{:S(2)}) copy-start(s32[3]{0:T(128)} %add_add_fusion.2.flags) | copy-start | bytes 40
  111.8 8.4 %collective-permute-start.5 = (bf16[32,5120]{1,0:T(8,128)(2,1)S(1)}, bf16[32,5120]{1,0:T(8,128)(2,1)S(1)}, u32[]{:S(2)}, u32[]{:S(2)}) collective-permute-start(bf16[32,5120]{1,0:T(8,128)(2,1)S(1)} %get-tuple-element.86), channel_id=1, source_target_pairs={{64,0},{128,64},{192,128},{256,192},{320,256},{384,320},{448,384},... | collective-permute-start | bytes 983048 | tf_op jit(solution)/shard_map/ppermute | solution.py:353
  120.8 8.4 %copy-start.48 = (s32[3]{0:T(128)S(1)}, s32[3]{0:T(128)}, u32[]{:S(2)}) copy-start(s32[3]{0:T(128)} %add_add_fusion.3.flags) | copy-start | bytes 40
  120.8 8.4 %collective-permute-start.6 = (bf16[32,5120]{1,0:T(8,128)(2,1)S(1)}, bf16[32,5120]{1,0:T(8,128)(2,1)S(1)}, u32[]{:S(2)}, u32[]{:S(2)}) collective-permute-start(bf16[32,5120]{1,0:T(8,128)(2,1)S(1)} %get-tuple-element.91), channel_id=1, source_target_pairs={{64,0},{128,64},{192,128},{256,192},{320,256},{384,320},{448,384},... | collective-permute-start | bytes 983048 | tf_op jit(solution)/shard_map/ppermute | solution.py:353
  129.8 8.8 %copy-start.47 = (s32[3]{0:T(128)S(1)}, s32[3]{0:T(128)}, u32[]{:S(2)}) copy-start(s32[3]{0:T(128)} %add_add_fusion.4.flags) | copy-start | bytes 40
  129.8 8.8 %collective-permute-start.7 = (bf16[32,5120]{1,0:T(8,128)(2,1)S(1)}, bf16[32,5120]{1,0:T(8,128)(2,1)S(1)}, u32[]{:S(2)}, u32[]{:S(2)}) collective-permute-start(bf16[32,5120]{1,0:T(8,128)(2,1)S(1)} %get-tuple-element.96), channel_id=1, source_target_pairs={{64,0},{128,64},{192,128},{256,192},{320,256},{384,320},{448,384},... | collective-permute-start | bytes 983048 | tf_op jit(solution)/shard_map/ppermute | solution.py:353
  139.4 12.4 %copy-start.46 = (s32[3]{0:T(128)S(1)}, s32[3]{0:T(128)}, u32[]{:S(2)}) copy-start(s32[3]{0:T(128)} %add_add_fusion.5.flags) | copy-start | bytes 40
  139.4 12.4 %collective-permute-start.8 = (bf16[32,5120]{1,0:T(8,128)(2,1)S(1)}, bf16[32,5120]{1,0:T(8,128)(2,1)S(1)}, u32[]{:S(2)}, u32[]{:S(2)}) collective-permute-start(bf16[32,5120]{1,0:T(8,128)(2,1)S(1)} %get-tuple-element.101), channel_id=1, source_target_pairs={{64,0},{128,64},{192,128},{256,192},{320,256},{384,320},{448,384},... | collective-permute-start | bytes 983048 | tf_op jit(solution)/shard_map/ppermute | solution.py:353
  155.6 8.8 %copy-start.45 = (s32[3]{0:T(128)S(1)}, s32[3]{0:T(128)}, u32[]{:S(2)}) copy-start(s32[3]{0:T(128)} %add_add_fusion.6.flags) | copy-start | bytes 40
  155.6 8.8 %collective-permute-start.9 = (bf16[32,5120]{1,0:T(8,128)(2,1)S(1)}, bf16[32,5120]{1,0:T(8,128)(2,1)S(1)}, u32[]{:S(2)}, u32[]{:S(2)}) collective-permute-start(bf16[32,5120]{1,0:T(8,128)(2,1)S(1)} %get-tuple-element.106), channel_id=1, source_target_pairs={{64,0},{128,64},{192,128},{256,192},{320,256},{384,320},{448,384},... | collective-permute-start | bytes 983048 | tf_op jit(solution)/shard_map/ppermute | solution.py:353
  168.1 8.8 %copy-start.44 = (s32[3]{0:T(128)S(1)}, s32[3]{0:T(128)}, u32[]{:S(2)}) copy-start(s32[3]{0:T(128)} %add_add_fusion.7.flags) | copy-start | bytes 40
  168.1 8.8 %collective-permute-start.10 = (bf16[32,5120]{1,0:T(8,128)(2,1)S(1)}, bf16[32,5120]{1,0:T(8,128)(2,1)S(1)}, u32[]{:S(2)}, u32[]{:S(2)}) collective-permute-start(bf16[32,5120]{1,0:T(8,128)(2,1)S(1)} %get-tuple-element.111), channel_id=1, source_target_pairs={{64,0},{128,64},{192,128},{256,192},{320,256},{384,320},{448,384},... | collective-permute-start | bytes 983048 | tf_op jit(solution)/shard_map/ppermute | solution.py:353
  180.7 8.4 %copy-start.43 = (s32[3]{0:T(128)S(1)}, s32[3]{0:T(128)}, u32[]{:S(2)}) copy-start(s32[3]{0:T(128)} %add_add_fusion.8.flags) | copy-start | bytes 40
  180.7 8.4 %collective-permute-start.11 = (bf16[32,5120]{1,0:T(8,128)(2,1)S(1)}, bf16[32,5120]{1,0:T(8,128)(2,1)S(1)}, u32[]{:S(2)}, u32[]{:S(2)}) collective-permute-start(bf16[32,5120]{1,0:T(8,128)(2,1)S(1)} %get-tuple-element.116), channel_id=1, source_target_pairs={{64,0},{128,64},{192,128},{256,192},{320,256},{384,320},{448,384},... | collective-permute-start | bytes 983048 | tf_op jit(solution)/shard_map/ppermute | solution.py:353
  182.7 10.8 %copy-start.52 = (bf16[128,5120]{1,0:T(8,128)(2,1)}, bf16[128,5120]{1,0:T(8,128)(2,1)S(1)}, u32[]{:S(2)}) copy-start(bf16[128,5120]{1,0:T(8,128)(2,1)S(1)} %select_dynamic-update-slice_fusion.11) | copy-start | bytes 3932164
  189.1 6.5 %copy-start.35 = (bf16[32,40,128]{2,1,0:T(8,128)(2,1)S(1)}, bf16[32,40,128]{2,1,0:T(8,128)(2,1)}, u32[]{:S(2)}) copy-start(bf16[32,40,128]{2,1,0:T(8,128)(2,1)} %reshape.40.packed) | copy-start | bytes 983044
  193.5 12.1 %collective-permute-start.12 = (bf16[32,5120]{1,0:T(8,128)(2,1)}, bf16[32,5120]{1,0:T(8,128)(2,1)}, u32[]{:S(2)}, u32[]{:S(2)}) collective-permute-start(bf16[32,5120]{1,0:T(8,128)(2,1)} %get-tuple-element.121), channel_id=1, source_target_pairs={{64,0},{128,64},{192,128},{256,192},{320,256},{384,320},{448,384},... | collective-permute-start | bytes 983048 | tf_op jit(solution)/shard_map/ppermute | solution.py:353
  197.8 32.5 %all-to-all-start.2 = ((bf16[32,120,128]{2,1,0:T(8,128)(2,1)}), bf16[32,120,128]{2,1,0:T(8,128)(2,1)}, u32[]{:S(2)}, u32[]{:S(2)}) async-start(bf16[32,120,128]{2,1,0:T(8,128)(2,1)} %copy-done.26), calls=%async_computation.2 | async-start | bytes 1966080 | tf_op jit(solution)/shard_map/all_to_all | solution.py:351
  211.8 5.9 %copy-start.8 = (bf16[128,5120]{1,0:T(8,128)(2,1)S(1)}, bf16[128,5120]{1,0:T(8,128)(2,1)}, u32[]{:S(2)}) copy-start(bf16[128,5120]{1,0:T(8,128)(2,1)} %copy-done.7) | copy-start | bytes 3932164
  212.9 9.4 %copy-start.38 = (bf16[32,5120]{1,0:T(8,128)(2,1)}, bf16[32,5120]{1,0:T(8,128)(2,1)S(1)}, u32[]{:S(2)}) copy-start(bf16[32,5120]{1,0:T(8,128)(2,1)S(1)} %get-tuple-element.126) | copy-start | bytes 983044
  212.9 9.3 %collective-permute-start.13 = (bf16[32,5120]{1,0:T(8,128)(2,1)S(1)}, bf16[32,5120]{1,0:T(8,128)(2,1)S(1)}, u32[]{:S(2)}, u32[]{:S(2)}) collective-permute-start(bf16[32,5120]{1,0:T(8,128)(2,1)S(1)} %get-tuple-element.126), channel_id=1, source_target_pairs={{64,0},{128,64},{192,128},{256,192},{320,256},{384,320},{448,384},... | collective-permute-start | bytes 983048 | tf_op jit(solution)/shard_map/ppermute | solution.py:353
  230.3 27.0 %all-to-all-start.3 = ((bf16[32,80,128]{2,1,0:T(8,128)(2,1)}), bf16[32,80,128]{2,1,0:T(8,128)(2,1)}, u32[]{:S(2)}, u32[]{:S(2)}) async-start(bf16[32,80,128]{2,1,0:T(8,128)(2,1)} %copy-done.32), calls=%async_computation.3 | async-start | bytes 1310720 | tf_op jit(solution)/shard_map/all_to_all | solution.py:336
  248.4 8.9 %copy-start.37 = (f32[80,256]{1,0:T(8,128)S(1)}, f32[80,256]{1,0:T(8,128)}, u32[]{:S(2)}) copy-start(f32[80,256]{1,0:T(8,128)} %copy-done.36) | copy-start | bytes 245764
  258.6 8.6 %copy-start.17 = (bf16[128,128]{1,0:T(8,128)(2,1)S(1)}, bf16[128,128]{1,0:T(8,128)(2,1)}, u32[]{:S(2)}) copy-start(bf16[128,128]{1,0:T(8,128)(2,1)} %copy-done.13) | copy-start | bytes 98308
  260.2 9.8 %collective-permute-start.14 = (f32[80,128]{1,0:T(8,128)S(1)}, f32[80,128]{1,0:T(8,128)S(1)}, u32[]{:S(2)}, u32[]{:S(2)}) collective-permute-start(f32[80,128]{1,0:T(8,128)S(1)} %slice_select_fusion), channel_id=1, source_target_pairs={{0,32},{32,0},{1,33},{33,1},{2,34},{34,2},{3,35},{35,3},{4,36},{36... | collective-permute-start | bytes 122888 | tf_op jit(solution)/shard_map/ppermute | solution.py:369
  (28 other events, 53.3 us)
Sparse Core Ops, SparseCore 0:
  48.5 43.0 all-gather.3
  103.3 79.1 all-gather.5

commit v5 on v4

--- a/solution.py
+++ b/solution.py
@@ -171,6 +171,19 @@
     flip(jnp.concatenate([first, gin[rows : tokens // 2, :]], axis=0), out)
 
 
+def finish_kernel(flags, kept, soon, last, out):
+    rows = soon.shape[0]
+    out[...] = kept[...]
+
+    @pl.when(flags[0] == 1)
+    def _():
+        out[pl.ds(pl.multiple_of(flags[1] * rows, rows), rows), :] = soon[...]
+
+    @pl.when(flags[2] == 1)
+    def _():
+        out[pl.ds(pl.multiple_of(flags[3] * rows, rows), rows), :] = last[...]
+
+
 def spread(a, times):
     none = jnp.zeros_like(a)
     return [jnp.concatenate([none] * i + [a] + [none] * (times - 1 - i), axis=1) for i in range(times)]
@@ -229,9 +242,11 @@
     for d in range(1, nx):
         turns_x.append(lax.ppermute(own, "x", [(i, (i + d) % nx) for i in range(nx)]))
     along_y = lax.all_to_all(jnp.broadcast_to(other[None], (ny, *other.shape)), "y", 0, 0, tiled=True)
-    mine, along_y, early_dy = lax.optimization_barrier((jnp.stack(turns_x)[None], along_y, early_dy))
+    mine = jnp.stack(turns_x)[None]
+    along_y, early_dy = lax.optimization_barrier((along_y, early_dy))
     wa = lax.all_gather(mine, "y", axis=0, tiled=True)
-    wb = lax.all_to_all(jnp.broadcast_to(along_y[None], (nx, *along_y.shape)), "x", 0, 0, tiled=True)
+    copies, x = lax.optimization_barrier((jnp.broadcast_to(along_y[None], (nx, *along_y.shape)), x))
+    wb = lax.all_to_all(copies, "x", 0, 0, tiled=True)
 
     wide = x.astype(f32)
     gain = norm_gain.astype(f32)
@@ -323,6 +338,7 @@
     halfway = sections + PARTS // 2 - 2
     for t in range(turns):
         if t == turns - 1:
+            recv, gx_all = lax.optimization_barrier((recv, gx_all))
             flag = (section == 0).astype(jnp.int32)[None]
             late = pl.pallas_call(
                 turn_late_half,
@@ -337,7 +353,10 @@
         elif t > 0:
             gin_all = keep(gin_all, recv, t, jnp.logical_not(is_top))
         send, *state = compute(t, recv, state)
-        gx_all = keep(gx_all, send, t, True)
+        if t < turns - 2:
+            gx_all = keep(gx_all, send, t, True)
+        elif t == turns - 2:
+            sent = send
         if t == halfway:
             gin_now, _ = lax.optimization_barrier((gin_all, send))
             soon = pl.pallas_call(
@@ -351,6 +370,16 @@
             got_soon = lax.all_to_all(soon, PLANE, 0, 0, tiled=True)
         if t < turns - 1:
             recv = lax.ppermute(send, SECTION, down)
+    (part_soon, on_soon), (part_last, on_last) = place(turns - 2), place(turns - 1)
+    flags = [on_soon.astype(jnp.int32), part_soon, on_last.astype(jnp.int32), part_last]
+    gx_all = pl.pallas_call(
+        finish_kernel,
+        name="finish",
+        in_specs=[SMEM] + [VMEM] * 3,
+        out_specs=VMEM,
+        out_shape=shape((tokens, width), bf16),
+        compiler_params=room,
+    )(jnp.stack(flags), gx_all, sent, send)
     _, _, gsc, go_all = state
     key_out = dot(gsc, q, 0, 0).astype(bf16)
     value_out = dot(pc.astype(bf16), go_all, 0, 0).astype(bf16)

time: 279 us -> 293 us (1.050)
  waiting for transfers between devices: 90.1 us -> 105 us
    all_to_all x1, waiting for transfers between devices: 6.13 us -> 26.3 us  [body(): lax.all_to_all(jnp.broadcast_to(other[None], (ny, *other.shape)), 'y', 0,...]
    all_to_all x1, waiting for transfers between devices: 6.28 us -> 10.4 us  [body(): got_late = lax.all_to_all(late, PLANE, 0, 0, tiled=True)]
    dynamic_update_slice x20 -> x17, other arithmetic: 7.25 us -> 3.62 us  [keep(): lax.dynamic_update_slice_in_dim(whole, jnp.where(jnp.logical_and(active,...]
    all_to_all x1, waiting for transfers between devices: 15 us -> 11.6 us  [body(): wb = lax.all_to_all(copies, 'x', 0, 0, tiled=True)]
    unnamed x111 -> x120, local copies, waits for them, and re-layouts: 21.6 us -> 22.2 us
  transfers between devices with their start and end apart: 21 -> 21, of which waited for: 17 -> 16; matrix products, arithmetic and copies ran while one was open for 13% -> 11% of each run, Pallas kernels for 8% -> 9%
where the time goes in v5:
time: 293 us; the launch traced here: 291 us
  waiting for transfers between devices  105 us (36%)
  starting transfers between devices  82 us (28%)
  local copies, waits for them, and re-layouts  37.5 us (13%)
  Pallas kernels  33.4 us (11%)
  other arithmetic  16.3 us (6%)
  between operations  15.5 us (5%)
    ppermute x10, waiting for transfers between devices, body(): recv = lax.ppermute(send, SECTION, down)  47.3 us
    ppermute x10, starting transfers between devices, body(): recv = lax.ppermute(send, SECTION, down)  30.2 us
    all_to_all x1, waiting for transfers between devices, body(): lax.all_to_all(jnp.broadcast_to(other[None], (ny, *other.shape)), 'y', 0,...  26.3 us
    pallas_call x11, Pallas kernels, compute(): stage(flags, recv, top_grad, w, x, gain, inv, q, kc, kn, vc, vn, pc, pn,...  22.4 us
    unnamed x120, local copies, waits for them, and re-layouts  22.2 us
    all_to_all x1, waiting for transfers between devices, body(): wb = lax.all_to_all(copies, 'x', 0, 0, tiled=True)  11.6 us
    ppermute x3, starting transfers between devices, body(): lax.ppermute(own, 'x', [(i, (i + d) % nx) for i in range(nx)])  10.5 us
    all_to_all x1, waiting for transfers between devices, body(): got_late = lax.all_to_all(late, PLANE, 0, 0, tiled=True)  10.4 us
  transfers between devices with their start and end apart: 21, of which 16 were waited for; matrix products, arithmetic and copies ran while one was open for 11% of the time, Pallas kernels for 9%

profile of v5, /device:TPU:66, one launch (start us, length us, event | category | flops | bytes accessed | tf_op | source)
XLA Modules:
  0.0 290.9 jit_solution(16752134211078687860)
XLA Ops:
  8.1 3.4 %collective-permute-start.1 = (bf16[80,512]{1,0:T(8,128)(2,1)S(1)}, bf16[80,512]{1,0:T(8,128)(2,1)S(1)}, u32[]{:S(2)}, u32[]{:S(2)}) collective-permute-start(bf16[80,512]{1,0:T(8,128)(2,1)S(1)} %get-tuple-element.147), channel_id=1, source_target_pairs={{0,1},{1,2},{2,3},{3,0},{4,5},{5,6},{6,7},{7,4},{8,9},{9,10},{10,1... | collective-permute-start | bytes 245768 | tf_op jit(solution)/shard_map/ppermute | solution.py:243
  11.5 3.0 %collective-permute-start.2 = (bf16[80,512]{1,0:T(8,128)(2,1)S(1)}, bf16[80,512]{1,0:T(8,128)(2,1)S(1)}, u32[]{:S(2)}, u32[]{:S(2)}) collective-permute-start(bf16[80,512]{1,0:T(8,128)(2,1)S(1)} %get-tuple-element.147), channel_id=1, source_target_pairs={{0,2},{1,3},{2,0},{3,1},{4,6},{5,7},{6,4},{7,5},{8,10},{9,11},{10,... | collective-permute-start | bytes 245768 | tf_op jit(solution)/shard_map/ppermute | solution.py:243
  14.5 4.1 %collective-permute-start.3 = (bf16[80,512]{1,0:T(8,128)(2,1)S(1)}, bf16[80,512]{1,0:T(8,128)(2,1)S(1)}, u32[]{:S(2)}, u32[]{:S(2)}) collective-permute-start(bf16[80,512]{1,0:T(8,128)(2,1)S(1)} %get-tuple-element.147), channel_id=1, source_target_pairs={{0,3},{1,0},{2,1},{3,2},{4,7},{5,4},{6,5},{7,6},{8,11},{9,8},{10,9... | collective-permute-start | bytes 245768 | tf_op jit(solution)/shard_map/ppermute | solution.py:243
  21.7 10.1 %collective-permute-start = (bf16[80,512]{1,0:T(8,128)(2,1)S(1)}, bf16[80,512]{1,0:T(8,128)(2,1)S(1)}, u32[]{:S(2)}, u32[]{:S(2)}) collective-permute-start(bf16[80,512]{1,0:T(8,128)(2,1)S(1)} %get-tuple-element.147), channel_id=1, source_target_pairs={{0,32},{32,0},{1,33},{33,1},{2,34},{34,2},{3,35},{35,3},{4,36},{36... | collective-permute-start | bytes 245768 | tf_op jit(solution)/shard_map/ppermute | solution.py:240
  37.1 7.1 %all-to-all-start = ((bf16[8,80,512]{2,1,0:T(8,128)(2,1)}), bf16[8,80,512]{2,1,0:T(8,128)(2,1)S(1)}, u32[]{:S(2)}, u32[]{:S(2)}) async-start(bf16[8,80,512]{2,1,0:T(8,128)(2,1)} %broadcast_in_dim.42), calls=%async_computation | async-start | bytes 1310720 | tf_op jit(solution)/shard_map/all_to_all | solution.py:244
  45.4 26.3 %all-to-all-done = bf16[8,80,512]{2,1,0:T(8,128)(2,1)S(1)} async-done(((bf16[8,80,512]{2,1,0:T(8,128)(2,1)}), bf16[8,80,512]{2,1,0:T(8,128)(2,1)S(1)}, u32[]{:S(2)}, u32[]{:S(2)}) %all-to-all-start) | async-done | bytes 655392 | tf_op jit(solution)/shard_map/all_to_all | solution.py:244
  71.7 1.8 broadcast_in_dim.43
  73.6 5.9 %all-to-all-start.1 = ((bf16[4,8,80,512]{3,2,1,0:T(8,128)(2,1)}), bf16[4,8,80,512]{3,2,1,0:T(8,128)(2,1)}, u32[]{:S(2)}, u32[]{:S(2)}) async-start(bf16[4,8,80,512]{3,2,1,0:T(8,128)(2,1)} %broadcast_in_dim.43), calls=%async_computation.1 | async-start | bytes 5242880 | tf_op jit(solution)/shard_map/all_to_all | solution.py:249
  82.5 2.9 reshape_squeeze.3
  85.4 5.5 %copy.105 = bf16[32,2,32,2,40]{0,3,1,4,2:T(2,128)(2,1)} copy(bf16[32,2,32,2,40]{4,3,2,1,0:T(2,128)(2,1)} %reshape_squeeze.3) | data formatting | bytes 655360 | tf_op jit(solution)/shard_map/reshape;squeeze | solution.py:256
  90.8 4.0 %reshape.38.packed = bf16[32,40,128]{2,1,0:T(8,128)(2,1)} reshape(bf16[32,40,2,2,32]{4,3,2,1,0:T(2,128)(2,1)} %bitcast.110) | data formatting | bytes 655360 | tf_op jit(solution)/shard_map/reshape | solution.py:257
  96.3 11.6 %all-to-all-done.1.wb = bf16[4,8,80,512]{3,2,1,0:T(8,128)(2,1)} async-done(((bf16[4,8,80,512]{3,2,1,0:T(8,128)(2,1)}), bf16[4,8,80,512]{3,2,1,0:T(8,128)(2,1)}, u32[]{:S(2)}, u32[]{:S(2)}) %all-to-all-start.1) | async-done | bytes 2621472 | tf_op jit(solution)/shard_map/all_to_all | solution.py:249
  107.9 5.0 %forward.1 = (bf16[2,8,4,80,512]{4,3,2,1,0:T(8,128)(2,1)S(1)}, bf16[128,128]{1,0:T(8,128)(2,1)S(1)}, bf16[128,128]{1,0:T(8,128)(2,1)S(1)}, bf16[128,128]{1,0:T(8...) custom-call(s32[3]{0:T(128)S(1)} %pad_add_fusion.1.place, ...), custom_call_target="tpu_custom_call" | custom-call | tf_op jit(solution)/shard_map/forward/pallas_call | solution.py:261
  113.6 1.8 stage.11
  116.0 1.9 collective-permute-start.4
  118.2 4.6 %collective-permute-done.4.recv = bf16[32,5120]{1,0:T(8,128)(2,1)} collective-permute-done((bf16[32,5120]{1,0:T(8,128)(2,1)}, bf16[32,5120]{1,0:T(8,128)(2,1)}, u32[]{:S(2)}, u32[]{:S(2)}) %collective-permute-start.4) | collective-permute-done | bytes 327712 | tf_op jit(solution)/shard_map/ppermute | solution.py:372
  122.8 2.5 copy-done.1
  126.4 3.8 %collective-permute-start.5 = (bf16[32,5120]{1,0:T(8,128)(2,1)S(1)}, bf16[32,5120]{1,0:T(8,128)(2,1)S(1)}, u32[]{:S(2)}, u32[]{:S(2)}) collective-permute-start(bf16[32,5120]{1,0:T(8,128)(2,1)S(1)} %get-tuple-element.90), channel_id=1, source_target_pairs={{64,0},{128,64},{192,128},{256,192},{320,256},{384,320},{448,384},... | collective-permute-start | bytes 983048 | tf_op jit(solution)/shard_map/ppermute | solution.py:372
  130.5 4.3 %collective-permute-done.5.recv = bf16[32,5120]{1,0:T(8,128)(2,1)S(1)} collective-permute-done((bf16[32,5120]{1,0:T(8,128)(2,1)S(1)}, bf16[32,5120]{1,0:T(8,128)(2,1)S(1)}, u32[]{:S(2)}, u32[]{:S(2)}) %collective-permute-start.5) | collective-permute-done | bytes 327712 | tf_op jit(solution)/shard_map/ppermute | solution.py:372
  135.5 4.0 %collective-permute-start.6 = (bf16[32,5120]{1,0:T(8,128)(2,1)S(1)}, bf16[32,5120]{1,0:T(8,128)(2,1)S(1)}, u32[]{:S(2)}, u32[]{:S(2)}) collective-permute-start(bf16[32,5120]{1,0:T(8,128)(2,1)S(1)} %get-tuple-element.95), channel_id=1, source_target_pairs={{64,0},{128,64},{192,128},{256,192},{320,256},{384,320},{448,384},... | collective-permute-start | bytes 983048 | tf_op jit(solution)/shard_map/ppermute | solution.py:372
  139.7 4.3 %collective-permute-done.6.recv = bf16[32,5120]{1,0:T(8,128)(2,1)S(1)} collective-permute-done((bf16[32,5120]{1,0:T(8,128)(2,1)S(1)}, bf16[32,5120]{1,0:T(8,128)(2,1)S(1)}, u32[]{:S(2)}, u32[]{:S(2)}) %collective-permute-start.6) | collective-permute-done | bytes 327712 | tf_op jit(solution)/shard_map/ppermute | solution.py:372
  144.7 4.2 %collective-permute-start.7 = (bf16[32,5120]{1,0:T(8,128)(2,1)S(1)}, bf16[32,5120]{1,0:T(8,128)(2,1)S(1)}, u32[]{:S(2)}, u32[]{:S(2)}) collective-permute-start(bf16[32,5120]{1,0:T(8,128)(2,1)S(1)} %get-tuple-element.100), channel_id=1, source_target_pairs={{64,0},{128,64},{192,128},{256,192},{320,256},{384,320},{448,384},... | collective-permute-start | bytes 983048 | tf_op jit(solution)/shard_map/ppermute | solution.py:372
  149.1 4.4 %collective-permute-done.7.recv = bf16[32,5120]{1,0:T(8,128)(2,1)S(1)} collective-permute-done((bf16[32,5120]{1,0:T(8,128)(2,1)S(1)}, bf16[32,5120]{1,0:T(8,128)(2,1)S(1)}, u32[]{:S(2)}, u32[]{:S(2)}) %collective-permute-start.7) | collective-permute-done | bytes 327712 | tf_op jit(solution)/shard_map/ppermute | solution.py:372
  154.3 3.8 %collective-permute-start.8 = (bf16[32,5120]{1,0:T(8,128)(2,1)S(1)}, bf16[32,5120]{1,0:T(8,128)(2,1)S(1)}, u32[]{:S(2)}, u32[]{:S(2)}) collective-permute-start(bf16[32,5120]{1,0:T(8,128)(2,1)S(1)} %get-tuple-element.105), channel_id=1, source_target_pairs={{64,0},{128,64},{192,128},{256,192},{320,256},{384,320},{448,384},... | collective-permute-start | bytes 983048 | tf_op jit(solution)/shard_map/ppermute | solution.py:372
  158.3 5.3 %collective-permute-done.8.recv = bf16[32,5120]{1,0:T(8,128)(2,1)S(1)} collective-permute-done((bf16[32,5120]{1,0:T(8,128)(2,1)S(1)}, bf16[32,5120]{1,0:T(8,128)(2,1)S(1)}, u32[]{:S(2)}, u32[]{:S(2)}) %collective-permute-start.8) | collective-permute-done | bytes 327712 | tf_op jit(solution)/shard_map/ppermute | solution.py:372
  163.6 3.8 %stage.16 = (bf16[32,5120]{1,0:T(8,128)(2,1)S(1)}, f32[128,128]{1,0:T(8,128)S(1)}, f32[128,128]{1,0:T(8,128)S(1)}, bf16[128,288]{1,0:T(8,128)(2,1)S(1)}, bf16[128,128]{1,0:T(8,128)(2,1)S(1)}) custom-call(s32[3]{0:T(128)S(1)} %copy-done.48, ...), custom_call_target="tpu_custom_call", output_to_operand_aliasing={{1}: (15, {}), {2}: (16, {}), {3}: (17, {}), {4}: (18, {})} | custom-call | tf_op jit(solution)/shard_map/stage/pallas_call | solution.py:323
  167.4 1.9 collective-permute-start.9
  169.5 7.0 %collective-permute-done.9.recv = bf16[32,5120]{1,0:T(8,128)(2,1)S(1)} collective-permute-done((bf16[32,5120]{1,0:T(8,128)(2,1)S(1)}, bf16[32,5120]{1,0:T(8,128)(2,1)S(1)}, u32[]{:S(2)}, u32[]{:S(2)}) %collective-permute-start.9) | collective-permute-done | bytes 327712 | tf_op jit(solution)/shard_map/ppermute | solution.py:372
  176.6 3.8 %stage.17 = (bf16[32,5120]{1,0:T(8,128)(2,1)S(1)}, f32[128,128]{1,0:T(8,128)S(1)}, f32[128,128]{1,0:T(8,128)S(1)}, bf16[128,288]{1,0:T(8,128)(2,1)S(1)}, bf16[128,128]{1,0:T(8,128)(2,1)S(1)}) custom-call(s32[3]{0:T(128)S(1)} %copy-done.46, ...), custom_call_target="tpu_custom_call", output_to_operand_aliasing={{1}: (15, {}), {2}: (16, {}), {3}: (17, {}), {4}: (18, {})} | custom-call | tf_op jit(solution)/shard_map/stage/pallas_call | solution.py:323
  180.3 1.9 collective-permute-start.10
  182.5 6.7 %collective-permute-done.10.recv = bf16[32,5120]{1,0:T(8,128)(2,1)S(1)} collective-permute-done((bf16[32,5120]{1,0:T(8,128)(2,1)S(1)}, bf16[32,5120]{1,0:T(8,128)(2,1)S(1)}, u32[]{:S(2)}, u32[]{:S(2)}) %collective-permute-start.10) | collective-permute-done | bytes 327712 | tf_op jit(solution)/shard_map/ppermute | solution.py:372
  189.1 3.8 %stage.18 = (bf16[32,5120]{1,0:T(8,128)(2,1)S(1)}, f32[128,128]{1,0:T(8,128)S(1)}, f32[128,128]{1,0:T(8,128)S(1)}, bf16[128,288]{1,0:T(8,128)(2,1)S(1)}, bf16[128,128]{1,0:T(8,128)(2,1)S(1)}) custom-call(s32[3]{0:T(128)S(1)} %copy-done.47, ...), custom_call_target="tpu_custom_call", output_to_operand_aliasing={{1}: (15, {}), {2}: (16, {}), {3}: (17, {}), {4}: (18, {})} | custom-call | tf_op jit(solution)/shard_map/stage/pallas_call | solution.py:323
  192.9 1.9 collective-permute-start.11
  195.1 6.2 %collective-permute-done.11.recv = bf16[32,5120]{1,0:T(8,128)(2,1)S(1)} collective-permute-done((bf16[32,5120]{1,0:T(8,128)(2,1)S(1)}, bf16[32,5120]{1,0:T(8,128)(2,1)S(1)}, u32[]{:S(2)}, u32[]{:S(2)}) %collective-permute-start.11) | collective-permute-done | bytes 327712 | tf_op jit(solution)/shard_map/ppermute | solution.py:372
  201.3 4.5 %stage.19 = (bf16[32,5120]{1,0:T(8,128)(2,1)}, f32[128,128]{1,0:T(8,128)S(1)}, f32[128,128]{1,0:T(8,128)S(1)}, bf16[128,288]{1,0:T(8,128)(2,1)S(1)}, bf16[128,128]{1,0:T(8,128)(2,1)S(1)}) custom-call(s32[3]{0:T(128)S(1)} %copy-done.53, ...), custom_call_target="tpu_custom_call", output_to_operand_aliasing={{1}: (15, {}), {2}: (16, {}), {3}: (17, {}), {4}: (18, {})} | custom-call | tf_op jit(solution)/shard_map/stage/pallas_call | solution.py:323
  205.8 1.9 collective-permute-start.12
  210.2 5.7 %all-to-all-start.2 = ((bf16[32,120,128]{2,1,0:T(8,128)(2,1)}), bf16[32,120,128]{2,1,0:T(8,128)(2,1)}, u32[]{:S(2)}, u32[]{:S(2)}) async-start(bf16[32,120,128]{2,1,0:T(8,128)(2,1)} %copy-done.28), calls=%async_computation.2 | async-start | bytes 1966080 | tf_op jit(solution)/shard_map/all_to_all | solution.py:370
  215.9 1.9 select_dynamic-update-slice_fusion.9.kept
  217.7 2.5 copy-done.2
  225.0 4.8 %collective-permute-start.13 = (bf16[32,5120]{1,0:T(8,128)(2,1)S(1)}, bf16[32,5120]{1,0:T(8,128)(2,1)S(1)}, u32[]{:S(2)}, u32[]{:S(2)}) collective-permute-start(bf16[32,5120]{1,0:T(8,128)(2,1)S(1)} %get-tuple-element.130.soon), channel_id=1, source_target_pairs={{64,0},{128,64},{192,128},{256,192},{320,256},{384,320},{448,384},... | collective-permute-start | bytes 983048 | tf_op jit(solution)/shard_map/ppermute | solution.py:372
  229.9 4.4 %collective-permute-done.13.recv = bf16[32,5120]{1,0:T(8,128)(2,1)S(1)} collective-permute-done((bf16[32,5120]{1,0:T(8,128)(2,1)S(1)}, bf16[32,5120]{1,0:T(8,128)(2,1)S(1)}, u32[]{:S(2)}, u32[]{:S(2)}) %collective-permute-start.13) | collective-permute-done | bytes 327712 | tf_op jit(solution)/shard_map/ppermute | solution.py:372
  236.2 6.3 %all-to-all-done.2.got = bf16[32,120,128]{2,1,0:T(8,128)(2,1)} async-done(((bf16[32,120,128]{2,1,0:T(8,128)(2,1)}), bf16[32,120,128]{2,1,0:T(8,128)(2,1)}, u32[]{:S(2)}, u32[]{:S(2)}) %all-to-all-start.2) | async-done | bytes 983072 | tf_op jit(solution)/shard_map/all_to_all | solution.py:370
  242.4 6.4 %all-to-all-start.3 = ((bf16[32,80,128]{2,1,0:T(8,128)(2,1)}), bf16[32,80,128]{2,1,0:T(8,128)(2,1)}, u32[]{:S(2)}, u32[]{:S(2)}) async-start(bf16[32,80,128]{2,1,0:T(8,128)(2,1)} %copy-done.34), calls=%async_computation.3 | async-start | bytes 1310720 | tf_op jit(solution)/shard_map/all_to_all | solution.py:352
  251.4 2.2 shard_map.129.sofar
  254.4 2.5 copy-done.3
  259.0 10.4 %all-to-all-done.3.got = bf16[32,80,128]{2,1,0:T(8,128)(2,1)} async-done(((bf16[32,80,128]{2,1,0:T(8,128)(2,1)}), bf16[32,80,128]{2,1,0:T(8,128)(2,1)}, u32[]{:S(2)}, u32[]{:S(2)}) %all-to-all-start.3) | async-done | bytes 655392 | tf_op jit(solution)/shard_map/all_to_all | solution.py:352
  273.2 6.0 %collective-permute-start.14 = (f32[80,128]{1,0:T(8,128)S(1)}, f32[80,128]{1,0:T(8,128)S(1)}, u32[]{:S(2)}, u32[]{:S(2)}) collective-permute-start(f32[80,128]{1,0:T(8,128)S(1)} %slice_select_fusion), channel_id=1, source_target_pairs={{0,32},{32,0},{1,33},{33,1},{2,34},{34,2},{3,35},{35,3},{4,36},{36... | collective-permute-start | bytes 122888 | tf_op jit(solution)/shard_map/ppermute | solution.py:398
  281.4 1.7 finish.1
  (186 shorter events, 41.7 us)
Async XLA Ops:
  7.2 100.7 %all-gather.5.cloned.1.call-start = ((), (), s32[]{:S(2)}) async-start(), calls=%async_computation.4 | async-start | bytes 2949120 | tf_op jit(solution)/shard_map/all_gather | solution.py:247
  8.1 10.5 %collective-permute-start.1 = (bf16[80,512]{1,0:T(8,128)(2,1)S(1)}, bf16[80,512]{1,0:T(8,128)(2,1)S(1)}, u32[]{:S(2)}, u32[]{:S(2)}) collective-permute-start(bf16[80,512]{1,0:T(8,128)(2,1)S(1)} %get-tuple-element.147), channel_id=1, source_target_pairs={{0,1},{1,2},{2,3},{3,0},{4,5},{5,6},{6,7},{7,4},{8,9},{9,10},{10,1... | collective-permute-start | bytes 245768 | tf_op jit(solution)/shard_map/ppermute | solution.py:243
  11.5 8.2 %collective-permute-start.2 = (bf16[80,512]{1,0:T(8,128)(2,1)S(1)}, bf16[80,512]{1,0:T(8,128)(2,1)S(1)}, u32[]{:S(2)}, u32[]{:S(2)}) collective-permute-start(bf16[80,512]{1,0:T(8,128)(2,1)S(1)} %get-tuple-element.147), channel_id=1, source_target_pairs={{0,2},{1,3},{2,0},{3,1},{4,6},{5,7},{6,4},{7,5},{8,10},{9,11},{10,... | collective-permute-start | bytes 245768 | tf_op jit(solution)/shard_map/ppermute | solution.py:243
  14.5 6.4 %collective-permute-start.3 = (bf16[80,512]{1,0:T(8,128)(2,1)S(1)}, bf16[80,512]{1,0:T(8,128)(2,1)S(1)}, u32[]{:S(2)}, u32[]{:S(2)}) collective-permute-start(bf16[80,512]{1,0:T(8,128)(2,1)S(1)} %get-tuple-element.147), channel_id=1, source_target_pairs={{0,3},{1,0},{2,1},{3,2},{4,7},{5,4},{6,5},{7,6},{8,11},{9,8},{10,9... | collective-permute-start | bytes 245768 | tf_op jit(solution)/shard_map/ppermute | solution.py:243
  21.7 22.6 %copy-start.5 = (bf16[128,5120]{1,0:T(8,128)(2,1)S(1)}, bf16[128,5120]{1,0:T(8,128)(2,1)}, u32[]{:S(2)}) copy-start(bf16[128,5120]{1,0:T(8,128)(2,1)} %top.21) | copy-start | bytes 3932164
  21.7 14.6 %collective-permute-start = (bf16[80,512]{1,0:T(8,128)(2,1)S(1)}, bf16[80,512]{1,0:T(8,128)(2,1)S(1)}, u32[]{:S(2)}, u32[]{:S(2)}) collective-permute-start(bf16[80,512]{1,0:T(8,128)(2,1)S(1)} %get-tuple-element.147), channel_id=1, source_target_pairs={{0,32},{32,0},{1,33},{33,1},{2,34},{34,2},{3,35},{35,3},{4,36},{36... | collective-permute-start | bytes 245768 | tf_op jit(solution)/shard_map/ppermute | solution.py:240
  37.1 34.6 %all-to-all-start = ((bf16[8,80,512]{2,1,0:T(8,128)(2,1)}), bf16[8,80,512]{2,1,0:T(8,128)(2,1)S(1)}, u32[]{:S(2)}, u32[]{:S(2)}) async-start(bf16[8,80,512]{2,1,0:T(8,128)(2,1)} %broadcast_in_dim.42), calls=%async_computation | async-start | bytes 1310720 | tf_op jit(solution)/shard_map/all_to_all | solution.py:244
  73.6 6.5 %copy-start.59 = (bf16[1,5120]{1,0:T(2,128)(2,1)S(1)}, bf16[1,5120]{1,0:T(2,128)(2,1)}, u32[]{:S(2)}) copy-start(bf16[1,5120]{1,0:T(2,128)(2,1)} %param.12) | copy-start | bytes 30724
  73.6 8.4 %copy-start.4 = (bf16[1,128,5120]{2,1,0:T(8,128)(2,1)S(1)}, bf16[1,128,5120]{2,1,0:T(8,128)(2,1)}, u32[]{:S(2)}) copy-start(bf16[1,128,5120]{2,1,0:T(8,128)(2,1)} %param.10) | copy-start | bytes 3932164
  73.6 34.3 %all-to-all-start.1 = ((bf16[4,8,80,512]{3,2,1,0:T(8,128)(2,1)}), bf16[4,8,80,512]{3,2,1,0:T(8,128)(2,1)}, u32[]{:S(2)}, u32[]{:S(2)}) async-start(bf16[4,8,80,512]{3,2,1,0:T(8,128)(2,1)} %broadcast_in_dim.43), calls=%async_computation.1 | async-start | bytes 5242880 | tf_op jit(solution)/shard_map/all_to_all | solution.py:249
  79.5 170.6 %all-gather.7.cloned.1.call-start = ((), (), s32[]{:S(2)}) async-start(), calls=%async_computation.5 | async-start | bytes 1351680 | tf_op jit(solution)/shard_map/all_gather | solution.py:286
  80.1 14.7 %copy-start.29 = (f32[1,5120]{1,0:T(1,128)}, f32[1,5120]{1,0:T(1,128)S(1)}, u32[]{:S(2)}) copy-start(f32[1,5120]{1,0:T(1,128)S(1)} %convert_element_type.13.gain) | copy-start | bytes 61444
  94.8 13.1 %copy-start.11 = (bf16[1,288,128]{2,1,0:T(8,128)(2,1)S(1)}, bf16[1,288,128]{2,1,0:T(8,128)(2,1)}, u32[]{:S(2)}) copy-start(bf16[1,288,128]{2,1,0:T(8,128)(2,1)} %param.15) | copy-start | bytes 221188
  94.8 13.1 %copy-start.12 = (bf16[1,288,128]{2,1,0:T(8,128)(2,1)S(1)}, bf16[1,288,128]{2,1,0:T(8,128)(2,1)}, u32[]{:S(2)}) copy-start(bf16[1,288,128]{2,1,0:T(8,128)(2,1)} %param.16) | copy-start | bytes 221188
  94.8 13.1 %copy-start.45 = (bf16[1,32,128]{2,1,0:T(8,128)(2,1)S(1)}, bf16[1,32,128]{2,1,0:T(8,128)(2,1)}, u32[]{:S(2)}) copy-start(bf16[1,32,128]{2,1,0:T(8,128)(2,1)} %param.18) | copy-start | bytes 24580
  107.9 5.7 %copy-start.30 = (f32[1,5120]{1,0:T(1,128)S(1)}, f32[1,5120]{1,0:T(1,128)}, u32[]{:S(2)}) copy-start(f32[1,5120]{1,0:T(1,128)} %copy-done.29) | copy-start | bytes 61444
  107.9 5.7 %copy-start.55 = (s32[3]{0:T(128)S(1)}, s32[3]{0:T(128)}, u32[]{:S(2)}) copy-start(s32[3]{0:T(128)} %add_add_fusion.9.flags) | copy-start | bytes 40
  116.0 6.8 %collective-permute-start.4 = (bf16[32,5120]{1,0:T(8,128)(2,1)}, bf16[32,5120]{1,0:T(8,128)(2,1)}, u32[]{:S(2)}, u32[]{:S(2)}) collective-permute-start(bf16[32,5120]{1,0:T(8,128)(2,1)} %get-tuple-element.85), channel_id=1, source_target_pairs={{64,0},{128,64},{192,128},{256,192},{320,256},{384,320},{448,384},... | collective-permute-start | bytes 983048 | tf_op jit(solution)/shard_map/ppermute | solution.py:372
  117.9 4.9 %copy-start.16 = (bf16[128,128]{1,0:T(8,128)(2,1)S(1)}, bf16[128,128]{1,0:T(8,128)(2,1)}, u32[]{:S(2)}) copy-start(bf16[128,128]{1,0:T(8,128)(2,1)} %copy-done.15) | copy-start | bytes 98308
  117.9 4.9 %copy-start.21 = (bf16[128,128]{1,0:T(8,128)(2,1)S(1)}, bf16[128,128]{1,0:T(8,128)(2,1)}, u32[]{:S(2)}) copy-start(bf16[128,128]{1,0:T(8,128)(2,1)} %copy-done.20) | copy-start | bytes 98308
  125.3 5.1 %copy-start.6 = (bf16[128,5120]{1,0:T(8,128)(2,1)S(1)}, bf16[128,5120]{1,0:T(8,128)(2,1)}, u32[]{:S(2)}) copy-start(bf16[128,5120]{1,0:T(8,128)(2,1)} %broadcast_select_fusion) | copy-start | bytes 3932164
  126.4 8.4 %copy-start.52 = (s32[3]{0:T(128)S(1)}, s32[3]{0:T(128)}, u32[]{:S(2)}) copy-start(s32[3]{0:T(128)} %add_add_fusion.7.flags) | copy-start | bytes 40
  126.4 8.4 %collective-permute-start.5 = (bf16[32,5120]{1,0:T(8,128)(2,1)S(1)}, bf16[32,5120]{1,0:T(8,128)(2,1)S(1)}, u32[]{:S(2)}, u32[]{:S(2)}) collective-permute-start(bf16[32,5120]{1,0:T(8,128)(2,1)S(1)} %get-tuple-element.90), channel_id=1, source_target_pairs={{64,0},{128,64},{192,128},{256,192},{320,256},{384,320},{448,384},... | collective-permute-start | bytes 983048 | tf_op jit(solution)/shard_map/ppermute | solution.py:372
  135.5 8.6 %copy-start.51 = (s32[3]{0:T(128)S(1)}, s32[3]{0:T(128)}, u32[]{:S(2)}) copy-start(s32[3]{0:T(128)} %add_add_fusion.6.flags) | copy-start | bytes 40
  135.5 8.6 %collective-permute-start.6 = (bf16[32,5120]{1,0:T(8,128)(2,1)S(1)}, bf16[32,5120]{1,0:T(8,128)(2,1)S(1)}, u32[]{:S(2)}, u32[]{:S(2)}) collective-permute-start(bf16[32,5120]{1,0:T(8,128)(2,1)S(1)} %get-tuple-element.95), channel_id=1, source_target_pairs={{64,0},{128,64},{192,128},{256,192},{320,256},{384,320},{448,384},... | collective-permute-start | bytes 983048 | tf_op jit(solution)/shard_map/ppermute | solution.py:372
  144.7 8.8 %copy-start.49 = (s32[3]{0:T(128)S(1)}, s32[3]{0:T(128)}, u32[]{:S(2)}) copy-start(s32[3]{0:T(128)} %add_add_fusion.5.flags) | copy-start | bytes 40
  144.7 8.8 %collective-permute-start.7 = (bf16[32,5120]{1,0:T(8,128)(2,1)S(1)}, bf16[32,5120]{1,0:T(8,128)(2,1)S(1)}, u32[]{:S(2)}, u32[]{:S(2)}) collective-permute-start(bf16[32,5120]{1,0:T(8,128)(2,1)S(1)} %get-tuple-element.100), channel_id=1, source_target_pairs={{64,0},{128,64},{192,128},{256,192},{320,256},{384,320},{448,384},... | collective-permute-start | bytes 983048 | tf_op jit(solution)/shard_map/ppermute | solution.py:372
  154.3 9.4 %copy-start.48 = (s32[3]{0:T(128)S(1)}, s32[3]{0:T(128)}, u32[]{:S(2)}) copy-start(s32[3]{0:T(128)} %add_add_fusion.4.flags) | copy-start | bytes 40
  154.3 9.4 %collective-permute-start.8 = (bf16[32,5120]{1,0:T(8,128)(2,1)S(1)}, bf16[32,5120]{1,0:T(8,128)(2,1)S(1)}, u32[]{:S(2)}, u32[]{:S(2)}) collective-permute-start(bf16[32,5120]{1,0:T(8,128)(2,1)S(1)} %get-tuple-element.105), channel_id=1, source_target_pairs={{64,0},{128,64},{192,128},{256,192},{320,256},{384,320},{448,384},... | collective-permute-start | bytes 983048 | tf_op jit(solution)/shard_map/ppermute | solution.py:372
  167.4 9.2 %copy-start.46 = (s32[3]{0:T(128)S(1)}, s32[3]{0:T(128)}, u32[]{:S(2)}) copy-start(s32[3]{0:T(128)} %add_add_fusion.3.flags) | copy-start | bytes 40
  167.4 9.2 %collective-permute-start.9 = (bf16[32,5120]{1,0:T(8,128)(2,1)S(1)}, bf16[32,5120]{1,0:T(8,128)(2,1)S(1)}, u32[]{:S(2)}, u32[]{:S(2)}) collective-permute-start(bf16[32,5120]{1,0:T(8,128)(2,1)S(1)} %get-tuple-element.110), channel_id=1, source_target_pairs={{64,0},{128,64},{192,128},{256,192},{320,256},{384,320},{448,384},... | collective-permute-start | bytes 983048 | tf_op jit(solution)/shard_map/ppermute | solution.py:372
  180.3 8.8 %copy-start.47 = (s32[3]{0:T(128)S(1)}, s32[3]{0:T(128)}, u32[]{:S(2)}) copy-start(s32[3]{0:T(128)} %add_add_fusion.2.flags) | copy-start | bytes 40
  180.3 8.8 %collective-permute-start.10 = (bf16[32,5120]{1,0:T(8,128)(2,1)S(1)}, bf16[32,5120]{1,0:T(8,128)(2,1)S(1)}, u32[]{:S(2)}, u32[]{:S(2)}) collective-permute-start(bf16[32,5120]{1,0:T(8,128)(2,1)S(1)} %get-tuple-element.115), channel_id=1, source_target_pairs={{64,0},{128,64},{192,128},{256,192},{320,256},{384,320},{448,384},... | collective-permute-start | bytes 983048 | tf_op jit(solution)/shard_map/ppermute | solution.py:372
  192.9 8.4 %copy-start.53 = (s32[3]{0:T(128)S(1)}, s32[3]{0:T(128)}, u32[]{:S(2)}) copy-start(s32[3]{0:T(128)} %add_add_fusion.1.flags) | copy-start | bytes 40
  192.9 8.4 %collective-permute-start.11 = (bf16[32,5120]{1,0:T(8,128)(2,1)S(1)}, bf16[32,5120]{1,0:T(8,128)(2,1)S(1)}, u32[]{:S(2)}, u32[]{:S(2)}) collective-permute-start(bf16[32,5120]{1,0:T(8,128)(2,1)S(1)} %get-tuple-element.120), channel_id=1, source_target_pairs={{64,0},{128,64},{192,128},{256,192},{320,256},{384,320},{448,384},... | collective-permute-start | bytes 983048 | tf_op jit(solution)/shard_map/ppermute | solution.py:372
  194.9 10.8 %copy-start.9 = (bf16[128,5120]{1,0:T(8,128)(2,1)}, bf16[128,5120]{1,0:T(8,128)(2,1)S(1)}, u32[]{:S(2)}) copy-start(bf16[128,5120]{1,0:T(8,128)(2,1)S(1)} %select_dynamic-update-slice_fusion.10) | copy-start | bytes 3932164
  201.3 6.5 %copy-start.37 = (bf16[32,40,128]{2,1,0:T(8,128)(2,1)S(1)}, bf16[32,40,128]{2,1,0:T(8,128)(2,1)}, u32[]{:S(2)}) copy-start(bf16[32,40,128]{2,1,0:T(8,128)(2,1)} %reshape.38.packed) | copy-start | bytes 983044
  205.8 12.0 %collective-permute-start.12 = (bf16[32,5120]{1,0:T(8,128)(2,1)}, bf16[32,5120]{1,0:T(8,128)(2,1)}, u32[]{:S(2)}, u32[]{:S(2)}) collective-permute-start(bf16[32,5120]{1,0:T(8,128)(2,1)} %get-tuple-element.125), channel_id=1, source_target_pairs={{64,0},{128,64},{192,128},{256,192},{320,256},{384,320},{448,384},... | collective-permute-start | bytes 983048 | tf_op jit(solution)/shard_map/ppermute | solution.py:372
  210.2 32.3 %all-to-all-start.2 = ((bf16[32,120,128]{2,1,0:T(8,128)(2,1)}), bf16[32,120,128]{2,1,0:T(8,128)(2,1)}, u32[]{:S(2)}, u32[]{:S(2)}) async-start(bf16[32,120,128]{2,1,0:T(8,128)(2,1)} %copy-done.28), calls=%async_computation.2 | async-start | bytes 1966080 | tf_op jit(solution)/shard_map/all_to_all | solution.py:370
  223.8 5.9 %copy-start.8 = (bf16[128,5120]{1,0:T(8,128)(2,1)S(1)}, bf16[128,5120]{1,0:T(8,128)(2,1)}, u32[]{:S(2)}) copy-start(bf16[128,5120]{1,0:T(8,128)(2,1)} %copy-done.7) | copy-start | bytes 3932164
  225.0 9.4 %copy-start.40 = (bf16[32,5120]{1,0:T(8,128)(2,1)}, bf16[32,5120]{1,0:T(8,128)(2,1)S(1)}, u32[]{:S(2)}) copy-start(bf16[32,5120]{1,0:T(8,128)(2,1)S(1)} %get-tuple-element.130.soon) | copy-start | bytes 983044
  225.0 9.3 %collective-permute-start.13 = (bf16[32,5120]{1,0:T(8,128)(2,1)S(1)}, bf16[32,5120]{1,0:T(8,128)(2,1)S(1)}, u32[]{:S(2)}, u32[]{:S(2)}) collective-permute-start(bf16[32,5120]{1,0:T(8,128)(2,1)S(1)} %get-tuple-element.130.soon), channel_id=1, source_target_pairs={{64,0},{128,64},{192,128},{256,192},{320,256},{384,320},{448,384},... | collective-permute-start | bytes 983048 | tf_op jit(solution)/shard_map/ppermute | solution.py:372
  242.4 26.9 %all-to-all-start.3 = ((bf16[32,80,128]{2,1,0:T(8,128)(2,1)}), bf16[32,80,128]{2,1,0:T(8,128)(2,1)}, u32[]{:S(2)}, u32[]{:S(2)}) async-start(bf16[32,80,128]{2,1,0:T(8,128)(2,1)} %copy-done.34), calls=%async_computation.3 | async-start | bytes 1310720 | tf_op jit(solution)/shard_map/all_to_all | solution.py:352
  258.2 21.1 %copy-start.19 = (bf16[128,128]{1,0:T(8,128)(2,1)S(1)}, bf16[128,128]{1,0:T(8,128)(2,1)}, u32[]{:S(2)}) copy-start(bf16[128,128]{1,0:T(8,128)(2,1)} %copy-done.15) | copy-start | bytes 98308
  258.2 21.9 %copy-start.57 = (s32[4]{0:T(128)S(1)}, s32[4]{0:T(128)}, u32[]{:S(2)}) copy-start(s32[4]{0:T(128)} %pad_add_fusion.flags) | copy-start | bytes 52
  271.6 8.5 %copy-start.41 = (bf16[32,5120]{1,0:T(8,128)(2,1)S(1)}, bf16[32,5120]{1,0:T(8,128)(2,1)}, u32[]{:S(2)}) copy-start(bf16[32,5120]{1,0:T(8,128)(2,1)} %copy-done.40) | copy-start | bytes 983044
  271.6 8.5 %copy-start.43 = (bf16[32,5120]{1,0:T(8,128)(2,1)S(1)}, bf16[32,5120]{1,0:T(8,128)(2,1)}, u32[]{:S(2)}) copy-start(bf16[32,5120]{1,0:T(8,128)(2,1)} %copy-done.42) | copy-start | bytes 983044
  273.2 10.2 %collective-permute-start.14 = (f32[80,128]{1,0:T(8,128)S(1)}, f32[80,128]{1,0:T(8,128)S(1)}, u32[]{:S(2)}, u32[]{:S(2)}) collective-permute-start(f32[80,128]{1,0:T(8,128)S(1)} %slice_select_fusion), channel_id=1, source_target_pairs={{0,32},{32,0},{1,33},{33,1},{2,34},{34,2},{3,35},{35,3},{4,36},{36... | collective-permute-start | bytes 122888 | tf_op jit(solution)/shard_map/ppermute | solution.py:398
  (33 other events, 67.7 us)
Sparse Core Ops, SparseCore 0:
  21.8 62.8 all-gather.4
  118.0 75.8 all-gather.6
